TPU v7x, 512 devices: a whole 4x8x8 slice. The times are simulated.
512 devices in a mesh: row: 32 (over z, x_lo, core), col: 16 (over x_hi, y).
Axes of the slice: x: 4 (x_hi: 2, x_lo: 2; x = x_hi * 2 + x_lo), y: 8, z: 8, core: 2. Of those that a mesh axis runs over, the one named last changes fastest.
Arguments:
- grm_prior: float32 [4096, 4096], P('row', 'col'), may hold values from -0.6 to 0.6
- dosage_now: bfloat16 [4096, 4096], P('row', 'col'), may hold values from 0 to 2
- mask_now: int32 [4096, 4096], P('row', 'col'), may hold values 0 or 1
- dosage_prev: bfloat16 [4096, 256], P('row'), may hold values from 0 to 2
- mask_prev: int32 [4096, 256], P('row'), may hold values 0 or 1
- expression: bfloat16 [4096, 20480], P('row', 'col'), may hold values from -18 to 18
Outputs:
- grm_total: float32 [4096, 4096], P('row', 'col')
- assoc_score: float32 [256, 20480], P('row', 'col')
All inputs are finite; a program needn't handle non-finite values. No bound on the sum of `mask_now` or of `mask_prev` on one device may be relied on, other than what follows from the above.
Results may differ from a plain program's by a relative error of at most 0.0029.
Values may be sent and summed in bfloat16 or wider, within the bound.
No kernel may reach another device: no remote copies, remote signals or barrier semaphores. Data moves between devices by JAX's collectives and lax.ppermute only.
A program may use at most 64 MiB of HBM per device.

v0:
```python
import math

import jax
import jax.numpy as jnp
from jax import lax
from jax.sharding import PartitionSpec as P

VARIANTS = 4096


epsilon = 1e-05


def sent_to_all(shard, axis):
    peers = lax.axis_size(axis)
    return lax.all_to_all(
        jnp.broadcast_to(shard[None], (peers, *shard.shape)), axis, 0, 0, tiled=True
    )


def of_everyone(shard, axis):
    everything = sent_to_all(shard, axis)
    return jnp.sum(everything, axis=0)


def in_one(arrays, axis):
    ravelled, at, outs = (jnp.concatenate([a.reshape(-1) for a in arrays]), 0, [])
    total = of_everyone(ravelled, axis)
    for a in arrays:
        outs.append(total[at : at + a.size].reshape(a.shape))
        at += a.size
    return tuple(outs)


def joined_along(pieces, dim):
    lengths = list(pieces.shape[1:])
    lengths[dim] *= pieces.shape[0]
    return jnp.moveaxis(pieces, 0, dim).reshape(lengths)


def collect(shard, axis, dim):
    pieces = sent_to_all(shard, axis)
    return joined_along(pieces, dim)


def spread(value, axis, source):
    kept = jnp.where(lax.axis_index(axis) == source, value, 0).astype(value.dtype)
    return lax.psum(kept, axis)


def cut_along(shard, dim, peers):
    lengths = shard.shape
    pieces = shard.reshape(*lengths[:dim], peers, lengths[dim] // peers, *lengths[dim + 1 :])
    return jnp.moveaxis(pieces, dim, 0)


def sent_and_summed(shard, axis, dim):
    pieces = cut_along(shard, dim, lax.axis_size(axis))
    arrived = lax.all_to_all(pieces, axis, split_axis=0, concat_axis=0, tiled=True)
    return arrived.sum(axis=0)


def local_sums(dosage, present):
    values = dosage.astype(jnp.float32)
    weight = present.astype(jnp.float32)
    return (values, weight, jnp.sum(weight, 0), jnp.sum(weight * values, 0))


def body(grm_prior, dosage_now, mask_now, dosage_prev, mask_prev, expression):
    samples_all = dosage_now.shape[0] * lax.axis_size("row")
    values_now, weight_now, seen_now, summed_now = local_sums(dosage_now, mask_now)
    values_prev, weight_prev, seen_prev, summed_prev = local_sums(dosage_prev, mask_prev)
    traits = expression.astype(jnp.float32)
    squares_trait = jnp.sum(traits * traits, 0)
    raw_now = jnp.sum(weight_now * values_now * values_now, 0)
    raw_prev = jnp.sum(weight_prev * values_prev * values_prev, 0)
    seen_now, summed_now, raw_now, seen_prev, summed_prev, raw_prev, squares_trait = in_one(
        (seen_now, summed_now, raw_now, seen_prev, summed_prev, raw_prev, squares_trait), "row"
    )
    observed_now = jnp.maximum(seen_now, 1.0)
    observed_prev = jnp.maximum(seen_prev, 1.0)
    centre_now = summed_now / observed_now
    centre_prev = summed_prev / observed_prev
    offset_now = weight_now * (values_now - centre_now)
    offset_prev = weight_prev * (values_prev - centre_prev)
    spread_now = raw_now / observed_now - centre_now * centre_now
    spread_prev = raw_prev / observed_prev - centre_prev * centre_prev
    scaled = (offset_now * lax.rsqrt(spread_now + epsilon)).astype(jnp.bfloat16)
    own_panel = collect(scaled, "col", 1)
    panels = lax.axis_size("row") // lax.axis_size("col")
    column = lax.axis_index("col")
    blocks = []
    for member in range(panels):
        remote = spread(own_panel, "row", column * panels + member)
        blocks.append(
            lax.dot_general(
                own_panel, remote, (((1,), (1,)), ((), ())), preferred_element_type=jnp.float32
            )
        )
    grm_total = grm_prior + jnp.concatenate(blocks, 1) / VARIANTS
    genotype = offset_prev.astype(jnp.bfloat16)
    out_rows = genotype.shape[1] // lax.axis_size("row")
    first_row = lax.axis_index("row") * out_rows
    cross_sum = sent_and_summed(
        lax.dot_general(
            genotype, expression, (((0,), (0,)), ((), ())), preferred_element_type=jnp.float32
        ),
        "row",
        0,
    )
    spread_rows = lax.dynamic_slice_in_dim(spread_prev, first_row, out_rows, 0)
    power = squares_trait / samples_all
    assoc_score = (
        cross_sum
        * lax.rsqrt(spread_rows + epsilon)[:, None]
        * lax.rsqrt(power + epsilon)[None, :]
        / math.sqrt(samples_all)
    )
    return (grm_total, assoc_score)


def solution(mesh):
    in_specs = (
        P("row", "col"),
        P("row", "col"),
        P("row", "col"),
        P("row", None),
        P("row", None),
        P("row", "col"),
    )
    out_specs = (P("row", "col"), P("row", "col"))
    return jax.shard_map(body, mesh=mesh, in_specs=in_specs, out_specs=out_specs, check_vma=False)
```

profile of v0, /device:TPU:1, one launch (start us, length us, event | category | flops | bytes accessed | tf_op | source)
XLA Modules:
  0.0 331.7 jit_solution(8352742839686152913)
XLA Ops:
  7.2 0.0 copy-start.5
  7.2 0.0 copy-start.3
  7.2 1.1 multiply_reduce_fusion
  8.3 1.0 fusion
  9.3 1.0 fusion.4
  10.4 0.2 broadcast_in_dim.8
  10.6 26.0 %all_to_all.16 = f32[32,1,2816]{2,1,0:T(1,128)S(1)} all-to-all(f32[32,1,2816]{2,1,0:T(1,128)S(1)} %broadcast_in_dim.8), channel_id=1, replica_groups=mesh['row'=32,'col'=16] {'row'}, dimensions={0} | all-to-all | bytes 720896 | tf_op jit(solution)/shard_map/all_to_all | solution.py:16
  36.6 0.2 reduce_sum.88
  36.8 0.0 copy-done.5
  36.8 0.0 copy-done.3
  36.9 0.1 copy.17
  37.0 1.2 broadcast_in_dim.9
  38.2 9.2 %all-to-all-start.1 = ((bf16[16,128,256]{1,2,0:T(8,128)(2,1)}), bf16[16,128,256]{1,2,0:T(8,128)(2,1)S(1)}, u32[]{:S(2)}, u32[]{:S(2)}) async-start(bf16[16,128,256]{1,2,0:T(8,128)(2,1)} %broadcast_in_dim.9), calls=%async_computation.1 | async-start | bytes 2097152 | tf_op jit(solution)/shard_map/all_to_all | solution.py:16
  47.4 0.0 copy-done
  47.5 0.0 copy-done.2
  47.5 0.0 copy-done.4
  47.5 1.4 convolution_bitcast_fusion
  48.9 24.2 %all-to-all-done.1 = bf16[16,128,256]{1,2,0:T(8,128)(2,1)S(1)} async-done(((bf16[16,128,256]{1,2,0:T(8,128)(2,1)}), bf16[16,128,256]{1,2,0:T(8,128)(2,1)S(1)}, u32[]{:S(2)}, u32[]{:S(2)}) %all-to-all-start.1) | async-done | bytes 1048608 | tf_op jit(solution)/shard_map/all_to_all | solution.py:16
  73.1 7.5 %all-to-all-start.2 = ((f32[32,8,1280]{2,1,0:T(8,128)}), f32[32,8,1280]{2,1,0:T(8,128)S(1)}, u32[]{:S(2)}, u32[]{:S(2)}) async-start(f32[32,8,1280]{2,1,0:T(8,128)} %convolution_bitcast_fusion), calls=%async_computation.2 | async-start | bytes 2621440 | tf_op jit(solution)/shard_map/all_to_all | solution.py:59
  80.7 0.0 all-reduce.3.cloned.1.call-start
  80.7 1.6 broadcast_select_fusion.1
  82.3 0.0 all-reduce.3.cloned.1.call-update
  82.3 0.9 copy-done.6
  83.2 0.1 copy.18
  83.3 0.1 add_rsqrt_fusion.1
  83.4 31.0 %all-to-all-done.2 = f32[32,8,1280]{2,1,0:T(8,128)S(1)} async-done(((f32[32,8,1280]{2,1,0:T(8,128)}), f32[32,8,1280]{2,1,0:T(8,128)S(1)}, u32[]{:S(2)}, u32[]{:S(2)}) %all-to-all-start.2) | async-done | bytes 1310752 | tf_op jit(solution)/shard_map/all_to_all | solution.py:59
  114.4 0.1 reduce_sum.89
  114.5 0.7 multiply_multiply_fusion
  115.2 206.6 %all-reduce.3.cloned.1.call-done = (bf16[128,4096]{0,1:T(8,128)(2,1)}, bf16[128,4096]{0,1:T(8,128)(2,1)}) async-done(((bf16[128,4096]{0,1:T(8,128)(2,1)}, bf16[128,4096]{0,1:T(8,128)(2,1)}), (bf16[128,4096]{0,1:T(8,128)(2,1)}, bf16[128,4096]{0,1:T(8,128)(2,1)})) %all-reduce.3.cloned.1.call-update) | async-done | bytes 2097168 | tf_op jit(solution)/shard_map/psum | solution.py:48
  321.8 1.8 fusion.16
  323.6 0.5 fusion.17
  324.1 0.8 copy.19
  (18 shorter events, 0.1 us)
Async XLA Ops:
  7.2 29.7 %copy-start.5 = (bf16[128,256]{1,0:T(8,128)(2,1)S(1)}, bf16[128,256]{1,0:T(8,128)(2,1)}, u32[]{:S(2)}) copy-start(bf16[128,256]{1,0:T(8,128)(2,1)} %param.7) | copy-start | bytes 196612
  7.2 29.7 %copy-start.3 = (s32[128,256]{1,0:T(8,128)S(1)}, s32[128,256]{1,0:T(8,128)}, u32[]{:S(2)}) copy-start(s32[128,256]{1,0:T(8,128)} %param.8) | copy-start | bytes 393220
  38.2 9.3 %copy-start = (bf16[128,1280]{1,0:T(8,128)(2,1)S(1)}, bf16[128,1280]{1,0:T(8,128)(2,1)}, u32[]{:S(2)}) copy-start(bf16[128,1280]{1,0:T(8,128)(2,1)} %param.11) | copy-start | bytes 983044
  38.2 9.3 %copy-start.2 = (s32[128,256]{1,0:T(8,128)S(1)}, s32[128,256]{1,0:T(8,128)}, u32[]{:S(2)}) copy-start(s32[128,256]{1,0:T(8,128)} %param.10) | copy-start | bytes 393220
  38.2 9.3 %copy-start.4 = (bf16[128,256]{1,0:T(8,128)(2,1)S(1)}, bf16[128,256]{1,0:T(8,128)(2,1)}, u32[]{:S(2)}) copy-start(bf16[128,256]{1,0:T(8,128)(2,1)} %param.9) | copy-start | bytes 196612
  38.2 34.9 %all-to-all-start.1 = ((bf16[16,128,256]{1,2,0:T(8,128)(2,1)}), bf16[16,128,256]{1,2,0:T(8,128)(2,1)S(1)}, u32[]{:S(2)}, u32[]{:S(2)}) async-start(bf16[16,128,256]{1,2,0:T(8,128)(2,1)} %broadcast_in_dim.9), calls=%async_computation.1 | async-start | bytes 2097152 | tf_op jit(solution)/shard_map/all_to_all | solution.py:16
  73.1 41.2 %all-to-all-start.2 = ((f32[32,8,1280]{2,1,0:T(8,128)}), f32[32,8,1280]{2,1,0:T(8,128)S(1)}, u32[]{:S(2)}, u32[]{:S(2)}) async-start(f32[32,8,1280]{2,1,0:T(8,128)} %convolution_bitcast_fusion), calls=%async_computation.2 | async-start | bytes 2621440 | tf_op jit(solution)/shard_map/all_to_all | solution.py:59
  80.7 241.1 %all-reduce.3.cloned.1.call-start = ((), (), s32[]{:S(2)}) async-start(), calls=%async_computation.3 | async-start | bytes 4194304 | tf_op jit(solution)/shard_map/psum | solution.py:48
  82.3 0.9 copy-start.6
  321.8 1.8 copy-start.1
Sparse Core Ops, SparseCore 0:
  84.5 237.2 all-reduce.2
where the time goes:
time: 332 us
  waiting for transfers between devices  262 us (79%)
  blocking collectives  26 us (8%)
  starting transfers between devices  16.8 us (5%)
  between operations  14.2 us (4%)
  other arithmetic  5.8 us (2%)
  matrix products  3.69 us (1%)
    psum x1, waiting for transfers between devices, spread(): return lax.psum(kept, axis)  207 us
    all_to_all x1, waiting for transfers between devices, sent_and_summed(): lax.all_to_all(pieces, axis, split_axis=0, concat_axis=0, tiled=True)  31 us
    all_to_all x1, blocking collectives, sent_to_all(): lax.all_to_all(jnp.broadcast_to(shard[None], (peers, *shard.shape)), axis...  26 us
    all_to_all x1, waiting for transfers between devices, sent_to_all(): lax.all_to_all(jnp.broadcast_to(shard[None], (peers, *shard.shape)), axis...  24.2 us
    all_to_all x1, starting transfers between devices, sent_to_all(): lax.all_to_all(jnp.broadcast_to(shard[None], (peers, *shard.shape)), axis...  9.22 us
    all_to_all x1, starting transfers between devices, sent_and_summed(): lax.all_to_all(pieces, axis, split_axis=0, concat_axis=0, tiled=True)  7.52 us
  transfers between devices with their start and end apart: 3, of which 3 were waited for; matrix products, arithmetic and copies ran while one was open for 1% of the time, Pallas kernels for 0%

commit v1 on v0

v1 whole, which is shorter than its diff:
```python
import math

import jax
import jax.numpy as jnp
from jax import lax
from jax.sharding import PartitionSpec as P

VARIANTS = 4096
epsilon = 1e-05
EVERY = ("row", "col")
CORES = 2


def local_moments(dosage, present):
    values = dosage.astype(jnp.float32)
    weight = present.astype(jnp.float32)
    kept = weight * values
    return jnp.stack([jnp.sum(weight, 0), jnp.sum(kept, 0), jnp.sum(kept * values, 0)])


def summed_over_rows(flat):
    peers = lax.axis_size("row")
    sent = jnp.broadcast_to(flat[None, None], (peers, 1, flat.size))
    return jnp.sum(lax.all_to_all(sent, "row", 0, 0, tiled=True), axis=(0, 1))


def finished(moments):
    seen, summed, raw = moments
    observed = jnp.maximum(seen, 1.0)
    centre = summed / observed
    return centre, raw / observed - centre * centre


def half_of(stacked, bit, axis=0):
    return lax.dynamic_index_in_dim(stacked, bit, axis, keepdims=False)


def folded(stacked, bit, pairs):
    arrived = lax.ppermute(half_of(stacked, 1 - bit), EVERY, pairs)
    return half_of(stacked, bit) + arrived


def body(grm_prior, dosage_now, mask_now, dosage_prev, mask_prev, expression):
    rows, cols = lax.axis_size("row"), lax.axis_size("col")
    chips = rows // CORES
    row, col = lax.axis_index("row"), lax.axis_index("col")
    core = row % CORES
    samples_all = dosage_now.shape[0] * rows
    width = dosage_now.shape[1]
    tested = dosage_prev.shape[1]

    def at(chip, half, column):
        return (chip * CORES + half) * cols + column

    blocks = [(k, c) for k in range(chips) for c in range(cols)]

    traits = expression.astype(jnp.float32)
    moments_now = local_moments(dosage_now, mask_now)
    moments_prev = local_moments(dosage_prev, mask_prev)
    squares = jnp.sum(traits * traits, 0)
    total = summed_over_rows(
        jnp.concatenate([moments_now.reshape(-1), moments_prev.reshape(-1), squares])
    )
    centre_now, spread_now = finished(total[: 3 * width].reshape(3, width))
    centre_prev, spread_prev = finished(
        total[3 * width : 3 * (width + tested)].reshape(3, tested)
    )
    squares = total[3 * (width + tested) :]

    weight_now = mask_now.astype(jnp.float32)
    scaled = (
        weight_now * (dosage_now.astype(jnp.float32) - centre_now)
        * lax.rsqrt(spread_now + epsilon)
    ).astype(jnp.bfloat16)
    crossed = lax.ppermute(
        scaled,
        EVERY,
        [(at(k, 1, c), at(k, 0, c)) for k, c in blocks]
        + [(at(c, 0, k), at(k, 1, c)) for k, c in blocks],
    )
    mirrored = lax.ppermute(
        scaled, EVERY, [(at(c, 1, k), at(k, 1, c)) for k, c in blocks]
    )
    first = core == 0
    chip_block = jnp.stack(
        [jnp.where(first, scaled, crossed), jnp.where(first, crossed, mirrored)]
    )
    groups = [[at(k, 0, c) for c in range(cols)] for k in range(chips)] + [
        [at(k, 1, c) for k in range(chips)] for c in range(cols)
    ]
    panel = lax.all_to_all(
        jnp.broadcast_to(chip_block[None], (cols, *chip_block.shape)),
        EVERY,
        0,
        0,
        tiled=True,
        axis_index_groups=groups,
    )

    weight_prev = mask_prev.astype(jnp.float32)
    genotype = (weight_prev * (dosage_prev.astype(jnp.float32) - centre_prev)).astype(jnp.bfloat16)
    cross = lax.dot_general(
        genotype, expression, (((0,), (0,)), ((), ())), preferred_element_type=jnp.float32
    )
    out_rows = tested // rows
    genes = expression.shape[1]
    cross = cross.reshape(chips, CORES, out_rows, genes)
    cross = folded(
        jnp.moveaxis(cross, 1, 0),
        core,
        [(at(k, h, c), at(k, 1 - h, c)) for k, c in blocks for h in range(CORES)],
    )
    chip = row // CORES
    span = 1
    while span < chips:
        bit = (chip // span) % 2
        cross = folded(
            jnp.moveaxis(cross.reshape(-1, 2, out_rows, genes), 1, 0),
            bit,
            [(at(k, h, c), at(k ^ span, h, c)) for k, c in blocks for h in range(CORES)],
        )
        span *= 2
    cross = cross.reshape(out_rows, genes)
    spread_rows = lax.dynamic_slice_in_dim(spread_prev, row * out_rows, out_rows, 0)
    power = squares / samples_all
    assoc_score = (
        cross
        * lax.rsqrt(spread_rows + epsilon)[:, None]
        * lax.rsqrt(power + epsilon)[None, :]
        / math.sqrt(samples_all)
    )

    upper, lower = panel[:, 0], panel[:, 1]
    swap = [(at(k, h, c), at(k, 1 - h, c)) for k, c in blocks for h in range(CORES)]
    other = lax.ppermute(jnp.where(first, lower, upper), EVERY, swap)
    rest = lax.ppermute(lower, EVERY, [(at(k, 1, c), at(k, 0, c)) for k, c in blocks])

    def product(a, b):
        return lax.dot_general(
            a, b, (((0, 2), (0, 2)), ((), ())), preferred_element_type=jnp.float32
        )

    mine = jnp.where(first, upper, other)
    left = product(mine, jnp.where(first, other, upper))
    right = product(mine, jnp.where(first, rest, lower))
    grm_total = grm_prior + jnp.concatenate([left, right], 1) / VARIANTS
    return (grm_total, assoc_score)


def solution(mesh):
    assert mesh.shape["row"] == CORES * mesh.shape["col"]
    in_specs = (
        P("row", "col"),
        P("row", "col"),
        P("row", "col"),
        P("row", None),
        P("row", None),
        P("row", "col"),
    )
    out_specs = (P("row", "col"), P("row", "col"))
    return jax.shard_map(body, mesh=mesh, in_specs=in_specs, out_specs=out_specs, check_vma=False)
```

time: 332 us -> 119 us (0.36)
  waiting for transfers between devices: 262 us -> 45.7 us
  starting transfers between devices: 16.8 us -> 58.1 us
  blocking collectives: 26 us -> 0 us
  between operations: 14.2 us -> 1.26 us
    psum x1 -> x0, waiting for transfers between devices: 207 us -> none  [spread(): return lax.psum(kept, axis)]
    all_to_all x2, waiting for transfers between devices: 55.2 us -> 13.3 us  [the longest x1 13.3 us: summed_over_rows(): return jnp.sum(lax.all_to_all(sent, 'row', 0, 0, tiled=True), axis=(0, 1))]
    ppermute x0 -> x9, waiting for transfers between devices: none -> 32.4 us  [the longest x5 32.4 us: folded(): arrived = lax.ppermute(half_of(stacked, 1 - bit), EVERY, pairs)]
    ppermute x0 -> x9, starting transfers between devices: none -> 30.9 us  [the longest x5 19.4 us: folded(): arrived = lax.ppermute(half_of(stacked, 1 - bit), EVERY, pairs)]
    all_to_all x1 -> x0, blocking collectives: 26 us -> none  [sent_to_all(): lax.all_to_all(jnp.broadcast_to(shard[None], (peers, *shard.shape)), axis...]
    all_to_all x2, starting transfers between devices: 16.7 us -> 27.1 us  [the longest x1 14.2 us: body(): lax.all_to_all(jnp.broadcast_to(chip_block[None], (cols, *chip_block.shap...]
  transfers between devices with their start and end apart: 3 -> 11, of which waited for: 3 -> 5; matrix products, arithmetic and copies ran while one was open for 1% -> 6% of each run, Pallas kernels for 0% -> 0%
where the time goes in v1:
time: 119 us; the launch traced here: 118 us
  starting transfers between devices  58.1 us (49%)
  waiting for transfers between devices  45.7 us (38%)
  other arithmetic  6.57 us (6%)
  local copies, waits for them, and re-layouts  5.29 us (4%)
  matrix products  1.35 us (1%)
  between operations  1.26 us (1%)
    ppermute x5, waiting for transfers between devices, folded(): arrived = lax.ppermute(half_of(stacked, 1 - bit), EVERY, pairs)  32.4 us
    ppermute x5, starting transfers between devices, folded(): arrived = lax.ppermute(half_of(stacked, 1 - bit), EVERY, pairs)  19.4 us
    all_to_all x1, starting transfers between devices, body(): lax.all_to_all(jnp.broadcast_to(chip_block[None], (cols, *chip_block.shap...  14.2 us
    all_to_all x1, waiting for transfers between devices, summed_over_rows(): return jnp.sum(lax.all_to_all(sent, 'row', 0, 0, tiled=True), axis=(0, 1))  13.3 us
    all_to_all x1, starting transfers between devices, summed_over_rows(): return jnp.sum(lax.all_to_all(sent, 'row', 0, 0, tiled=True), axis=(0, 1))  12.9 us
    ppermute x1, starting transfers between devices, body(): other = lax.ppermute(jnp.where(first, lower, upper), EVERY, swap)  5.46 us
    ppermute x1, starting transfers between devices, body(): lax.ppermute(scaled, EVERY, [(at(k, 1, c), at(k, 0, c)) for k, c in block...  3.37 us
  transfers between devices with their start and end apart: 11, of which 5 were waited for; matrix products, arithmetic and copies ran while one was open for 6% of the time, Pallas kernels for 0%

profile of v1, /device:TPU:1, one launch (start us, length us, event | category | flops | bytes accessed | tf_op | source)
XLA Modules:
  0.0 118.2 jit_solution(6935724140241588480)
XLA Ops:
  0.7 1.1 fusion.12
  1.8 1.0 fusion.13
  2.8 1.1 multiply_reduce_fusion
  3.9 0.9 broadcast_in_dim.4
  4.8 12.9 %all-to-all-start = ((f32[32,1,2816]{2,1,0:T(1,128)}), f32[32,1,2816]{2,1,0:T(1,128)S(1)}, u32[]{:S(2)}, u32[]{:S(2)}) async-start(f32[32,1,2816]{2,1,0:T(1,128)} %broadcast_in_dim.4), calls=%async_computation | async-start | bytes 720896 | tf_op jit(solution)/shard_map/all_to_all | solution.py:24
  17.7 13.3 %all-to-all-done = f32[32,1,2816]{2,1,0:T(1,128)S(1)} async-done(((f32[32,1,2816]{2,1,0:T(1,128)}), f32[32,1,2816]{2,1,0:T(1,128)S(1)}, u32[]{:S(2)}, u32[]{:S(2)}) %all-to-all-start) | async-done | bytes 360480 | tf_op jit(solution)/shard_map/all_to_all | solution.py:24
  31.0 0.2 reduce_sum.79
  31.3 3.4 %collective-permute-start = (bf16[128,256]{1,0:T(8,128)(2,1)S(1)}, bf16[128,256]{1,0:T(8,128)(2,1)S(1)}, u32[]{:S(2)}, u32[]{:S(2)}) collective-permute-start(bf16[128,256]{1,0:T(8,128)(2,1)S(1)} %fusion.7), channel_id=1, source_target_pairs={{16,0},{17,1},{18,2},{19,3},{20,4},{21,5},{22,6},{23,7},{24,8},{25... | collective-permute-start | bytes 196616 | tf_op jit(solution)/shard_map/ppermute | solution.py:75
  34.7 0.7 collective-permute-start.1
  35.4 0.4 fusion.14
  35.7 0.9 dynamic-slice_bitcast_fusion
  36.6 1.9 %collective-permute-start.4 = (f32[16,8,1280]{2,1,0:T(8,128)}, f32[16,8,1280]{2,1,0:T(8,128)}, u32[]{:S(2)}, u32[]{:S(2)}) collective-permute-start(f32[16,8,1280]{2,1,0:T(8,128)} %dynamic-slice_bitcast_fusion), channel_id=1, source_target_pairs={{0,16},{16,0},{1,17},{17,1},{2,18},{18,2},{3,19},{19,3},{4,20},{20... | collective-permute-start | bytes 1966088 | tf_op jit(solution)/shard_map/ppermute | solution.py:39
  38.6 1.6 %broadcast_in_dim.5 = bf16[16,2,128,256]{3,2,1,0:T(8,128)(2,1)} broadcast(bf16[2,128,256]{2,1,0:T(8,128)(2,1)S(1)} %pad_maximum_fusion), dimensions={1,2,3} | broadcast | bytes 2228224 | tf_op jit(solution)/shard_map/broadcast_in_dim | solution.py:92
  40.2 14.2 %all-to-all-start.1 = ((bf16[16,2,128,256]{3,2,1,0:T(8,128)(2,1)}), bf16[16,2,128,256]{3,2,1,0:T(8,128)(2,1)S(1)}, u32[]{:S(2)}, u32[]{:S(2)}) async-start(bf16[16,2,128,256]{3,2,1,0:T(8,128)(2,1)} %broadcast_in_dim.5), calls=%async_computation.1 | async-start | bytes 4194304 | tf_op jit(solution)/shard_map/all_to_all | solution.py:91
  54.5 1.2 %bitcast_add_fusion = f32[16,8,1280]{2,1,0:T(8,128)S(1)} fusion(f32[16,8,1280]{2,1,0:T(8,128)} %collective-permute-done.4, f32[16,2,8,1280]{3,2,1,0:T(8,128)S(1)} %bitcast.63, s32[]{:T(128)S(6)} %select_n.116), kind=kLoop, calls=%fused_computation.10 | loop fusion | flops 163840 | bytes 1966084 | tf_op jit(solution)/shard_map/add | solution.py:40
  55.7 0.8 copy-done
  56.6 3.3 %collective-permute-start.5 = (f32[8,8,1280]{2,1,0:T(8,128)S(1)}, f32[8,8,1280]{2,1,0:T(8,128)S(1)}, u32[]{:S(2)}, u32[]{:S(2)}) collective-permute-start(f32[8,8,1280]{2,1,0:T(8,128)S(1)} %dynamic-slice_bitcast_fusion.1), channel_id=1, source_target_pairs={{0,32},{16,48},{1,33},{17,49},{2,34},{18,50},{3,35},{19,51},{4,36}... | collective-permute-start | bytes 983048 | tf_op jit(solution)/shard_map/ppermute | solution.py:39
  59.9 24.5 %collective-permute-done.5 = f32[8,8,1280]{2,1,0:T(8,128)S(1)} collective-permute-done((f32[8,8,1280]{2,1,0:T(8,128)S(1)}, f32[8,8,1280]{2,1,0:T(8,128)S(1)}, u32[]{:S(2)}, u32[]{:S(2)}) %collective-permute-start.5) | collective-permute-done | bytes 327712 | tf_op jit(solution)/shard_map/ppermute | solution.py:39
  84.5 1.0 bitcast_add_fusion.1
  85.5 3.3 %collective-permute-start.6 = (f32[4,8,1280]{2,1,0:T(8,128)S(1)}, f32[4,8,1280]{2,1,0:T(8,128)S(1)}, u32[]{:S(2)}, u32[]{:S(2)}) collective-permute-start(f32[4,8,1280]{2,1,0:T(8,128)S(1)} %dynamic-slice_bitcast_fusion.2), channel_id=1, source_target_pairs={{0,64},{16,80},{1,65},{17,81},{2,66},{18,82},{3,67},{19,83},{4,68}... | collective-permute-start | bytes 491528 | tf_op jit(solution)/shard_map/ppermute | solution.py:39
  89.1 3.9 %collective-permute-done.6 = f32[4,8,1280]{2,1,0:T(8,128)S(1)} collective-permute-done((f32[4,8,1280]{2,1,0:T(8,128)S(1)}, f32[4,8,1280]{2,1,0:T(8,128)S(1)}, u32[]{:S(2)}, u32[]{:S(2)}) %collective-permute-start.6) | collective-permute-done | bytes 163872 | tf_op jit(solution)/shard_map/ppermute | solution.py:39
  93.0 4.2 %collective-permute-start.7 = (f32[2,8,1280]{2,1,0:T(8,128)S(1)}, f32[2,8,1280]{2,1,0:T(8,128)S(1)}, u32[]{:S(2)}, u32[]{:S(2)}) collective-permute-start(f32[2,8,1280]{2,1,0:T(8,128)S(1)} %dynamic-slice_bitcast_fusion.3), channel_id=1, source_target_pairs={{0,128},{16,144},{1,129},{17,145},{2,130},{18,146},{3,131},{19,147... | collective-permute-start | bytes 245768 | tf_op jit(solution)/shard_map/ppermute | solution.py:39
  97.2 1.9 %collective-permute-done.7 = f32[2,8,1280]{2,1,0:T(8,128)S(1)} collective-permute-done((f32[2,8,1280]{2,1,0:T(8,128)S(1)}, f32[2,8,1280]{2,1,0:T(8,128)S(1)}, u32[]{:S(2)}, u32[]{:S(2)}) %collective-permute-start.7) | collective-permute-done | bytes 81952 | tf_op jit(solution)/shard_map/ppermute | solution.py:39
  99.1 0.1 broadcast_select_fusion.1
  99.2 5.5 %collective-permute-start.2 = (bf16[16,128,256]{2,1,0:T(8,128)(2,1)S(1)}, bf16[16,128,256]{2,1,0:T(8,128)(2,1)S(1)}, u32[]{:S(2)}, u32[]{:S(2)}) collective-permute-start(bf16[16,128,256]{2,1,0:T(8,128)(2,1)S(1)} %broadcast_select_fusion.1), channel_id=1, source_target_pairs={{0,16},{16,0},{1,17},{17,1},{2,18},{18,2},{3,19},{19,3},{4,20},{20... | collective-permute-start | bytes 3145736 | tf_op jit(solution)/shard_map/ppermute | solution.py:135
  104.8 2.0 %collective-permute-start.3 = (bf16[16,128,256]{2,1,0:T(8,128)(2,1)S(1)}, bf16[16,128,256]{2,1,0:T(8,128)(2,1)S(1)}, u32[]{:S(2)}, u32[]{:S(2)}) collective-permute-start(bf16[16,128,256]{2,1,0:T(8,128)(2,1)S(1)} %slice_bitcast_fusion), channel_id=1, source_target_pairs={{16,0},{17,1},{18,2},{19,3},{20,4},{21,5},{22,6},{23,7},{24,8},{25... | collective-permute-start | bytes 3145736 | tf_op jit(solution)/shard_map/ppermute | solution.py:136
  106.8 6.8 %collective-permute-start.8 = (f32[1,8,1280]{2,1,0:T(8,128)S(1)}, f32[1,8,1280]{2,1,0:T(8,128)S(1)}, u32[]{:S(2)}, u32[]{:S(2)}) collective-permute-start(f32[1,8,1280]{2,1,0:T(8,128)S(1)} %constant_dynamic-slice_fusion), channel_id=1, source_target_pairs={{0,256},{16,272},{1,257},{17,273},{2,258},{18,274},{3,259},{19,275... | collective-permute-start | bytes 122888 | tf_op jit(solution)/shard_map/ppermute | solution.py:39
  113.6 2.1 %collective-permute-done.8 = f32[1,8,1280]{2,1,0:T(8,128)S(1)} collective-permute-done((f32[1,8,1280]{2,1,0:T(8,128)S(1)}, f32[1,8,1280]{2,1,0:T(8,128)S(1)}, u32[]{:S(2)}, u32[]{:S(2)}) %collective-permute-start.8) | collective-permute-done | bytes 40992 | tf_op jit(solution)/shard_map/ppermute | solution.py:39
  115.7 0.7 fusion.18
  116.4 0.5 convolution_bitcast_fusion.1
  116.9 0.5 convolution_bitcast_fusion
  117.5 0.8 copy.25
  (39 shorter events, 0.5 us)
Async XLA Ops:
  0.6 30.6 %copy-start.5 = (bf16[128,256]{1,0:T(8,128)(2,1)S(1)}, bf16[128,256]{1,0:T(8,128)(2,1)}, u32[]{:S(2)}) copy-start(bf16[128,256]{1,0:T(8,128)(2,1)} %param.7) | copy-start | bytes 196612
  0.6 30.6 %copy-start.3 = (s32[128,256]{1,0:T(8,128)S(1)}, s32[128,256]{1,0:T(8,128)}, u32[]{:S(2)}) copy-start(s32[128,256]{1,0:T(8,128)} %param.8) | copy-start | bytes 393220
  0.6 34.7 %copy-start.2 = (s32[128,256]{1,0:T(8,128)S(1)}, s32[128,256]{1,0:T(8,128)}, u32[]{:S(2)}) copy-start(s32[128,256]{1,0:T(8,128)} %param.10) | copy-start | bytes 393220
  0.7 34.7 %copy-start.4 = (bf16[128,256]{1,0:T(8,128)(2,1)S(1)}, bf16[128,256]{1,0:T(8,128)(2,1)}, u32[]{:S(2)}) copy-start(bf16[128,256]{1,0:T(8,128)(2,1)} %param.9) | copy-start | bytes 196612
  0.7 34.7 %copy-start.1 = (bf16[128,1280]{1,0:T(8,128)(2,1)S(1)}, bf16[128,1280]{1,0:T(8,128)(2,1)}, u32[]{:S(2)}) copy-start(bf16[128,1280]{1,0:T(8,128)(2,1)} %param.11) | copy-start | bytes 983044
  4.8 26.2 %all-to-all-start = ((f32[32,1,2816]{2,1,0:T(1,128)}), f32[32,1,2816]{2,1,0:T(1,128)S(1)}, u32[]{:S(2)}, u32[]{:S(2)}) async-start(f32[32,1,2816]{2,1,0:T(1,128)} %broadcast_in_dim.4), calls=%async_computation | async-start | bytes 720896 | tf_op jit(solution)/shard_map/all_to_all | solution.py:24
  31.3 7.3 %collective-permute-start = (bf16[128,256]{1,0:T(8,128)(2,1)S(1)}, bf16[128,256]{1,0:T(8,128)(2,1)S(1)}, u32[]{:S(2)}, u32[]{:S(2)}) collective-permute-start(bf16[128,256]{1,0:T(8,128)(2,1)S(1)} %fusion.7), channel_id=1, source_target_pairs={{16,0},{17,1},{18,2},{19,3},{20,4},{21,5},{22,6},{23,7},{24,8},{25... | collective-permute-start | bytes 196616 | tf_op jit(solution)/shard_map/ppermute | solution.py:75
  34.7 3.9 %collective-permute-start.1 = (bf16[128,256]{1,0:T(8,128)(2,1)S(1)}, bf16[128,256]{1,0:T(8,128)(2,1)S(1)}, u32[]{:S(2)}, u32[]{:S(2)}) collective-permute-start(bf16[128,256]{1,0:T(8,128)(2,1)S(1)} %fusion.7), channel_id=1, source_target_pairs={{16,16},{48,17},{80,18},{112,19},{144,20},{176,21},{208,22},{240,2... | collective-permute-start | bytes 196616 | tf_op jit(solution)/shard_map/ppermute | solution.py:81
  36.6 17.9 %collective-permute-start.4 = (f32[16,8,1280]{2,1,0:T(8,128)}, f32[16,8,1280]{2,1,0:T(8,128)}, u32[]{:S(2)}, u32[]{:S(2)}) collective-permute-start(f32[16,8,1280]{2,1,0:T(8,128)} %dynamic-slice_bitcast_fusion), channel_id=1, source_target_pairs={{0,16},{16,0},{1,17},{17,1},{2,18},{18,2},{3,19},{19,3},{4,20},{20... | collective-permute-start | bytes 1966088 | tf_op jit(solution)/shard_map/ppermute | solution.py:39
  40.2 58.9 %all-to-all-start.1 = ((bf16[16,2,128,256]{3,2,1,0:T(8,128)(2,1)}), bf16[16,2,128,256]{3,2,1,0:T(8,128)(2,1)S(1)}, u32[]{:S(2)}, u32[]{:S(2)}) async-start(bf16[16,2,128,256]{3,2,1,0:T(8,128)(2,1)} %broadcast_in_dim.5), calls=%async_computation.1 | async-start | bytes 4194304 | tf_op jit(solution)/shard_map/all_to_all | solution.py:91
  54.5 34.5 %copy-start.6 = (f32[128,256]{1,0:T(8,128)S(1)}, f32[128,256]{1,0:T(8,128)}, u32[]{:S(2)}) copy-start(f32[128,256]{1,0:T(8,128)} %param.6) | copy-start | bytes 393220
  55.7 0.9 copy-start
  56.6 27.9 %collective-permute-start.5 = (f32[8,8,1280]{2,1,0:T(8,128)S(1)}, f32[8,8,1280]{2,1,0:T(8,128)S(1)}, u32[]{:S(2)}, u32[]{:S(2)}) collective-permute-start(f32[8,8,1280]{2,1,0:T(8,128)S(1)} %dynamic-slice_bitcast_fusion.1), channel_id=1, source_target_pairs={{0,32},{16,48},{1,33},{17,49},{2,34},{18,50},{3,35},{19,51},{4,36}... | collective-permute-start | bytes 983048 | tf_op jit(solution)/shard_map/ppermute | solution.py:39
  85.5 7.4 %collective-permute-start.6 = (f32[4,8,1280]{2,1,0:T(8,128)S(1)}, f32[4,8,1280]{2,1,0:T(8,128)S(1)}, u32[]{:S(2)}, u32[]{:S(2)}) collective-permute-start(f32[4,8,1280]{2,1,0:T(8,128)S(1)} %dynamic-slice_bitcast_fusion.2), channel_id=1, source_target_pairs={{0,64},{16,80},{1,65},{17,81},{2,66},{18,82},{3,67},{19,83},{4,68}... | collective-permute-start | bytes 491528 | tf_op jit(solution)/shard_map/ppermute | solution.py:39
  93.0 6.1 %collective-permute-start.7 = (f32[2,8,1280]{2,1,0:T(8,128)S(1)}, f32[2,8,1280]{2,1,0:T(8,128)S(1)}, u32[]{:S(2)}, u32[]{:S(2)}) collective-permute-start(f32[2,8,1280]{2,1,0:T(8,128)S(1)} %dynamic-slice_bitcast_fusion.3), channel_id=1, source_target_pairs={{0,128},{16,144},{1,129},{17,145},{2,130},{18,146},{3,131},{19,147... | collective-permute-start | bytes 245768 | tf_op jit(solution)/shard_map/ppermute | solution.py:39
  99.2 17.2 %collective-permute-start.2 = (bf16[16,128,256]{2,1,0:T(8,128)(2,1)S(1)}, bf16[16,128,256]{2,1,0:T(8,128)(2,1)S(1)}, u32[]{:S(2)}, u32[]{:S(2)}) collective-permute-start(bf16[16,128,256]{2,1,0:T(8,128)(2,1)S(1)} %broadcast_select_fusion.1), channel_id=1, source_target_pairs={{0,16},{16,0},{1,17},{17,1},{2,18},{18,2},{3,19},{19,3},{4,20},{20... | collective-permute-start | bytes 3145736 | tf_op jit(solution)/shard_map/ppermute | solution.py:135
  104.8 12.2 %collective-permute-start.3 = (bf16[16,128,256]{2,1,0:T(8,128)(2,1)S(1)}, bf16[16,128,256]{2,1,0:T(8,128)(2,1)S(1)}, u32[]{:S(2)}, u32[]{:S(2)}) collective-permute-start(bf16[16,128,256]{2,1,0:T(8,128)(2,1)S(1)} %slice_bitcast_fusion), channel_id=1, source_target_pairs={{16,0},{17,1},{18,2},{19,3},{20,4},{21,5},{22,6},{23,7},{24,8},{25... | collective-permute-start | bytes 3145736 | tf_op jit(solution)/shard_map/ppermute | solution.py:136
  106.8 8.9 %collective-permute-start.8 = (f32[1,8,1280]{2,1,0:T(8,128)S(1)}, f32[1,8,1280]{2,1,0:T(8,128)S(1)}, u32[]{:S(2)}, u32[]{:S(2)}) collective-permute-start(f32[1,8,1280]{2,1,0:T(8,128)S(1)} %constant_dynamic-slice_fusion), channel_id=1, source_target_pairs={{0,256},{16,272},{1,257},{17,273},{2,258},{18,274},{3,259},{19,275... | collective-permute-start | bytes 122888 | tf_op jit(solution)/shard_map/ppermute | solution.py:39

commit v2 on v1

--- a/solution.py
+++ b/solution.py
@@ -18,10 +18,11 @@
     return jnp.stack([jnp.sum(weight, 0), jnp.sum(kept, 0), jnp.sum(kept * values, 0)])
 
 
-def summed_over_rows(flat):
-    peers = lax.axis_size("row")
+def summed_over(flat, groups):
+    peers = len(groups[0])
     sent = jnp.broadcast_to(flat[None, None], (peers, 1, flat.size))
-    return jnp.sum(lax.all_to_all(sent, "row", 0, 0, tiled=True), axis=(0, 1))
+    arrived = lax.all_to_all(sent, EVERY, 0, 0, tiled=True, axis_index_groups=groups)
+    return jnp.sum(arrived, axis=(0, 1))
 
 
 def finished(moments):
@@ -36,8 +37,8 @@
 
 
 def folded(stacked, bit, pairs):
-    arrived = lax.ppermute(half_of(stacked, 1 - bit), EVERY, pairs)
-    return half_of(stacked, bit) + arrived
+    leaving = half_of(stacked, 1 - bit).astype(jnp.bfloat16)
+    return half_of(stacked, bit) + lax.ppermute(leaving, EVERY, pairs).astype(jnp.float32)
 
 
 def body(grm_prior, dosage_now, mask_now, dosage_prev, mask_prev, expression):
@@ -58,9 +59,11 @@
     moments_now = local_moments(dosage_now, mask_now)
     moments_prev = local_moments(dosage_prev, mask_prev)
     squares = jnp.sum(traits * traits, 0)
-    total = summed_over_rows(
-        jnp.concatenate([moments_now.reshape(-1), moments_prev.reshape(-1), squares])
-    )
+    swap = [(at(k, h, c), at(k, 1 - h, c)) for k, c in blocks for h in range(CORES)]
+    partial = jnp.concatenate([moments_now.reshape(-1), moments_prev.reshape(-1), squares])
+    partial = partial + lax.ppermute(partial, EVERY, swap)
+    columns = [[at(k, h, c) for k in range(chips)] for c in range(cols) for h in range(CORES)]
+    total = summed_over(partial, columns)
     centre_now, spread_now = finished(total[: 3 * width].reshape(3, width))
     centre_prev, spread_prev = finished(
         total[3 * width : 3 * (width + tested)].reshape(3, tested)
@@ -81,13 +84,36 @@
     mirrored = lax.ppermute(
         scaled, EVERY, [(at(c, 1, k), at(k, 1, c)) for k, c in blocks]
     )
+    weight_prev = mask_prev.astype(jnp.float32)
+    genotype = (weight_prev * (dosage_prev.astype(jnp.float32) - centre_prev)).astype(jnp.bfloat16)
+    cross = lax.dot_general(
+        genotype, expression, (((0,), (0,)), ((), ())), preferred_element_type=jnp.float32
+    )
+    out_rows = tested // rows
+    genes = expression.shape[1]
+    layers = chips // 2
+    chip = row // CORES
+    level, side = chip // 2, chip % 2
+    near = layers // 2
+    cross = cross.reshape(layers, 2, CORES * out_rows, genes)
+    cross = jnp.concatenate([cross, cross], 0)
+    above = lax.dynamic_slice_in_dim(cross, level + 1, near, 0)
+    below = lax.dynamic_slice_in_dim(cross, level + 1 + near, near, 0)
     first = core == 0
+    leaving = jnp.where(first, below, above).astype(jnp.bfloat16)
+    cross = jnp.where(first, above, below) + lax.ppermute(leaving, EVERY, swap).astype(jnp.float32)
+    cross = folded(
+        jnp.moveaxis(cross, 1, 0),
+        side,
+        [(at(k, h, c), at(k ^ 1, h, c)) for k, c in blocks for h in range(CORES)],
+    )
     chip_block = jnp.stack(
         [jnp.where(first, scaled, crossed), jnp.where(first, crossed, mirrored)]
     )
     groups = [[at(k, 0, c) for c in range(cols)] for k in range(chips)] + [
         [at(k, 1, c) for k in range(chips)] for c in range(cols)
     ]
+    chip_block, cross = lax.optimization_barrier((chip_block, cross))
     panel = lax.all_to_all(
         jnp.broadcast_to(chip_block[None], (cols, *chip_block.shape)),
         EVERY,
@@ -97,30 +123,19 @@
         axis_index_groups=groups,
     )
 
-    weight_prev = mask_prev.astype(jnp.float32)
-    genotype = (weight_prev * (dosage_prev.astype(jnp.float32) - centre_prev)).astype(jnp.bfloat16)
-    cross = lax.dot_general(
-        genotype, expression, (((0,), (0,)), ((), ())), preferred_element_type=jnp.float32
-    )
-    out_rows = tested // rows
-    genes = expression.shape[1]
-    cross = cross.reshape(chips, CORES, out_rows, genes)
-    cross = folded(
-        jnp.moveaxis(cross, 1, 0),
-        core,
-        [(at(k, h, c), at(k, 1 - h, c)) for k, c in blocks for h in range(CORES)],
-    )
-    chip = row // CORES
-    span = 1
-    while span < chips:
-        bit = (chip // span) % 2
-        cross = folded(
-            jnp.moveaxis(cross.reshape(-1, 2, out_rows, genes), 1, 0),
-            bit,
-            [(at(k, h, c), at(k ^ span, h, c)) for k, c in blocks for h in range(CORES)],
-        )
-        span *= 2
-    cross = cross.reshape(out_rows, genes)
+    wire = cross.astype(jnp.bfloat16)
+    total_rows = jnp.where(first, 0.0, cross[near - 1])
+    for far in range(1, near + 1):
+        upward = [(at(k, 0, c), at((k + 2 * far) % chips, 0, c)) for k, c in blocks]
+        downward = [(at(k, 1, c), at((k - 2 * far) % chips, 1, c)) for k, c in blocks]
+        if far < near:
+            leaving = jnp.where(first, wire[far - 1], wire[near - 1 - far])
+            arrived = lax.ppermute(leaving, EVERY, upward + downward)
+        else:
+            arrived = lax.ppermute(wire[far - 1], EVERY, upward)
+        total_rows = total_rows + arrived.astype(jnp.float32)
+    shares = total_rows.reshape(CORES, out_rows, genes)
+    cross = half_of(shares, core) + lax.ppermute(half_of(shares, 1 - core), EVERY, swap)
     spread_rows = lax.dynamic_slice_in_dim(spread_prev, row * out_rows, out_rows, 0)
     power = squares / samples_all
     assoc_score = (
@@ -131,7 +146,6 @@
     )
 
     upper, lower = panel[:, 0], panel[:, 1]
-    swap = [(at(k, h, c), at(k, 1 - h, c)) for k, c in blocks for h in range(CORES)]
     other = lax.ppermute(jnp.where(first, lower, upper), EVERY, swap)
     rest = lax.ppermute(lower, EVERY, [(at(k, 1, c), at(k, 0, c)) for k, c in blocks])
 

time: 119 us -> 105 us (0.88)
  waiting for transfers between devices: 45.7 us -> 36.9 us
  starting transfers between devices: 58.1 us -> 56 us
  local copies, waits for them, and re-layouts: 5.29 us -> 3.33 us
  other arithmetic: 6.57 us -> 4.76 us
    ppermute x5 -> x8, starting transfers between devices: 19.4 us -> 32.6 us  [the longest x3 11.6 us: body(): arrived = lax.ppermute(leaving, EVERY, upward + downward)]
    all_to_all x1, starting transfers between devices: 12.9 us -> 5.83 us  [summed_over(): lax.all_to_all(sent, EVERY, 0, 0, tiled=True, axis_index_groups=groups)]
    ppermute x5 -> x8, waiting for transfers between devices: 32.4 us -> 27.6 us  [the longest x3 20.7 us: body(): arrived = lax.ppermute(leaving, EVERY, upward + downward)]
    all_to_all x1, waiting for transfers between devices: 13.3 us -> 9.31 us  [summed_over(): lax.all_to_all(sent, EVERY, 0, 0, tiled=True, axis_index_groups=groups)]
    all_to_all x1, starting transfers between devices: 14.2 us -> 10.5 us  [body(): lax.all_to_all(jnp.broadcast_to(chip_block[None], (cols, *chip_block.shap...]
    ppermute x1, starting transfers between devices: 5.46 us -> 1.92 us  [body(): other = lax.ppermute(jnp.where(first, lower, upper), EVERY, swap)]
    add x4 -> x3, other arithmetic: 2.23 us -> 0.31 us  [the longest x1 0.27 us: body(): jnp.where(first, above, below)]
    ppermute x1, starting transfers between devices: 3.37 us -> 1.92 us  [body(): lax.ppermute(scaled, EVERY, [(at(k, 1, c), at(k, 0, c)) for k, c in block...]
  transfers between devices with their start and end apart: 11 -> 14, of which waited for: 5 -> 7; matrix products, arithmetic and copies ran while one was open for 6% -> 2% of each run, Pallas kernels for 0% -> 0%
where the time goes in v2:
time: 105 us; the launch traced here: 104 us
  starting transfers between devices  56 us (53%)
  waiting for transfers between devices  36.9 us (35%)
  other arithmetic  4.76 us (5%)
  local copies, waits for them, and re-layouts  3.33 us (3%)
  matrix products  2.42 us (2%)
  between operations  1.09 us (1%)
    ppermute x3, waiting for transfers between devices, body(): arrived = lax.ppermute(leaving, EVERY, upward + downward)  20.7 us
    ppermute x3, starting transfers between devices, body(): arrived = lax.ppermute(leaving, EVERY, upward + downward)  11.6 us
    all_to_all x1, starting transfers between devices, body(): lax.all_to_all(jnp.broadcast_to(chip_block[None], (cols, *chip_block.shap...  10.5 us
    all_to_all x1, waiting for transfers between devices, summed_over(): lax.all_to_all(sent, EVERY, 0, 0, tiled=True, axis_index_groups=groups)  9.31 us
    ppermute x1, starting transfers between devices, body(): partial = partial + lax.ppermute(partial, EVERY, swap)  8.79 us
    all_to_all x1, starting transfers between devices, summed_over(): lax.all_to_all(sent, EVERY, 0, 0, tiled=True, axis_index_groups=groups)  5.83 us
    ppermute x1, starting transfers between devices, folded(): lax.ppermute(leaving, EVERY, pairs).astype(jnp.float32)  5.63 us
    ppermute x1, waiting for transfers between devices, folded(): lax.ppermute(leaving, EVERY, pairs).astype(jnp.float32)  4.93 us
  transfers between devices with their start and end apart: 14, of which 7 were waited for; matrix products, arithmetic and copies ran while one was open for 2% of the time, Pallas kernels for 0%

profile of v2, /device:TPU:1, one launch (start us, length us, event | category | flops | bytes accessed | tf_op | source)
XLA Modules:
  0.0 104.4 jit_solution(9679873024734846676)
XLA Ops:
  0.6 1.0 fusion.15
  1.6 1.0 fusion.16
  2.7 1.1 %multiply_reduce_fusion = f32[1280]{0:T(1024)S(1)} fusion(bf16[128,1280]{1,0:T(8,128)(2,1)} %param.11), kind=kLoop, calls=%fused_computation.18 | loop fusion | flops 490240 | bytes 332800 | tf_op jit(solution)/shard_map/reduce_sum | solution.py:61
  3.7 8.8 %collective-permute-start = (f32[2816]{0:T(1024)S(1)}, f32[2816]{0:T(1024)S(1)}, u32[]{:S(2)}, u32[]{:S(2)}) collective-permute-start(f32[2816]{0:T(1024)S(1)} %pad_maximum_fusion.1), channel_id=1, source_target_pairs={{0,16},{16,0},{1,17},{17,1},{2,18},{18,2},{3,19},{19,3},{4,20},{20... | collective-permute-start | bytes 33800 | tf_op jit(solution)/shard_map/ppermute | solution.py:64
  12.5 0.8 collective-permute-done
  13.4 0.8 broadcast_in_dim.7
  14.1 5.8 %all-to-all-start = ((f32[16,1,2816]{2,1,0:T(1,128)}), f32[16,1,2816]{2,1,0:T(1,128)S(1)}, u32[]{:S(2)}, u32[]{:S(2)}) async-start(f32[16,1,2816]{2,1,0:T(1,128)} %broadcast_in_dim.7), calls=%async_computation | async-start | bytes 360448 | tf_op jit(solution)/shard_map/all_to_all | solution.py:24
  20.0 9.3 %all-to-all-done = f32[16,1,2816]{2,1,0:T(1,128)S(1)} async-done(((f32[16,1,2816]{2,1,0:T(1,128)}), f32[16,1,2816]{2,1,0:T(1,128)S(1)}, u32[]{:S(2)}, u32[]{:S(2)}) %all-to-all-start) | async-done | bytes 180256 | tf_op jit(solution)/shard_map/all_to_all | solution.py:24
  29.5 1.4 %fusion.21 = f32[256,1280]{1,0:T(8,128)S(1)} fusion(bf16[128,1280]{1,0:T(8,128)(2,1)} %param.11, bf16[128,256]{1,0:T(8,128)(2,1)} %param.9, s32[128,256]{1,0:T(8,128)} %param.10, f32[256]{0:T(256)S(1)} %get-tuple-element.21), kind=kOutput, calls=%fused_computation.47 | convolution fusion | flops 84049920 | bytes 1836032 | tf_op jit(solution)/shard_map/dot_general | solution.py:89
  31.1 4.1 %collective-permute-start.3 = (bf16[4,2,16,1280]{3,2,1,0:T(8,128)(2,1)S(1)}, bf16[4,2,16,1280]{3,2,1,0:T(8,128)(2,1)S(1)}, u32[]{:S(2)}, u32[]{:S(2)}) collective-permute-start(bf16[4,2,16,1280]{3,2,1,0:T(8,128)(2,1)S(1)} %select_convert_fusion), channel_id=1, source_target_pairs={{0,16},{16,0},{1,17},{17,1},{2,18},{18,2},{3,19},{19,3},{4,20},{20... | collective-permute-start | bytes 983048 | tf_op jit(solution)/shard_map/ppermute | solution.py:104
  35.3 1.9 %collective-permute-start.1 = (bf16[128,256]{1,0:T(8,128)(2,1)S(1)}, bf16[128,256]{1,0:T(8,128)(2,1)S(1)}, u32[]{:S(2)}, u32[]{:S(2)}) collective-permute-start(bf16[128,256]{1,0:T(8,128)(2,1)S(1)} %fusion.10), channel_id=1, source_target_pairs={{16,0},{17,1},{18,2},{19,3},{20,4},{21,5},{22,6},{23,7},{24,8},{25... | collective-permute-start | bytes 196616 | tf_op jit(solution)/shard_map/ppermute | solution.py:78
  37.2 0.7 collective-permute-start.2
  37.9 0.3 convert_add_fusion
  38.2 5.6 %collective-permute-start.4 = (bf16[4,16,1280]{2,1,0:T(8,128)(2,1)S(1)}, bf16[4,16,1280]{2,1,0:T(8,128)(2,1)S(1)}, u32[]{:S(2)}, u32[]{:S(2)}) collective-permute-start(bf16[4,16,1280]{2,1,0:T(8,128)(2,1)S(1)} %fusion.6), channel_id=1, source_target_pairs={{0,32},{16,48},{1,33},{17,49},{2,34},{18,50},{3,35},{19,51},{4,36}... | collective-permute-start | bytes 491528 | tf_op jit(solution)/shard_map/ppermute | solution.py:41
  43.9 4.9 %collective-permute-done.4 = bf16[4,16,1280]{2,1,0:T(8,128)(2,1)S(1)} collective-permute-done((bf16[4,16,1280]{2,1,0:T(8,128)(2,1)S(1)}, bf16[4,16,1280]{2,1,0:T(8,128)(2,1)S(1)}, u32[]{:S(2)}, u32[]{:S(2)}) %collective-permute-start.4) | collective-permute-done | bytes 163872 | tf_op jit(solution)/shard_map/ppermute | solution.py:41
  48.9 1.6 %broadcast_in_dim.8 = bf16[16,2,128,256]{3,2,1,0:T(8,128)(2,1)} broadcast(bf16[2,128,256]{2,1,0:T(8,128)(2,1)S(1)} %pad_maximum_fusion), dimensions={1,2,3} | broadcast | bytes 2228224 | tf_op jit(solution)/shard_map/broadcast_in_dim | solution.py:118
  50.5 10.5 %all-to-all-start.1 = ((bf16[16,2,128,256]{3,2,1,0:T(8,128)(2,1)}), bf16[16,2,128,256]{3,2,1,0:T(8,128)(2,1)S(1)}, u32[]{:S(2)}, u32[]{:S(2)}) async-start(bf16[16,2,128,256]{3,2,1,0:T(8,128)(2,1)} %broadcast_in_dim.8), calls=%async_computation.1 | async-start | bytes 4194304 | tf_op jit(solution)/shard_map/all_to_all | solution.py:117
  61.2 0.7 collective-permute-start.10
  61.9 4.5 %collective-permute-start.7 = (bf16[16,1280]{1,0:T(8,128)(2,1)S(1)}, bf16[16,1280]{1,0:T(8,128)(2,1)S(1)}, u32[]{:S(2)}, u32[]{:S(2)}) collective-permute-start(bf16[16,1280]{1,0:T(8,128)(2,1)S(1)} %get-tuple-element.24), channel_id=1, source_target_pairs={{0,64},{1,65},{2,66},{3,67},{4,68},{5,69},{6,70},{7,71},{8,72},{9,... | collective-permute-start | bytes 122888 | tf_op jit(solution)/shard_map/ppermute | solution.py:133
  66.3 4.0 %collective-permute-start.8 = (bf16[16,1280]{1,0:T(8,128)(2,1)S(1)}, bf16[16,1280]{1,0:T(8,128)(2,1)S(1)}, u32[]{:S(2)}, u32[]{:S(2)}) collective-permute-start(bf16[16,1280]{1,0:T(8,128)(2,1)S(1)} %get-tuple-element.26), channel_id=1, source_target_pairs={{0,128},{1,129},{2,130},{3,131},{4,132},{5,133},{6,134},{7,135},{8... | collective-permute-start | bytes 122888 | tf_op jit(solution)/shard_map/ppermute | solution.py:133
  70.3 3.1 %collective-permute-start.9 = (bf16[16,1280]{1,0:T(8,128)(2,1)S(1)}, bf16[16,1280]{1,0:T(8,128)(2,1)S(1)}, u32[]{:S(2)}, u32[]{:S(2)}) collective-permute-start(bf16[16,1280]{1,0:T(8,128)(2,1)S(1)} %get-tuple-element.27), channel_id=1, source_target_pairs={{0,192},{1,193},{2,194},{3,195},{4,196},{5,197},{6,198},{7,199},{8... | collective-permute-start | bytes 122888 | tf_op jit(solution)/shard_map/ppermute | solution.py:133
  73.5 15.4 %collective-permute-done.7 = bf16[16,1280]{1,0:T(8,128)(2,1)S(1)} collective-permute-done((bf16[16,1280]{1,0:T(8,128)(2,1)S(1)}, bf16[16,1280]{1,0:T(8,128)(2,1)S(1)}, u32[]{:S(2)}, u32[]{:S(2)}) %collective-permute-start.7) | collective-permute-done | bytes 40992 | tf_op jit(solution)/shard_map/ppermute | solution.py:133
  88.9 1.9 %collective-permute-done.8 = bf16[16,1280]{1,0:T(8,128)(2,1)S(1)} collective-permute-done((bf16[16,1280]{1,0:T(8,128)(2,1)S(1)}, bf16[16,1280]{1,0:T(8,128)(2,1)S(1)}, u32[]{:S(2)}, u32[]{:S(2)}) %collective-permute-start.8) | collective-permute-done | bytes 40992 | tf_op jit(solution)/shard_map/ppermute | solution.py:133
  90.8 3.4 %collective-permute-done.9 = bf16[16,1280]{1,0:T(8,128)(2,1)S(1)} collective-permute-done((bf16[16,1280]{1,0:T(8,128)(2,1)S(1)}, bf16[16,1280]{1,0:T(8,128)(2,1)S(1)}, u32[]{:S(2)}, u32[]{:S(2)}) %collective-permute-start.9) | collective-permute-done | bytes 40992 | tf_op jit(solution)/shard_map/ppermute | solution.py:133
  94.3 1.9 %collective-permute-start.5 = (bf16[16,128,256]{2,1,0:T(8,128)(2,1)S(1)}, bf16[16,128,256]{2,1,0:T(8,128)(2,1)S(1)}, u32[]{:S(2)}, u32[]{:S(2)}) collective-permute-start(bf16[16,128,256]{2,1,0:T(8,128)(2,1)S(1)} %broadcast_select_fusion.1), channel_id=1, source_target_pairs={{0,16},{16,0},{1,17},{17,1},{2,18},{18,2},{3,19},{19,3},{4,20},{20... | collective-permute-start | bytes 3145736 | tf_op jit(solution)/shard_map/ppermute | solution.py:149
  96.4 2.5 %collective-permute-start.6 = (bf16[16,128,256]{2,1,0:T(8,128)(2,1)S(1)}, bf16[16,128,256]{2,1,0:T(8,128)(2,1)S(1)}, u32[]{:S(2)}, u32[]{:S(2)}) collective-permute-start(bf16[16,128,256]{2,1,0:T(8,128)(2,1)S(1)} %slice_bitcast_fusion), channel_id=1, source_target_pairs={{16,0},{17,1},{18,2},{19,3},{20,4},{21,5},{22,6},{23,7},{24,8},{25... | collective-permute-start | bytes 3145736 | tf_op jit(solution)/shard_map/ppermute | solution.py:150
  98.8 1.9 %collective-permute-start.11 = (f32[8,1280]{1,0:T(8,128)S(1)}, f32[8,1280]{1,0:T(8,128)S(1)}, u32[]{:S(2)}, u32[]{:S(2)}) collective-permute-start(f32[8,1280]{1,0:T(8,128)S(1)} %dynamic-slice_bitcast_fusion), channel_id=1, source_target_pairs={{0,16},{16,0},{1,17},{17,1},{2,18},{18,2},{3,19},{19,3},{4,20},{20... | collective-permute-start | bytes 122888 | tf_op jit(solution)/shard_map/ppermute | solution.py:138
  100.9 1.1 %collective-permute-done.11 = f32[8,1280]{1,0:T(8,128)S(1)} collective-permute-done((f32[8,1280]{1,0:T(8,128)S(1)}, f32[8,1280]{1,0:T(8,128)S(1)}, u32[]{:S(2)}, u32[]{:S(2)}) %collective-permute-start.11) | collective-permute-done | bytes 40992 | tf_op jit(solution)/shard_map/ppermute | solution.py:138
  102.0 0.7 fusion.26
  102.7 0.5 convolution_bitcast_fusion.1
  103.2 0.5 convolution_bitcast_fusion
  103.7 0.8 copy.19
  (37 shorter events, 1.0 us)
Async XLA Ops:
  3.7 9.6 %collective-permute-start = (f32[2816]{0:T(1024)S(1)}, f32[2816]{0:T(1024)S(1)}, u32[]{:S(2)}, u32[]{:S(2)}) collective-permute-start(f32[2816]{0:T(1024)S(1)} %pad_maximum_fusion.1), channel_id=1, source_target_pairs={{0,16},{16,0},{1,17},{17,1},{2,18},{18,2},{3,19},{19,3},{4,20},{20... | collective-permute-start | bytes 33800 | tf_op jit(solution)/shard_map/ppermute | solution.py:64
  14.1 21.1 %copy-start = (s32[128,256]{1,0:T(8,128)S(1)}, s32[128,256]{1,0:T(8,128)}, u32[]{:S(2)}) copy-start(s32[128,256]{1,0:T(8,128)} %param.8) | copy-start | bytes 393220
  14.1 21.1 %copy-start.1 = (bf16[128,256]{1,0:T(8,128)(2,1)S(1)}, bf16[128,256]{1,0:T(8,128)(2,1)}, u32[]{:S(2)}) copy-start(bf16[128,256]{1,0:T(8,128)(2,1)} %param.7) | copy-start | bytes 196612
  14.1 15.2 %all-to-all-start = ((f32[16,1,2816]{2,1,0:T(1,128)}), f32[16,1,2816]{2,1,0:T(1,128)S(1)}, u32[]{:S(2)}, u32[]{:S(2)}) async-start(f32[16,1,2816]{2,1,0:T(1,128)} %broadcast_in_dim.7), calls=%async_computation | async-start | bytes 360448 | tf_op jit(solution)/shard_map/all_to_all | solution.py:24
  31.1 6.8 %collective-permute-start.3 = (bf16[4,2,16,1280]{3,2,1,0:T(8,128)(2,1)S(1)}, bf16[4,2,16,1280]{3,2,1,0:T(8,128)(2,1)S(1)}, u32[]{:S(2)}, u32[]{:S(2)}) collective-permute-start(bf16[4,2,16,1280]{3,2,1,0:T(8,128)(2,1)S(1)} %select_convert_fusion), channel_id=1, source_target_pairs={{0,16},{16,0},{1,17},{17,1},{2,18},{18,2},{3,19},{19,3},{4,20},{20... | collective-permute-start | bytes 983048 | tf_op jit(solution)/shard_map/ppermute | solution.py:104
  35.3 8.6 %collective-permute-start.1 = (bf16[128,256]{1,0:T(8,128)(2,1)S(1)}, bf16[128,256]{1,0:T(8,128)(2,1)S(1)}, u32[]{:S(2)}, u32[]{:S(2)}) collective-permute-start(bf16[128,256]{1,0:T(8,128)(2,1)S(1)} %fusion.10), channel_id=1, source_target_pairs={{16,0},{17,1},{18,2},{19,3},{20,4},{21,5},{22,6},{23,7},{24,8},{25... | collective-permute-start | bytes 196616 | tf_op jit(solution)/shard_map/ppermute | solution.py:78
  37.2 6.6 %collective-permute-start.2 = (bf16[128,256]{1,0:T(8,128)(2,1)S(1)}, bf16[128,256]{1,0:T(8,128)(2,1)S(1)}, u32[]{:S(2)}, u32[]{:S(2)}) collective-permute-start(bf16[128,256]{1,0:T(8,128)(2,1)S(1)} %fusion.10), channel_id=1, source_target_pairs={{16,16},{48,17},{80,18},{112,19},{144,20},{176,21},{208,22},{240,2... | collective-permute-start | bytes 196616 | tf_op jit(solution)/shard_map/ppermute | solution.py:84
  38.2 10.6 %collective-permute-start.4 = (bf16[4,16,1280]{2,1,0:T(8,128)(2,1)S(1)}, bf16[4,16,1280]{2,1,0:T(8,128)(2,1)S(1)}, u32[]{:S(2)}, u32[]{:S(2)}) collective-permute-start(bf16[4,16,1280]{2,1,0:T(8,128)(2,1)S(1)} %fusion.6), channel_id=1, source_target_pairs={{0,32},{16,48},{1,33},{17,49},{2,34},{18,50},{3,35},{19,51},{4,36}... | collective-permute-start | bytes 491528 | tf_op jit(solution)/shard_map/ppermute | solution.py:41
  50.5 10.6 %copy-start.2 = (f32[128,256]{1,0:T(8,128)S(1)}, f32[128,256]{1,0:T(8,128)}, u32[]{:S(2)}) copy-start(f32[128,256]{1,0:T(8,128)} %param.6) | copy-start | bytes 393220
  50.5 43.8 %all-to-all-start.1 = ((bf16[16,2,128,256]{3,2,1,0:T(8,128)(2,1)}), bf16[16,2,128,256]{3,2,1,0:T(8,128)(2,1)S(1)}, u32[]{:S(2)}, u32[]{:S(2)}) async-start(bf16[16,2,128,256]{3,2,1,0:T(8,128)(2,1)} %broadcast_in_dim.8), calls=%async_computation.1 | async-start | bytes 4194304 | tf_op jit(solution)/shard_map/all_to_all | solution.py:117
  61.2 12.3 %collective-permute-start.10 = (bf16[16,1280]{1,0:T(8,128)(2,1)S(1)}, bf16[16,1280]{1,0:T(8,128)(2,1)S(1)}, u32[]{:S(2)}, u32[]{:S(2)}) collective-permute-start(bf16[16,1280]{1,0:T(8,128)(2,1)S(1)} %get-tuple-element.25), channel_id=1, source_target_pairs={{0,256},{1,257},{2,258},{3,259},{4,260},{5,261},{6,262},{7,263},{8... | collective-permute-start | bytes 122888 | tf_op jit(solution)/shard_map/ppermute | solution.py:135
  61.9 27.0 %collective-permute-start.7 = (bf16[16,1280]{1,0:T(8,128)(2,1)S(1)}, bf16[16,1280]{1,0:T(8,128)(2,1)S(1)}, u32[]{:S(2)}, u32[]{:S(2)}) collective-permute-start(bf16[16,1280]{1,0:T(8,128)(2,1)S(1)} %get-tuple-element.24), channel_id=1, source_target_pairs={{0,64},{1,65},{2,66},{3,67},{4,68},{5,69},{6,70},{7,71},{8,72},{9,... | collective-permute-start | bytes 122888 | tf_op jit(solution)/shard_map/ppermute | solution.py:133
  66.3 24.5 %collective-permute-start.8 = (bf16[16,1280]{1,0:T(8,128)(2,1)S(1)}, bf16[16,1280]{1,0:T(8,128)(2,1)S(1)}, u32[]{:S(2)}, u32[]{:S(2)}) collective-permute-start(bf16[16,1280]{1,0:T(8,128)(2,1)S(1)} %get-tuple-element.26), channel_id=1, source_target_pairs={{0,128},{1,129},{2,130},{3,131},{4,132},{5,133},{6,134},{7,135},{8... | collective-permute-start | bytes 122888 | tf_op jit(solution)/shard_map/ppermute | solution.py:133
  70.3 23.8 %collective-permute-start.9 = (bf16[16,1280]{1,0:T(8,128)(2,1)S(1)}, bf16[16,1280]{1,0:T(8,128)(2,1)S(1)}, u32[]{:S(2)}, u32[]{:S(2)}) collective-permute-start(bf16[16,1280]{1,0:T(8,128)(2,1)S(1)} %get-tuple-element.27), channel_id=1, source_target_pairs={{0,192},{1,193},{2,194},{3,195},{4,196},{5,197},{6,198},{7,199},{8... | collective-permute-start | bytes 122888 | tf_op jit(solution)/shard_map/ppermute | solution.py:133
  94.3 8.3 %collective-permute-start.5 = (bf16[16,128,256]{2,1,0:T(8,128)(2,1)S(1)}, bf16[16,128,256]{2,1,0:T(8,128)(2,1)S(1)}, u32[]{:S(2)}, u32[]{:S(2)}) collective-permute-start(bf16[16,128,256]{2,1,0:T(8,128)(2,1)S(1)} %broadcast_select_fusion.1), channel_id=1, source_target_pairs={{0,16},{16,0},{1,17},{17,1},{2,18},{18,2},{3,19},{19,3},{4,20},{20... | collective-permute-start | bytes 3145736 | tf_op jit(solution)/shard_map/ppermute | solution.py:149
  96.4 6.8 %collective-permute-start.6 = (bf16[16,128,256]{2,1,0:T(8,128)(2,1)S(1)}, bf16[16,128,256]{2,1,0:T(8,128)(2,1)S(1)}, u32[]{:S(2)}, u32[]{:S(2)}) collective-permute-start(bf16[16,128,256]{2,1,0:T(8,128)(2,1)S(1)} %slice_bitcast_fusion), channel_id=1, source_target_pairs={{16,0},{17,1},{18,2},{19,3},{20,4},{21,5},{22,6},{23,7},{24,8},{25... | collective-permute-start | bytes 3145736 | tf_op jit(solution)/shard_map/ppermute | solution.py:150
  98.8 3.1 %collective-permute-start.11 = (f32[8,1280]{1,0:T(8,128)S(1)}, f32[8,1280]{1,0:T(8,128)S(1)}, u32[]{:S(2)}, u32[]{:S(2)}) collective-permute-start(f32[8,1280]{1,0:T(8,128)S(1)} %dynamic-slice_bitcast_fusion), channel_id=1, source_target_pairs={{0,16},{16,0},{1,17},{17,1},{2,18},{18,2},{3,19},{19,3},{4,20},{20... | collective-permute-start | bytes 122888 | tf_op jit(solution)/shard_map/ppermute | solution.py:138

commit v3 on v2

--- a/solution.py
+++ b/solution.py
@@ -37,8 +37,33 @@
 
 
 def folded(stacked, bit, pairs):
-    leaving = half_of(stacked, 1 - bit).astype(jnp.bfloat16)
-    return half_of(stacked, bit) + lax.ppermute(leaving, EVERY, pairs).astype(jnp.float32)
+    return half_of(stacked, bit) + lax.ppermute(half_of(stacked, 1 - bit), EVERY, pairs)
+
+
+def landing(chips, cols):
+    sides, tall, wide = 2, chips // 2, cols // 2
+    steps = sorted(range(wide), key=lambda d: min(d, wide - d))
+    climbs = sorted(range(tall), key=lambda d: -min(d, tall - d))
+    table = []
+    for c in range(cols):
+        z, low, high, y = c // sides, c % sides, c // wide, c % wide
+        targets = [0] * cols
+        for step, climb in zip(steps, climbs):
+            sources = [half * wide + (y + step) % wide for half in range(2)]
+            ends = [(z + climb) % tall * sides + side for side in range(sides)]
+
+            def reach(source, end):
+                gap = (source // wide * 2 + low - high * 2 - end % sides) % 4
+                return min(gap, 4 - gap)
+
+            straight = [reach(sources[i], ends[i]) for i in range(2)]
+            turned = [reach(sources[i], ends[1 - i]) for i in range(2)]
+            if max(turned) < max(straight):
+                ends = ends[::-1]
+            for source, end in zip(sources, ends):
+                targets[source] = end
+        table.append(targets)
+    return table
 
 
 def body(grm_prior, dosage_now, mask_now, dosage_prev, mask_prev, expression):
@@ -53,6 +78,7 @@
     def at(chip, half, column):
         return (chip * CORES + half) * cols + column
 
+    lands = landing(chips, cols)
     blocks = [(k, c) for k in range(chips) for c in range(cols)]
 
     traits = expression.astype(jnp.float32)
@@ -70,6 +96,19 @@
     )
     squares = total[3 * (width + tested) :]
 
+    chip = row // CORES
+    level, side = chip // 2, chip % 2
+    across = [(at(k, h, c), at(k ^ 1, h, c)) for k, c in blocks for h in range(CORES)]
+    genes = expression.shape[1]
+    share = genes // 2
+    halves = expression.reshape(-1, 2, share)
+    weight_prev = mask_prev.astype(jnp.bfloat16)
+    tested_raw = [weight_prev * dosage_prev, weight_prev]
+    raw = jnp.concatenate([half_of(halves, 1 - side, 1), *tested_raw], 1)
+    held = jnp.concatenate([half_of(halves, side, 1), *tested_raw], 1)
+    held = jnp.concatenate([held, lax.ppermute(raw, EVERY, across)], 0)
+    held = jnp.concatenate([held, lax.ppermute(held, EVERY, swap)], 0)
+
     weight_now = mask_now.astype(jnp.float32)
     scaled = (
         weight_now * (dosage_now.astype(jnp.float32) - centre_now)
@@ -79,39 +118,27 @@
         scaled,
         EVERY,
         [(at(k, 1, c), at(k, 0, c)) for k, c in blocks]
-        + [(at(c, 0, k), at(k, 1, c)) for k, c in blocks],
+        + [(at(c, 0, v), at(lands[c][v], 1, c)) for c, v in blocks],
     )
     mirrored = lax.ppermute(
-        scaled, EVERY, [(at(c, 1, k), at(k, 1, c)) for k, c in blocks]
-    )
-    weight_prev = mask_prev.astype(jnp.float32)
-    genotype = (weight_prev * (dosage_prev.astype(jnp.float32) - centre_prev)).astype(jnp.bfloat16)
+        scaled, EVERY, [(at(c, 1, v), at(lands[c][v], 1, c)) for c, v in blocks]
+    )
+    genotype = (
+        held[:, share + tested :].astype(jnp.float32)
+        * (held[:, share : share + tested].astype(jnp.float32) - centre_prev)
+    ).astype(jnp.bfloat16)
+    layers = chips // 2
+    near = layers // 2
+    out_rows = tested // rows
     cross = lax.dot_general(
-        genotype, expression, (((0,), (0,)), ((), ())), preferred_element_type=jnp.float32
-    )
-    out_rows = tested // rows
-    genes = expression.shape[1]
-    layers = chips // 2
-    chip = row // CORES
-    level, side = chip // 2, chip % 2
-    near = layers // 2
-    cross = cross.reshape(layers, 2, CORES * out_rows, genes)
-    cross = jnp.concatenate([cross, cross], 0)
-    above = lax.dynamic_slice_in_dim(cross, level + 1, near, 0)
-    below = lax.dynamic_slice_in_dim(cross, level + 1 + near, near, 0)
+        genotype, held[:, :share], (((0,), (0,)), ((), ())), preferred_element_type=jnp.float32
+    ).reshape(layers, 2 * CORES * out_rows, share)
     first = core == 0
-    leaving = jnp.where(first, below, above).astype(jnp.bfloat16)
-    cross = jnp.where(first, above, below) + lax.ppermute(leaving, EVERY, swap).astype(jnp.float32)
-    cross = folded(
-        jnp.moveaxis(cross, 1, 0),
-        side,
-        [(at(k, h, c), at(k ^ 1, h, c)) for k, c in blocks for h in range(CORES)],
-    )
     chip_block = jnp.stack(
         [jnp.where(first, scaled, crossed), jnp.where(first, crossed, mirrored)]
     )
     groups = [[at(k, 0, c) for c in range(cols)] for k in range(chips)] + [
-        [at(k, 1, c) for k in range(chips)] for c in range(cols)
+        [at(k, 1, c) for k in lands[c]] for c in range(cols)
     ]
     chip_block, cross = lax.optimization_barrier((chip_block, cross))
     panel = lax.all_to_all(
@@ -123,19 +150,33 @@
         axis_index_groups=groups,
     )
 
-    wire = cross.astype(jnp.bfloat16)
-    total_rows = jnp.where(first, 0.0, cross[near - 1])
+    kept = jnp.where(first, 0.0, lax.dynamic_index_in_dim(cross, level, 0, keepdims=False))
+    arrivals = []
     for far in range(1, near + 1):
-        upward = [(at(k, 0, c), at((k + 2 * far) % chips, 0, c)) for k, c in blocks]
-        downward = [(at(k, 1, c), at((k - 2 * far) % chips, 1, c)) for k, c in blocks]
+        routes = [(at(k, 0, c), at((k + 2 * far) % chips, 0, c)) for k, c in blocks]
+        goal = (level + far) % layers
         if far < near:
-            leaving = jnp.where(first, wire[far - 1], wire[near - 1 - far])
-            arrived = lax.ppermute(leaving, EVERY, upward + downward)
-        else:
-            arrived = lax.ppermute(wire[far - 1], EVERY, upward)
-        total_rows = total_rows + arrived.astype(jnp.float32)
-    shares = total_rows.reshape(CORES, out_rows, genes)
-    cross = half_of(shares, core) + lax.ppermute(half_of(shares, 1 - core), EVERY, swap)
+            routes += [(at(k, 1, c), at((k - 2 * far) % chips, 1, c)) for k, c in blocks]
+            goal = jnp.where(first, goal, (level + layers - far) % layers)
+        leaving = lax.dynamic_index_in_dim(cross, goal, 0, keepdims=False)
+        arrivals.append(lax.ppermute(leaving, EVERY, routes))
+
+    upper, lower = panel[:, 0], panel[:, 1]
+    leaving, kept = lax.optimization_barrier((jnp.where(first, lower, upper), kept))
+    other = lax.ppermute(leaving, EVERY, swap)
+    rest = lax.ppermute(lower, EVERY, [(at(k, 1, c), at(k, 0, c)) for k, c in blocks])
+
+    total_rows = kept
+    for arrived in arrivals:
+        total_rows = total_rows + arrived
+    shares = folded(
+        jnp.moveaxis(total_rows.reshape(2, CORES, out_rows, share), 1, 0), core, swap
+    )
+    own, other_half = half_of(shares, side), lax.ppermute(half_of(shares, 1 - side), EVERY, across)
+    left_chip = side == 0
+    cross = jnp.concatenate(
+        [jnp.where(left_chip, own, other_half), jnp.where(left_chip, other_half, own)], 1
+    )
     spread_rows = lax.dynamic_slice_in_dim(spread_prev, row * out_rows, out_rows, 0)
     power = squares / samples_all
     assoc_score = (
@@ -145,10 +186,6 @@
         / math.sqrt(samples_all)
     )
 
-    upper, lower = panel[:, 0], panel[:, 1]
-    other = lax.ppermute(jnp.where(first, lower, upper), EVERY, swap)
-    rest = lax.ppermute(lower, EVERY, [(at(k, 1, c), at(k, 0, c)) for k, c in blocks])
-
     def product(a, b):
         return lax.dot_general(
             a, b, (((0, 2), (0, 2)), ((), ())), preferred_element_type=jnp.float32

time: 105 us -> 103 us (0.981)
  waiting for transfers between devices: 36.9 us -> 34.5 us
  local copies, waits for them, and re-layouts: 3.33 us -> 4.87 us
  matrix products: 2.42 us -> 1.32 us
    ppermute x9 -> x10, waiting for transfers between devices: 26.8 us -> 4.71 us  [the longest x1 1.68 us: body(): lax.ppermute(scaled, EVERY, [(at(c, 1, v), at(lands[c][v], 1, c)) for c,...]
    all_to_all x1, waiting for transfers between devices: 0.01 us -> 20.2 us  [body(): lax.all_to_all(jnp.broadcast_to(chip_block[None], (cols, *chip_block.shap...]
    ppermute x1, waiting for transfers between devices: 0.01 us -> 4.8 us  [body(): lax.ppermute(scaled, EVERY, [(at(k, 1, c), at(k, 0, c)) for k, c in block...]
    all_to_all x1, waiting for transfers between devices: 9.31 us -> 4.85 us  [summed_over(): lax.all_to_all(sent, EVERY, 0, 0, tiled=True, axis_index_groups=groups)]
    ppermute x1, starting transfers between devices: 1.92 us -> 3.92 us  [body(): lax.ppermute(scaled, EVERY, [(at(k, 1, c), at(k, 0, c)) for k, c in block...]
    ppermute x9 -> x10, starting transfers between devices: 26.4 us -> 25.1 us  [the longest x4 10.2 us: body(): arrivals.append(lax.ppermute(leaving, EVERY, routes))]
    unnamed x8 -> x13, local copies, waits for them, and re-layouts: 0.86 us -> 2.05 us
  transfers between devices with their start and end apart: 14 -> 15, of which waited for: 7 -> 6; matrix products, arithmetic and copies ran while one was open for 2% -> 4% of each run, Pallas kernels for 0% -> 0%
where the time goes in v3:
time: 103 us; the launch traced here: 102 us
  starting transfers between devices  55.4 us (54%)
  waiting for transfers between devices  34.5 us (33%)
  local copies, waits for them, and re-layouts  4.87 us (5%)
  other arithmetic  4.4 us (4%)
  matrix products  1.32 us (1%)
  between operations  1.16 us (1%)
    all_to_all x1, waiting for transfers between devices, body(): lax.all_to_all(jnp.broadcast_to(chip_block[None], (cols, *chip_block.shap...  20.2 us
    ppermute x4, starting transfers between devices, body(): arrivals.append(lax.ppermute(leaving, EVERY, routes))  10.2 us
    all_to_all x1, starting transfers between devices, body(): lax.all_to_all(jnp.broadcast_to(chip_block[None], (cols, *chip_block.shap...  9.59 us
    ppermute x1, starting transfers between devices, body(): partial = partial + lax.ppermute(partial, EVERY, swap)  8.79 us
    all_to_all x1, starting transfers between devices, summed_over(): lax.all_to_all(sent, EVERY, 0, 0, tiled=True, axis_index_groups=groups)  5.97 us
    all_to_all x1, waiting for transfers between devices, summed_over(): lax.all_to_all(sent, EVERY, 0, 0, tiled=True, axis_index_groups=groups)  4.85 us
    ppermute x1, waiting for transfers between devices, body(): lax.ppermute(scaled, EVERY, [(at(k, 1, c), at(k, 0, c)) for k, c in block...  4.8 us
    ppermute x1, starting transfers between devices, body(): lax.ppermute(scaled, EVERY, [(at(k, 1, c), at(k, 0, c)) for k, c in block...  3.92 us
  transfers between devices with their start and end apart: 15, of which 6 were waited for; matrix products, arithmetic and copies ran while one was open for 4% of the time, Pallas kernels for 0%

profile of v3, /device:TPU:1, one launch (start us, length us, event | category | flops | bytes accessed | tf_op | source)
XLA Modules:
  0.0 101.7 jit_solution(7642498452278566589)
XLA Ops:
  0.7 1.0 %fusion.32 = (f32[256]{0:T(256)S(1)}, f32[256]{0:T(256)S(1)}, f32[256]{0:T(256)S(1)}) fusion(bf16[128,256]{1,0:T(8,128)(2,1)} %param.7, s32[128,256]{1,0:T(8,128)} %param.8), kind=kLoop, calls=%fused_computation.55 | loop fusion | flops 228608 | bytes 199680 | tf_op jit(solution)/shard_map/reduce_sum | solution.py:18
  1.7 1.0 fusion.31
  2.7 1.1 %multiply_reduce_fusion = f32[1280]{0:T(1024)S(1)} fusion(bf16[128,1280]{1,0:T(8,128)(2,1)} %param.11), kind=kLoop, calls=%fused_computation.16 | loop fusion | flops 490240 | bytes 332800 | tf_op jit(solution)/shard_map/reduce_sum | solution.py:87
  3.8 8.8 %collective-permute-start = (f32[2816]{0:T(1024)S(1)}, f32[2816]{0:T(1024)S(1)}, u32[]{:S(2)}, u32[]{:S(2)}) collective-permute-start(f32[2816]{0:T(1024)S(1)} %pad_maximum_fusion.11), channel_id=1, source_target_pairs={{0,16},{16,0},{1,17},{17,1},{2,18},{18,2},{3,19},{19,3},{4,20},{20... | collective-permute-start | bytes 33800 | tf_op jit(solution)/shard_map/ppermute | solution.py:90
  12.6 1.2 %copy.30 = bf16[128,1280]{0,1:T(8,128)(2,1)S(1)} copy(bf16[128,1280]{1,0:T(8,128)(2,1)} %param.11) | data formatting | bytes 655360 | tf_op args[5]
  14.1 2.1 %collective-permute-start.3 = (bf16[128,1152]{1,0:T(8,128)(2,1)S(1)}, bf16[128,1152]{1,0:T(8,128)(2,1)S(1)}, u32[]{:S(2)}, u32[]{:S(2)}) collective-permute-start(bf16[128,1152]{1,0:T(8,128)(2,1)S(1)} %pad_maximum_fusion.9), channel_id=1, source_target_pairs={{0,32},{16,48},{1,33},{17,49},{2,34},{18,50},{3,35},{19,51},{4,36}... | collective-permute-start | bytes 884744 | tf_op jit(solution)/shard_map/ppermute | solution.py:109
  16.2 0.8 broadcast_in_dim.7
  17.0 6.0 %all-to-all-start = ((f32[16,1,2816]{2,1,0:T(1,128)}), f32[16,1,2816]{2,1,0:T(1,128)S(1)}, u32[]{:S(2)}, u32[]{:S(2)}) async-start(f32[16,1,2816]{2,1,0:T(1,128)} %broadcast_in_dim.7), calls=%async_computation | async-start | bytes 360448 | tf_op jit(solution)/shard_map/all_to_all | solution.py:24
  23.1 1.7 %collective-permute-done.3 = bf16[128,1152]{1,0:T(8,128)(2,1)S(1)} collective-permute-done((bf16[128,1152]{1,0:T(8,128)(2,1)S(1)}, bf16[128,1152]{1,0:T(8,128)(2,1)S(1)}, u32[]{:S(2)}, u32[]{:S(2)}) %collective-permute-start.3) | collective-permute-done | bytes 294944 | tf_op jit(solution)/shard_map/ppermute | solution.py:109
  24.8 2.7 %collective-permute-start.4 = (bf16[256,1152]{1,0:T(8,128)(2,1)S(1)}, bf16[256,1152]{1,0:T(8,128)(2,1)S(1)}, u32[]{:S(2)}, u32[]{:S(2)}) collective-permute-start(bf16[256,1152]{1,0:T(8,128)(2,1)S(1)} %pad_maximum_fusion.8), channel_id=1, source_target_pairs={{0,16},{16,0},{1,17},{17,1},{2,18},{18,2},{3,19},{19,3},{4,20},{20... | collective-permute-start | bytes 1769480 | tf_op jit(solution)/shard_map/ppermute | solution.py:110
  27.6 4.9 %all-to-all-done = f32[16,1,2816]{2,1,0:T(1,128)S(1)} async-done(((f32[16,1,2816]{2,1,0:T(1,128)}), f32[16,1,2816]{2,1,0:T(1,128)S(1)}, u32[]{:S(2)}, u32[]{:S(2)}) %all-to-all-start) | async-done | bytes 180256 | tf_op jit(solution)/shard_map/all_to_all | solution.py:24
  32.6 3.9 %collective-permute-start.1 = (bf16[128,256]{1,0:T(8,128)(2,1)S(1)}, bf16[128,256]{1,0:T(8,128)(2,1)S(1)}, u32[]{:S(2)}, u32[]{:S(2)}) collective-permute-start(bf16[128,256]{1,0:T(8,128)(2,1)S(1)} %fusion.29), channel_id=1, source_target_pairs={{16,0},{17,1},{18,2},{19,3},{20,4},{21,5},{22,6},{23,7},{24,8},{25... | collective-permute-start | bytes 196616 | tf_op jit(solution)/shard_map/ppermute | solution.py:117
  36.5 2.6 %collective-permute-start.2 = (bf16[128,256]{1,0:T(8,128)(2,1)S(1)}, bf16[128,256]{1,0:T(8,128)(2,1)S(1)}, u32[]{:S(2)}, u32[]{:S(2)}) collective-permute-start(bf16[128,256]{1,0:T(8,128)(2,1)S(1)} %fusion.29), channel_id=1, source_target_pairs={{16,272},{17,208},{18,144},{19,80},{20,16},{21,464},{22,400},{23,3... | collective-permute-start | bytes 196616 | tf_op jit(solution)/shard_map/ppermute | solution.py:123
  39.2 4.8 %collective-permute-done.1 = bf16[128,256]{1,0:T(8,128)(2,1)S(1)} collective-permute-done((bf16[128,256]{1,0:T(8,128)(2,1)S(1)}, bf16[128,256]{1,0:T(8,128)(2,1)S(1)}, u32[]{:S(2)}, u32[]{:S(2)}) %collective-permute-start.1) | collective-permute-done | bytes 65568 | tf_op jit(solution)/shard_map/ppermute | solution.py:117
  44.0 1.7 %collective-permute-done.2 = bf16[128,256]{1,0:T(8,128)(2,1)S(1)} collective-permute-done((bf16[128,256]{1,0:T(8,128)(2,1)S(1)}, bf16[128,256]{1,0:T(8,128)(2,1)S(1)}, u32[]{:S(2)}, u32[]{:S(2)}) %collective-permute-start.2) | collective-permute-done | bytes 65568 | tf_op jit(solution)/shard_map/ppermute | solution.py:123
  45.7 0.4 fusion.4
  46.1 1.6 %broadcast_in_dim.8 = bf16[16,2,128,256]{3,2,1,0:T(8,128)(2,1)} broadcast(bf16[2,128,256]{2,1,0:T(8,128)(2,1)S(1)} %pad_maximum_fusion.10), dimensions={1,2,3} | broadcast | bytes 2228224 | tf_op jit(solution)/shard_map/broadcast_in_dim | solution.py:145
  47.7 9.6 %all-to-all-start.1 = ((bf16[16,2,128,256]{3,2,1,0:T(8,128)(2,1)}), bf16[16,2,128,256]{3,2,1,0:T(8,128)(2,1)S(1)}, u32[]{:S(2)}, u32[]{:S(2)}) async-start(bf16[16,2,128,256]{3,2,1,0:T(8,128)(2,1)} %broadcast_in_dim.8), calls=%async_computation.1 | async-start | bytes 4194304 | tf_op jit(solution)/shard_map/all_to_all | solution.py:144
  57.5 0.7 collective-permute-start.10
  58.2 2.2 %collective-permute-start.7 = (f32[32,640]{1,0:T(8,128)S(1)}, f32[32,640]{1,0:T(8,128)S(1)}, u32[]{:S(2)}, u32[]{:S(2)}) collective-permute-start(f32[32,640]{1,0:T(8,128)S(1)} %get-tuple-element.34), channel_id=1, source_target_pairs={{0,64},{1,65},{2,66},{3,67},{4,68},{5,69},{6,70},{7,71},{8,72},{9,... | collective-permute-start | bytes 245768 | tf_op jit(solution)/shard_map/ppermute | solution.py:162
  60.4 2.2 %collective-permute-start.8 = (f32[32,640]{1,0:T(8,128)S(1)}, f32[32,640]{1,0:T(8,128)S(1)}, u32[]{:S(2)}, u32[]{:S(2)}) collective-permute-start(f32[32,640]{1,0:T(8,128)S(1)} %get-tuple-element.37), channel_id=1, source_target_pairs={{0,128},{1,129},{2,130},{3,131},{4,132},{5,133},{6,134},{7,135},{8... | collective-permute-start | bytes 245768 | tf_op jit(solution)/shard_map/ppermute | solution.py:162
  62.6 5.2 %collective-permute-start.9 = (f32[32,640]{1,0:T(8,128)S(1)}, f32[32,640]{1,0:T(8,128)S(1)}, u32[]{:S(2)}, u32[]{:S(2)}) collective-permute-start(f32[32,640]{1,0:T(8,128)S(1)} %get-tuple-element.36), channel_id=1, source_target_pairs={{0,192},{1,193},{2,194},{3,195},{4,196},{5,197},{6,198},{7,199},{8... | collective-permute-start | bytes 245768 | tf_op jit(solution)/shard_map/ppermute | solution.py:162
  67.8 20.2 %all-to-all-done.1 = bf16[16,2,128,256]{3,2,1,0:T(8,128)(2,1)S(1)} async-done(((bf16[16,2,128,256]{3,2,1,0:T(8,128)(2,1)}), bf16[16,2,128,256]{3,2,1,0:T(8,128)(2,1)S(1)}, u32[]{:S(2)}, u32[]{:S(2)}) %all-to-all-start.1) | async-done | bytes 2097184 | tf_op jit(solution)/shard_map/all_to_all | solution.py:144
  88.2 1.9 %collective-permute-start.11 = (f32[2,8,640]{2,1,0:T(8,128)S(1)}, f32[2,8,640]{2,1,0:T(8,128)S(1)}, u32[]{:S(2)}, u32[]{:S(2)}) collective-permute-start(f32[2,8,640]{2,1,0:T(8,128)S(1)} %dynamic-slice_bitcast_fusion.4), channel_id=1, source_target_pairs={{0,16},{16,0},{1,17},{17,1},{2,18},{18,2},{3,19},{19,3},{4,20},{20... | collective-permute-start | bytes 122888 | tf_op jit(solution)/shard_map/ppermute | solution.py:40
  90.1 2.4 %collective-permute-start.5 = (bf16[16,128,256]{2,1,0:T(8,128)(2,1)S(1)}, bf16[16,128,256]{2,1,0:T(8,128)(2,1)S(1)}, u32[]{:S(2)}, u32[]{:S(2)}) collective-permute-start(bf16[16,128,256]{2,1,0:T(8,128)(2,1)S(1)} %broadcast_select_fusion.1), channel_id=1, source_target_pairs={{0,16},{16,0},{1,17},{17,1},{2,18},{18,2},{3,19},{19,3},{4,20},{20... | collective-permute-start | bytes 3145736 | tf_op jit(solution)/shard_map/ppermute | solution.py:166
  92.6 2.0 %collective-permute-start.6 = (bf16[16,128,256]{2,1,0:T(8,128)(2,1)S(1)}, bf16[16,128,256]{2,1,0:T(8,128)(2,1)S(1)}, u32[]{:S(2)}, u32[]{:S(2)}) collective-permute-start(bf16[16,128,256]{2,1,0:T(8,128)(2,1)S(1)} %slice_bitcast_fusion), channel_id=1, source_target_pairs={{16,0},{17,1},{18,2},{19,3},{20,4},{21,5},{22,6},{23,7},{24,8},{25... | collective-permute-start | bytes 3145736 | tf_op jit(solution)/shard_map/ppermute | solution.py:167
  94.6 3.2 %collective-permute-start.12 = (f32[8,640]{1,0:T(8,128)S(1)}, f32[8,640]{1,0:T(8,128)S(1)}, u32[]{:S(2)}, u32[]{:S(2)}) collective-permute-start(f32[8,640]{1,0:T(8,128)S(1)} %dynamic-slice_bitcast_fusion.5), channel_id=1, source_target_pairs={{0,32},{16,48},{1,33},{17,49},{2,34},{18,50},{3,35},{19,51},{4,36}... | collective-permute-start | bytes 61448 | tf_op jit(solution)/shard_map/ppermute | solution.py:175
  97.9 1.3 %collective-permute-done.12 = f32[8,640]{1,0:T(8,128)S(1)} collective-permute-done((f32[8,640]{1,0:T(8,128)S(1)}, f32[8,640]{1,0:T(8,128)S(1)}, u32[]{:S(2)}, u32[]{:S(2)}) %collective-permute-start.12) | collective-permute-done | bytes 20512 | tf_op jit(solution)/shard_map/ppermute | solution.py:175
  99.2 0.7 fusion.34
  99.9 0.5 convolution_bitcast_fusion.1
  100.4 0.5 convolution_bitcast_fusion
  100.9 0.8 copy.35
  (48 shorter events, 1.2 us)
Async XLA Ops:
  0.6 13.2 %copy-start = (s32[128,256]{1,0:T(8,128)S(1)}, s32[128,256]{1,0:T(8,128)}, u32[]{:S(2)}) copy-start(s32[128,256]{1,0:T(8,128)} %param.10) | copy-start | bytes 393220
  0.6 13.2 %copy-start.2 = (bf16[128,256]{1,0:T(8,128)(2,1)S(1)}, bf16[128,256]{1,0:T(8,128)(2,1)}, u32[]{:S(2)}) copy-start(bf16[128,256]{1,0:T(8,128)(2,1)} %param.9) | copy-start | bytes 196612
  3.8 12.4 %collective-permute-start = (f32[2816]{0:T(1024)S(1)}, f32[2816]{0:T(1024)S(1)}, u32[]{:S(2)}, u32[]{:S(2)}) collective-permute-start(f32[2816]{0:T(1024)S(1)} %pad_maximum_fusion.11), channel_id=1, source_target_pairs={{0,16},{16,0},{1,17},{17,1},{2,18},{18,2},{3,19},{19,3},{4,20},{20... | collective-permute-start | bytes 33800 | tf_op jit(solution)/shard_map/ppermute | solution.py:90
  14.1 18.5 %copy-start.1 = (s32[128,256]{1,0:T(8,128)S(1)}, s32[128,256]{1,0:T(8,128)}, u32[]{:S(2)}) copy-start(s32[128,256]{1,0:T(8,128)} %param.8) | copy-start | bytes 393220
  14.1 18.5 %copy-start.3 = (bf16[128,256]{1,0:T(8,128)(2,1)S(1)}, bf16[128,256]{1,0:T(8,128)(2,1)}, u32[]{:S(2)}) copy-start(bf16[128,256]{1,0:T(8,128)(2,1)} %param.7) | copy-start | bytes 196612
  14.1 10.7 %collective-permute-start.3 = (bf16[128,1152]{1,0:T(8,128)(2,1)S(1)}, bf16[128,1152]{1,0:T(8,128)(2,1)S(1)}, u32[]{:S(2)}, u32[]{:S(2)}) collective-permute-start(bf16[128,1152]{1,0:T(8,128)(2,1)S(1)} %pad_maximum_fusion.9), channel_id=1, source_target_pairs={{0,32},{16,48},{1,33},{17,49},{2,34},{18,50},{3,35},{19,51},{4,36}... | collective-permute-start | bytes 884744 | tf_op jit(solution)/shard_map/ppermute | solution.py:109
  17.0 15.4 %all-to-all-start = ((f32[16,1,2816]{2,1,0:T(1,128)}), f32[16,1,2816]{2,1,0:T(1,128)S(1)}, u32[]{:S(2)}, u32[]{:S(2)}) async-start(f32[16,1,2816]{2,1,0:T(1,128)} %broadcast_in_dim.7), calls=%async_computation | async-start | bytes 360448 | tf_op jit(solution)/shard_map/all_to_all | solution.py:24
  24.8 20.9 %collective-permute-start.4 = (bf16[256,1152]{1,0:T(8,128)(2,1)S(1)}, bf16[256,1152]{1,0:T(8,128)(2,1)S(1)}, u32[]{:S(2)}, u32[]{:S(2)}) collective-permute-start(bf16[256,1152]{1,0:T(8,128)(2,1)S(1)} %pad_maximum_fusion.8), channel_id=1, source_target_pairs={{0,16},{16,0},{1,17},{17,1},{2,18},{18,2},{3,19},{19,3},{4,20},{20... | collective-permute-start | bytes 1769480 | tf_op jit(solution)/shard_map/ppermute | solution.py:110
  32.6 11.4 %collective-permute-start.1 = (bf16[128,256]{1,0:T(8,128)(2,1)S(1)}, bf16[128,256]{1,0:T(8,128)(2,1)S(1)}, u32[]{:S(2)}, u32[]{:S(2)}) collective-permute-start(bf16[128,256]{1,0:T(8,128)(2,1)S(1)} %fusion.29), channel_id=1, source_target_pairs={{16,0},{17,1},{18,2},{19,3},{20,4},{21,5},{22,6},{23,7},{24,8},{25... | collective-permute-start | bytes 196616 | tf_op jit(solution)/shard_map/ppermute | solution.py:117
  36.5 9.1 %collective-permute-start.2 = (bf16[128,256]{1,0:T(8,128)(2,1)S(1)}, bf16[128,256]{1,0:T(8,128)(2,1)S(1)}, u32[]{:S(2)}, u32[]{:S(2)}) collective-permute-start(bf16[128,256]{1,0:T(8,128)(2,1)S(1)} %fusion.29), channel_id=1, source_target_pairs={{16,272},{17,208},{18,144},{19,80},{20,16},{21,464},{22,400},{23,3... | collective-permute-start | bytes 196616 | tf_op jit(solution)/shard_map/ppermute | solution.py:123
  47.7 9.6 %copy-start.4 = (f32[128,256]{1,0:T(8,128)S(1)}, f32[128,256]{1,0:T(8,128)}, u32[]{:S(2)}) copy-start(f32[128,256]{1,0:T(8,128)} %param.6) | copy-start | bytes 393220
  47.7 40.2 %all-to-all-start.1 = ((bf16[16,2,128,256]{3,2,1,0:T(8,128)(2,1)}), bf16[16,2,128,256]{3,2,1,0:T(8,128)(2,1)S(1)}, u32[]{:S(2)}, u32[]{:S(2)}) async-start(bf16[16,2,128,256]{3,2,1,0:T(8,128)(2,1)} %broadcast_in_dim.8), calls=%async_computation.1 | async-start | bytes 4194304 | tf_op jit(solution)/shard_map/all_to_all | solution.py:144
  57.5 30.6 %collective-permute-start.10 = (f32[32,640]{1,0:T(8,128)S(1)}, f32[32,640]{1,0:T(8,128)S(1)}, u32[]{:S(2)}, u32[]{:S(2)}) collective-permute-start(f32[32,640]{1,0:T(8,128)S(1)} %get-tuple-element.35), channel_id=1, source_target_pairs={{0,256},{1,257},{2,258},{3,259},{4,260},{5,261},{6,262},{7,263},{8... | collective-permute-start | bytes 245768 | tf_op jit(solution)/shard_map/ppermute | solution.py:162
  58.2 29.9 %collective-permute-start.7 = (f32[32,640]{1,0:T(8,128)S(1)}, f32[32,640]{1,0:T(8,128)S(1)}, u32[]{:S(2)}, u32[]{:S(2)}) collective-permute-start(f32[32,640]{1,0:T(8,128)S(1)} %get-tuple-element.34), channel_id=1, source_target_pairs={{0,64},{1,65},{2,66},{3,67},{4,68},{5,69},{6,70},{7,71},{8,72},{9,... | collective-permute-start | bytes 245768 | tf_op jit(solution)/shard_map/ppermute | solution.py:162
  60.4 27.7 %collective-permute-start.8 = (f32[32,640]{1,0:T(8,128)S(1)}, f32[32,640]{1,0:T(8,128)S(1)}, u32[]{:S(2)}, u32[]{:S(2)}) collective-permute-start(f32[32,640]{1,0:T(8,128)S(1)} %get-tuple-element.37), channel_id=1, source_target_pairs={{0,128},{1,129},{2,130},{3,131},{4,132},{5,133},{6,134},{7,135},{8... | collective-permute-start | bytes 245768 | tf_op jit(solution)/shard_map/ppermute | solution.py:162
  62.6 25.5 %collective-permute-start.9 = (f32[32,640]{1,0:T(8,128)S(1)}, f32[32,640]{1,0:T(8,128)S(1)}, u32[]{:S(2)}, u32[]{:S(2)}) collective-permute-start(f32[32,640]{1,0:T(8,128)S(1)} %get-tuple-element.36), channel_id=1, source_target_pairs={{0,192},{1,193},{2,194},{3,195},{4,196},{5,197},{6,198},{7,199},{8... | collective-permute-start | bytes 245768 | tf_op jit(solution)/shard_map/ppermute | solution.py:162
  88.2 6.4 %collective-permute-start.11 = (f32[2,8,640]{2,1,0:T(8,128)S(1)}, f32[2,8,640]{2,1,0:T(8,128)S(1)}, u32[]{:S(2)}, u32[]{:S(2)}) collective-permute-start(f32[2,8,640]{2,1,0:T(8,128)S(1)} %dynamic-slice_bitcast_fusion.4), channel_id=1, source_target_pairs={{0,16},{16,0},{1,17},{17,1},{2,18},{18,2},{3,19},{19,3},{4,20},{20... | collective-permute-start | bytes 122888 | tf_op jit(solution)/shard_map/ppermute | solution.py:40
  90.1 9.8 %collective-permute-start.5 = (bf16[16,128,256]{2,1,0:T(8,128)(2,1)S(1)}, bf16[16,128,256]{2,1,0:T(8,128)(2,1)S(1)}, u32[]{:S(2)}, u32[]{:S(2)}) collective-permute-start(bf16[16,128,256]{2,1,0:T(8,128)(2,1)S(1)} %broadcast_select_fusion.1), channel_id=1, source_target_pairs={{0,16},{16,0},{1,17},{17,1},{2,18},{18,2},{3,19},{19,3},{4,20},{20... | collective-permute-start | bytes 3145736 | tf_op jit(solution)/shard_map/ppermute | solution.py:166
  92.6 7.8 %collective-permute-start.6 = (bf16[16,128,256]{2,1,0:T(8,128)(2,1)S(1)}, bf16[16,128,256]{2,1,0:T(8,128)(2,1)S(1)}, u32[]{:S(2)}, u32[]{:S(2)}) collective-permute-start(bf16[16,128,256]{2,1,0:T(8,128)(2,1)S(1)} %slice_bitcast_fusion), channel_id=1, source_target_pairs={{16,0},{17,1},{18,2},{19,3},{20,4},{21,5},{22,6},{23,7},{24,8},{25... | collective-permute-start | bytes 3145736 | tf_op jit(solution)/shard_map/ppermute | solution.py:167
  94.6 4.6 %collective-permute-start.12 = (f32[8,640]{1,0:T(8,128)S(1)}, f32[8,640]{1,0:T(8,128)S(1)}, u32[]{:S(2)}, u32[]{:S(2)}) collective-permute-start(f32[8,640]{1,0:T(8,128)S(1)} %dynamic-slice_bitcast_fusion.5), channel_id=1, source_target_pairs={{0,32},{16,48},{1,33},{17,49},{2,34},{18,50},{3,35},{19,51},{4,36}... | collective-permute-start | bytes 61448 | tf_op jit(solution)/shard_map/ppermute | solution.py:175

commit v4 on v3

--- a/solution.py
+++ b/solution.py
@@ -96,6 +96,11 @@
     )
     squares = total[3 * (width + tested) :]
 
+    first = core == 0
+    weight_now = mask_now.astype(jnp.bfloat16)
+    kept_now = weight_now * dosage_now
+    pair_now = lax.ppermute(jnp.stack([kept_now, weight_now]), EVERY, swap)
+
     chip = row // CORES
     level, side = chip // 2, chip % 2
     across = [(at(k, h, c), at(k ^ 1, h, c)) for k, c in blocks for h in range(CORES)]
@@ -109,20 +114,19 @@
     held = jnp.concatenate([held, lax.ppermute(raw, EVERY, across)], 0)
     held = jnp.concatenate([held, lax.ppermute(held, EVERY, swap)], 0)
 
-    weight_now = mask_now.astype(jnp.float32)
-    scaled = (
-        weight_now * (dosage_now.astype(jnp.float32) - centre_now)
-        * lax.rsqrt(spread_now + epsilon)
-    ).astype(jnp.bfloat16)
-    crossed = lax.ppermute(
-        scaled,
-        EVERY,
-        [(at(k, 1, c), at(k, 0, c)) for k, c in blocks]
-        + [(at(c, 0, v), at(lands[c][v], 1, c)) for c, v in blocks],
+    def standardized(kept, weight):
+        offset = weight.astype(jnp.float32) * (kept.astype(jnp.float32) - centre_now)
+        return (offset * lax.rsqrt(spread_now + epsilon)).astype(jnp.bfloat16)
+
+    mine = standardized(kept_now, weight_now)
+    partner = standardized(pair_now[0], pair_now[1])
+    chip_block = jnp.stack(
+        [jnp.where(first, mine, partner), jnp.where(first, partner, mine)]
     )
     mirrored = lax.ppermute(
-        scaled, EVERY, [(at(c, 1, v), at(lands[c][v], 1, c)) for c, v in blocks]
-    )
+        chip_block, EVERY, [(at(c, 1, v), at(lands[c][v], 1, c)) for c, v in blocks]
+    )
+    chip_block = jnp.where(first, chip_block, mirrored)
     genotype = (
         held[:, share + tested :].astype(jnp.float32)
         * (held[:, share : share + tested].astype(jnp.float32) - centre_prev)
@@ -133,10 +137,6 @@
     cross = lax.dot_general(
         genotype, held[:, :share], (((0,), (0,)), ((), ())), preferred_element_type=jnp.float32
     ).reshape(layers, 2 * CORES * out_rows, share)
-    first = core == 0
-    chip_block = jnp.stack(
-        [jnp.where(first, scaled, crossed), jnp.where(first, crossed, mirrored)]
-    )
     groups = [[at(k, 0, c) for c in range(cols)] for k in range(chips)] + [
         [at(k, 1, c) for k in lands[c]] for c in range(cols)
     ]

time: 103 us -> 101 us (0.981)
  the two profiles are of different devices: /device:TPU:1 before, /device:TPU:63 now
where the time goes in v4:
time: 101 us; the launch traced here: 100 us
  starting transfers between devices  59.3 us (59%)
  waiting for transfers between devices  31.9 us (32%)
  local copies, waits for them, and re-layouts  4.93 us (5%)
  other arithmetic  1.57 us (2%)
  matrix products  1.38 us (1%)
  between operations  1.19 us (1%)
    all_to_all x1, waiting for transfers between devices, body(): lax.all_to_all(jnp.broadcast_to(chip_block[None], (cols, *chip_block.shap...  18.2 us
    all_to_all x1, starting transfers between devices, body(): lax.all_to_all(jnp.broadcast_to(chip_block[None], (cols, *chip_block.shap...  15.1 us
    all_to_all x1, starting transfers between devices, summed_over(): lax.all_to_all(sent, EVERY, 0, 0, tiled=True, axis_index_groups=groups)  11.2 us
    ppermute x4, starting transfers between devices, body(): arrivals.append(lax.ppermute(leaving, EVERY, routes))  10.2 us
    ppermute x1, waiting for transfers between devices, body(): lax.ppermute(chip_block, EVERY, [(at(c, 1, v), at(lands[c][v], 1, c)) for...  6.51 us
    ppermute x1, starting transfers between devices, body(): lax.ppermute(chip_block, EVERY, [(at(c, 1, v), at(lands[c][v], 1, c)) for...  4.41 us
    all_to_all x1, waiting for transfers between devices, summed_over(): lax.all_to_all(sent, EVERY, 0, 0, tiled=True, axis_index_groups=groups)  3.06 us
    ppermute x1, starting transfers between devices, body(): partial = partial + lax.ppermute(partial, EVERY, swap)  2.86 us
  transfers between devices with their start and end apart: 15, of which 6 were waited for; matrix products, arithmetic and copies ran while one was open for 3% of the time, Pallas kernels for 0%

profile of v4, /device:TPU:63, one launch (start us, length us, event | category | flops | bytes accessed | tf_op | source)
XLA Modules:
  0.0 100.3 jit_solution(13764288340510548856)
XLA Ops:
  0.7 1.2 %copy.30 = bf16[128,1280]{0,1:T(8,128)(2,1)S(1)} copy(bf16[128,1280]{1,0:T(8,128)(2,1)} %param.11) | data formatting | bytes 655360 | tf_op args[5]
  2.0 0.2 copy.32
  2.3 2.5 %collective-permute-start.3 = (bf16[128,1152]{1,0:T(8,128)(2,1)S(1)}, bf16[128,1152]{1,0:T(8,128)(2,1)S(1)}, u32[]{:S(2)}, u32[]{:S(2)}) collective-permute-start(bf16[128,1152]{1,0:T(8,128)(2,1)S(1)} %pad_maximum_fusion.9), channel_id=1, source_target_pairs={{0,32},{16,48},{1,33},{17,49},{2,34},{18,50},{3,35},{19,51},{4,36}... | collective-permute-start | bytes 884744 | tf_op jit(solution)/shard_map/ppermute | solution.py:114
  5.0 2.9 %collective-permute-start = (f32[2816]{0:T(1024)S(1)}, f32[2816]{0:T(1024)S(1)}, u32[]{:S(2)}, u32[]{:S(2)}) collective-permute-start(f32[2816]{0:T(1024)S(1)} %pad_maximum_fusion.12), channel_id=1, source_target_pairs={{0,16},{16,0},{1,17},{17,1},{2,18},{18,2},{3,19},{19,3},{4,20},{20... | collective-permute-start | bytes 33800 | tf_op jit(solution)/shard_map/ppermute | solution.py:90
  7.9 0.8 collective-permute-done
  8.7 0.8 broadcast_in_dim.7
  9.5 11.2 %all-to-all-start = ((f32[16,1,2816]{2,1,0:T(1,128)}), f32[16,1,2816]{2,1,0:T(1,128)S(1)}, u32[]{:S(2)}, u32[]{:S(2)}) async-start(f32[16,1,2816]{2,1,0:T(1,128)} %broadcast_in_dim.7), calls=%async_computation | async-start | bytes 360448 | tf_op jit(solution)/shard_map/all_to_all | solution.py:24
  20.7 2.8 %collective-permute-start.1 = (bf16[2,128,256]{2,1,0:T(8,128)(2,1)S(1)}, bf16[2,128,256]{2,1,0:T(8,128)(2,1)S(1)}, u32[]{:S(2)}, u32[]{:S(2)}) collective-permute-start(bf16[2,128,256]{2,1,0:T(8,128)(2,1)S(1)} %pad_maximum_fusion.10), channel_id=1, source_target_pairs={{0,16},{16,0},{1,17},{17,1},{2,18},{18,2},{3,19},{19,3},{4,20},{20... | collective-permute-start | bytes 393224 | tf_op jit(solution)/shard_map/ppermute | solution.py:102
  23.6 0.2 copy.31
  23.8 1.9 %collective-permute-start.4 = (bf16[256,1152]{1,0:T(8,128)(2,1)S(1)}, bf16[256,1152]{1,0:T(8,128)(2,1)S(1)}, u32[]{:S(2)}, u32[]{:S(2)}) collective-permute-start(bf16[256,1152]{1,0:T(8,128)(2,1)S(1)} %pad_maximum_fusion.8), channel_id=1, source_target_pairs={{0,16},{16,0},{1,17},{17,1},{2,18},{18,2},{3,19},{19,3},{4,20},{20... | collective-permute-start | bytes 1769480 | tf_op jit(solution)/shard_map/ppermute | solution.py:115
  25.7 3.1 %all-to-all-done = f32[16,1,2816]{2,1,0:T(1,128)S(1)} async-done(((f32[16,1,2816]{2,1,0:T(1,128)}), f32[16,1,2816]{2,1,0:T(1,128)S(1)}, u32[]{:S(2)}, u32[]{:S(2)}) %all-to-all-start) | async-done | bytes 180256 | tf_op jit(solution)/shard_map/all_to_all | solution.py:24
  28.8 0.1 reduce_sum.79
  29.0 4.4 %collective-permute-start.2 = (bf16[2,128,256]{2,1,0:T(8,128)(2,1)S(1)}, bf16[2,128,256]{2,1,0:T(8,128)(2,1)S(1)}, u32[]{:S(2)}, u32[]{:S(2)}) collective-permute-start(bf16[2,128,256]{2,1,0:T(8,128)(2,1)S(1)} %pad_maximum_fusion.11), channel_id=1, source_target_pairs={{16,272},{17,208},{18,144},{19,80},{20,16},{21,464},{22,400},{23,3... | collective-permute-start | bytes 393224 | tf_op jit(solution)/shard_map/ppermute | solution.py:126
  33.4 6.5 %collective-permute-done.2 = bf16[2,128,256]{2,1,0:T(8,128)(2,1)S(1)} collective-permute-done((bf16[2,128,256]{2,1,0:T(8,128)(2,1)S(1)}, bf16[2,128,256]{2,1,0:T(8,128)(2,1)S(1)}, u32[]{:S(2)}, u32[]{:S(2)}) %collective-permute-start.2) | collective-permute-done | bytes 131104 | tf_op jit(solution)/shard_map/ppermute | solution.py:126
  40.0 0.4 fusion.4
  40.4 1.6 %broadcast_in_dim.8 = bf16[16,2,128,256]{3,2,1,0:T(8,128)(2,1)} broadcast(bf16[2,128,256]{2,1,0:T(8,128)(2,1)S(1)} %broadcast_select_fusion.4), dimensions={1,2,3} | broadcast | bytes 2228224 | tf_op jit(solution)/shard_map/broadcast_in_dim | solution.py:145
  42.0 15.1 %all-to-all-start.1 = ((bf16[16,2,128,256]{3,2,1,0:T(8,128)(2,1)}), bf16[16,2,128,256]{3,2,1,0:T(8,128)(2,1)S(1)}, u32[]{:S(2)}, u32[]{:S(2)}) async-start(bf16[16,2,128,256]{3,2,1,0:T(8,128)(2,1)} %broadcast_in_dim.8), calls=%async_computation.1 | async-start | bytes 4194304 | tf_op jit(solution)/shard_map/all_to_all | solution.py:144
  57.3 0.7 collective-permute-start.10
  58.0 4.3 %collective-permute-start.7 = (f32[32,640]{1,0:T(8,128)S(1)}, f32[32,640]{1,0:T(8,128)S(1)}, u32[]{:S(2)}, u32[]{:S(2)}) collective-permute-start(f32[32,640]{1,0:T(8,128)S(1)} %get-tuple-element.36), channel_id=1, source_target_pairs={{0,64},{1,65},{2,66},{3,67},{4,68},{5,69},{6,70},{7,71},{8,72},{9,... | collective-permute-start | bytes 245768 | tf_op jit(solution)/shard_map/ppermute | solution.py:162
  62.3 3.1 %collective-permute-start.8 = (f32[32,640]{1,0:T(8,128)S(1)}, f32[32,640]{1,0:T(8,128)S(1)}, u32[]{:S(2)}, u32[]{:S(2)}) collective-permute-start(f32[32,640]{1,0:T(8,128)S(1)} %get-tuple-element.39), channel_id=1, source_target_pairs={{0,128},{1,129},{2,130},{3,131},{4,132},{5,133},{6,134},{7,135},{8... | collective-permute-start | bytes 245768 | tf_op jit(solution)/shard_map/ppermute | solution.py:162
  65.4 2.2 %collective-permute-start.9 = (f32[32,640]{1,0:T(8,128)S(1)}, f32[32,640]{1,0:T(8,128)S(1)}, u32[]{:S(2)}, u32[]{:S(2)}) collective-permute-start(f32[32,640]{1,0:T(8,128)S(1)} %get-tuple-element.38), channel_id=1, source_target_pairs={{0,192},{1,193},{2,194},{3,195},{4,196},{5,197},{6,198},{7,199},{8... | collective-permute-start | bytes 245768 | tf_op jit(solution)/shard_map/ppermute | solution.py:162
  67.6 18.2 %all-to-all-done.1 = bf16[16,2,128,256]{3,2,1,0:T(8,128)(2,1)S(1)} async-done(((bf16[16,2,128,256]{3,2,1,0:T(8,128)(2,1)}), bf16[16,2,128,256]{3,2,1,0:T(8,128)(2,1)S(1)}, u32[]{:S(2)}, u32[]{:S(2)}) %all-to-all-start.1) | async-done | bytes 2097184 | tf_op jit(solution)/shard_map/all_to_all | solution.py:144
  85.9 0.7 collective-permute-done.9
  86.7 1.9 %collective-permute-start.11 = (f32[2,8,640]{2,1,0:T(8,128)S(1)}, f32[2,8,640]{2,1,0:T(8,128)S(1)}, u32[]{:S(2)}, u32[]{:S(2)}) collective-permute-start(f32[2,8,640]{2,1,0:T(8,128)S(1)} %dynamic-slice_bitcast_fusion.4), channel_id=1, source_target_pairs={{0,16},{16,0},{1,17},{17,1},{2,18},{18,2},{3,19},{19,3},{4,20},{20... | collective-permute-start | bytes 122888 | tf_op jit(solution)/shard_map/ppermute | solution.py:40
  88.6 2.4 %collective-permute-start.5 = (bf16[16,128,256]{2,1,0:T(8,128)(2,1)S(1)}, bf16[16,128,256]{2,1,0:T(8,128)(2,1)S(1)}, u32[]{:S(2)}, u32[]{:S(2)}) collective-permute-start(bf16[16,128,256]{2,1,0:T(8,128)(2,1)S(1)} %broadcast_select_fusion.1), channel_id=1, source_target_pairs={{0,16},{16,0},{1,17},{17,1},{2,18},{18,2},{3,19},{19,3},{4,20},{20... | collective-permute-start | bytes 3145736 | tf_op jit(solution)/shard_map/ppermute | solution.py:166
  91.1 2.0 %collective-permute-start.6 = (bf16[16,128,256]{2,1,0:T(8,128)(2,1)S(1)}, bf16[16,128,256]{2,1,0:T(8,128)(2,1)S(1)}, u32[]{:S(2)}, u32[]{:S(2)}) collective-permute-start(bf16[16,128,256]{2,1,0:T(8,128)(2,1)S(1)} %slice_bitcast_fusion), channel_id=1, source_target_pairs={{16,0},{17,1},{18,2},{19,3},{20,4},{21,5},{22,6},{23,7},{24,8},{25... | collective-permute-start | bytes 3145736 | tf_op jit(solution)/shard_map/ppermute | solution.py:167
  93.2 1.9 %collective-permute-start.12 = (f32[8,640]{1,0:T(8,128)S(1)}, f32[8,640]{1,0:T(8,128)S(1)}, u32[]{:S(2)}, u32[]{:S(2)}) collective-permute-start(f32[8,640]{1,0:T(8,128)S(1)} %dynamic-slice_bitcast_fusion.5), channel_id=1, source_target_pairs={{0,32},{16,48},{1,33},{17,49},{2,34},{18,50},{3,35},{19,51},{4,36}... | collective-permute-start | bytes 61448 | tf_op jit(solution)/shard_map/ppermute | solution.py:175
  95.2 2.6 %collective-permute-done.12 = f32[8,640]{1,0:T(8,128)S(1)} collective-permute-done((f32[8,640]{1,0:T(8,128)S(1)}, f32[8,640]{1,0:T(8,128)S(1)}, u32[]{:S(2)}, u32[]{:S(2)}) %collective-permute-start.12) | collective-permute-done | bytes 20512 | tf_op jit(solution)/shard_map/ppermute | solution.py:175
  97.8 0.7 fusion.34
  98.5 0.5 convolution_bitcast_fusion.1
  99.0 0.5 convolution_bitcast_fusion
  99.5 0.8 copy.35
  (52 shorter events, 1.0 us)
Async XLA Ops:
  0.6 1.6 %copy-start.2 = (s32[128,256]{1,0:T(8,128)S(1)}, s32[128,256]{1,0:T(8,128)}, u32[]{:S(2)}) copy-start(s32[128,256]{1,0:T(8,128)} %param.10) | copy-start | bytes 393220
  0.6 1.6 %copy-start.4 = (bf16[128,256]{1,0:T(8,128)(2,1)S(1)}, bf16[128,256]{1,0:T(8,128)(2,1)}, u32[]{:S(2)}) copy-start(bf16[128,256]{1,0:T(8,128)(2,1)} %param.9) | copy-start | bytes 196612
  0.7 4.1 %copy-start = (bf16[128,1280]{1,0:T(8,128)(2,1)S(1)}, bf16[128,1280]{1,0:T(8,128)(2,1)}, u32[]{:S(2)}) copy-start(bf16[128,1280]{1,0:T(8,128)(2,1)} %param.11) | copy-start | bytes 983044
  1.9 2.9 %copy-start.1 = (bf16[128,256]{1,0:T(8,128)(2,1)S(1)}, bf16[128,256]{1,0:T(8,128)(2,1)}, u32[]{:S(2)}) copy-start(bf16[128,256]{1,0:T(8,128)(2,1)} %param.7) | copy-start | bytes 196612
  2.0 2.9 %copy-start.3 = (s32[128,256]{1,0:T(8,128)S(1)}, s32[128,256]{1,0:T(8,128)}, u32[]{:S(2)}) copy-start(s32[128,256]{1,0:T(8,128)} %param.8) | copy-start | bytes 393220
  2.3 21.5 %collective-permute-start.3 = (bf16[128,1152]{1,0:T(8,128)(2,1)S(1)}, bf16[128,1152]{1,0:T(8,128)(2,1)S(1)}, u32[]{:S(2)}, u32[]{:S(2)}) collective-permute-start(bf16[128,1152]{1,0:T(8,128)(2,1)S(1)} %pad_maximum_fusion.9), channel_id=1, source_target_pairs={{0,32},{16,48},{1,33},{17,49},{2,34},{18,50},{3,35},{19,51},{4,36}... | collective-permute-start | bytes 884744 | tf_op jit(solution)/shard_map/ppermute | solution.py:114
  5.0 3.7 %collective-permute-start = (f32[2816]{0:T(1024)S(1)}, f32[2816]{0:T(1024)S(1)}, u32[]{:S(2)}, u32[]{:S(2)}) collective-permute-start(f32[2816]{0:T(1024)S(1)} %pad_maximum_fusion.12), channel_id=1, source_target_pairs={{0,16},{16,0},{1,17},{17,1},{2,18},{18,2},{3,19},{19,3},{4,20},{20... | collective-permute-start | bytes 33800 | tf_op jit(solution)/shard_map/ppermute | solution.py:90
  9.5 19.3 %all-to-all-start = ((f32[16,1,2816]{2,1,0:T(1,128)}), f32[16,1,2816]{2,1,0:T(1,128)S(1)}, u32[]{:S(2)}, u32[]{:S(2)}) async-start(f32[16,1,2816]{2,1,0:T(1,128)} %broadcast_in_dim.7), calls=%async_computation | async-start | bytes 360448 | tf_op jit(solution)/shard_map/all_to_all | solution.py:24
  20.7 8.2 %collective-permute-start.1 = (bf16[2,128,256]{2,1,0:T(8,128)(2,1)S(1)}, bf16[2,128,256]{2,1,0:T(8,128)(2,1)S(1)}, u32[]{:S(2)}, u32[]{:S(2)}) collective-permute-start(bf16[2,128,256]{2,1,0:T(8,128)(2,1)S(1)} %pad_maximum_fusion.10), channel_id=1, source_target_pairs={{0,16},{16,0},{1,17},{17,1},{2,18},{18,2},{3,19},{19,3},{4,20},{20... | collective-permute-start | bytes 393224 | tf_op jit(solution)/shard_map/ppermute | solution.py:102
  23.8 16.2 %collective-permute-start.4 = (bf16[256,1152]{1,0:T(8,128)(2,1)S(1)}, bf16[256,1152]{1,0:T(8,128)(2,1)S(1)}, u32[]{:S(2)}, u32[]{:S(2)}) collective-permute-start(bf16[256,1152]{1,0:T(8,128)(2,1)S(1)} %pad_maximum_fusion.8), channel_id=1, source_target_pairs={{0,16},{16,0},{1,17},{17,1},{2,18},{18,2},{3,19},{19,3},{4,20},{20... | collective-permute-start | bytes 1769480 | tf_op jit(solution)/shard_map/ppermute | solution.py:115
  29.0 10.9 %collective-permute-start.2 = (bf16[2,128,256]{2,1,0:T(8,128)(2,1)S(1)}, bf16[2,128,256]{2,1,0:T(8,128)(2,1)S(1)}, u32[]{:S(2)}, u32[]{:S(2)}) collective-permute-start(bf16[2,128,256]{2,1,0:T(8,128)(2,1)S(1)} %pad_maximum_fusion.11), channel_id=1, source_target_pairs={{16,272},{17,208},{18,144},{19,80},{20,16},{21,464},{22,400},{23,3... | collective-permute-start | bytes 393224 | tf_op jit(solution)/shard_map/ppermute | solution.py:126
  42.0 15.1 %copy-start.5 = (f32[128,256]{1,0:T(8,128)S(1)}, f32[128,256]{1,0:T(8,128)}, u32[]{:S(2)}) copy-start(f32[128,256]{1,0:T(8,128)} %param.6) | copy-start | bytes 393220
  42.0 43.8 %all-to-all-start.1 = ((bf16[16,2,128,256]{3,2,1,0:T(8,128)(2,1)}), bf16[16,2,128,256]{3,2,1,0:T(8,128)(2,1)S(1)}, u32[]{:S(2)}, u32[]{:S(2)}) async-start(bf16[16,2,128,256]{3,2,1,0:T(8,128)(2,1)} %broadcast_in_dim.8), calls=%async_computation.1 | async-start | bytes 4194304 | tf_op jit(solution)/shard_map/all_to_all | solution.py:144
  57.3 28.6 %collective-permute-start.10 = (f32[32,640]{1,0:T(8,128)S(1)}, f32[32,640]{1,0:T(8,128)S(1)}, u32[]{:S(2)}, u32[]{:S(2)}) collective-permute-start(f32[32,640]{1,0:T(8,128)S(1)} %get-tuple-element.37), channel_id=1, source_target_pairs={{0,256},{1,257},{2,258},{3,259},{4,260},{5,261},{6,262},{7,263},{8... | collective-permute-start | bytes 245768 | tf_op jit(solution)/shard_map/ppermute | solution.py:162
  58.0 27.9 %collective-permute-start.7 = (f32[32,640]{1,0:T(8,128)S(1)}, f32[32,640]{1,0:T(8,128)S(1)}, u32[]{:S(2)}, u32[]{:S(2)}) collective-permute-start(f32[32,640]{1,0:T(8,128)S(1)} %get-tuple-element.36), channel_id=1, source_target_pairs={{0,64},{1,65},{2,66},{3,67},{4,68},{5,69},{6,70},{7,71},{8,72},{9,... | collective-permute-start | bytes 245768 | tf_op jit(solution)/shard_map/ppermute | solution.py:162
  62.3 23.6 %collective-permute-start.8 = (f32[32,640]{1,0:T(8,128)S(1)}, f32[32,640]{1,0:T(8,128)S(1)}, u32[]{:S(2)}, u32[]{:S(2)}) collective-permute-start(f32[32,640]{1,0:T(8,128)S(1)} %get-tuple-element.39), channel_id=1, source_target_pairs={{0,128},{1,129},{2,130},{3,131},{4,132},{5,133},{6,134},{7,135},{8... | collective-permute-start | bytes 245768 | tf_op jit(solution)/shard_map/ppermute | solution.py:162
  65.4 21.2 %collective-permute-start.9 = (f32[32,640]{1,0:T(8,128)S(1)}, f32[32,640]{1,0:T(8,128)S(1)}, u32[]{:S(2)}, u32[]{:S(2)}) collective-permute-start(f32[32,640]{1,0:T(8,128)S(1)} %get-tuple-element.38), channel_id=1, source_target_pairs={{0,192},{1,193},{2,194},{3,195},{4,196},{5,197},{6,198},{7,199},{8... | collective-permute-start | bytes 245768 | tf_op jit(solution)/shard_map/ppermute | solution.py:162
  86.7 6.4 %collective-permute-start.11 = (f32[2,8,640]{2,1,0:T(8,128)S(1)}, f32[2,8,640]{2,1,0:T(8,128)S(1)}, u32[]{:S(2)}, u32[]{:S(2)}) collective-permute-start(f32[2,8,640]{2,1,0:T(8,128)S(1)} %dynamic-slice_bitcast_fusion.4), channel_id=1, source_target_pairs={{0,16},{16,0},{1,17},{17,1},{2,18},{18,2},{3,19},{19,3},{4,20},{20... | collective-permute-start | bytes 122888 | tf_op jit(solution)/shard_map/ppermute | solution.py:40
  88.6 9.8 %collective-permute-start.5 = (bf16[16,128,256]{2,1,0:T(8,128)(2,1)S(1)}, bf16[16,128,256]{2,1,0:T(8,128)(2,1)S(1)}, u32[]{:S(2)}, u32[]{:S(2)}) collective-permute-start(bf16[16,128,256]{2,1,0:T(8,128)(2,1)S(1)} %broadcast_select_fusion.1), channel_id=1, source_target_pairs={{0,16},{16,0},{1,17},{17,1},{2,18},{18,2},{3,19},{19,3},{4,20},{20... | collective-permute-start | bytes 3145736 | tf_op jit(solution)/shard_map/ppermute | solution.py:166
  91.1 7.9 %collective-permute-start.6 = (bf16[16,128,256]{2,1,0:T(8,128)(2,1)S(1)}, bf16[16,128,256]{2,1,0:T(8,128)(2,1)S(1)}, u32[]{:S(2)}, u32[]{:S(2)}) collective-permute-start(bf16[16,128,256]{2,1,0:T(8,128)(2,1)S(1)} %slice_bitcast_fusion), channel_id=1, source_target_pairs={{16,0},{17,1},{18,2},{19,3},{20,4},{21,5},{22,6},{23,7},{24,8},{25... | collective-permute-start | bytes 3145736 | tf_op jit(solution)/shard_map/ppermute | solution.py:167
  93.2 4.6 %collective-permute-start.12 = (f32[8,640]{1,0:T(8,128)S(1)}, f32[8,640]{1,0:T(8,128)S(1)}, u32[]{:S(2)}, u32[]{:S(2)}) collective-permute-start(f32[8,640]{1,0:T(8,128)S(1)} %dynamic-slice_bitcast_fusion.5), channel_id=1, source_target_pairs={{0,32},{16,48},{1,33},{17,49},{2,34},{18,50},{3,35},{19,51},{4,36}... | collective-permute-start | bytes 61448 | tf_op jit(solution)/shard_map/ppermute | solution.py:175

commit v5 on v4

--- a/solution.py
+++ b/solution.py
@@ -169,14 +169,13 @@
     total_rows = kept
     for arrived in arrivals:
         total_rows = total_rows + arrived
-    shares = folded(
-        jnp.moveaxis(total_rows.reshape(2, CORES, out_rows, share), 1, 0), core, swap
-    )
+    shares = total_rows.reshape(2, CORES, out_rows, share)
     own, other_half = half_of(shares, side), lax.ppermute(half_of(shares, 1 - side), EVERY, across)
     left_chip = side == 0
-    cross = jnp.concatenate(
-        [jnp.where(left_chip, own, other_half), jnp.where(left_chip, other_half, own)], 1
-    )
+    shares = jnp.concatenate(
+        [jnp.where(left_chip, own, other_half), jnp.where(left_chip, other_half, own)], 2
+    )
+    cross = folded(shares, core, swap)
     spread_rows = lax.dynamic_slice_in_dim(spread_prev, row * out_rows, out_rows, 0)
     power = squares / samples_all
     assoc_score = (

time: 101 us -> 100 us (0.990)
  the two profiles are of different devices: /device:TPU:63 before, /device:TPU:61 now
where the time goes in v5:
time: 100 us; the launch traced here: 99.7 us
  starting transfers between devices  55.5 us (56%)
  waiting for transfers between devices  35 us (35%)
  local copies, waits for them, and re-layouts  4.92 us (5%)
  other arithmetic  1.58 us (2%)
  matrix products  1.38 us (1%)
  between operations  1.21 us (1%)
    all_to_all x1, waiting for transfers between devices, body(): lax.all_to_all(jnp.broadcast_to(chip_block[None], (cols, *chip_block.shap...  18.1 us
    all_to_all x1, starting transfers between devices, body(): lax.all_to_all(jnp.broadcast_to(chip_block[None], (cols, *chip_block.shap...  12.9 us
    all_to_all x1, starting transfers between devices, summed_over(): lax.all_to_all(sent, EVERY, 0, 0, tiled=True, axis_index_groups=groups)  10.4 us
    ppermute x4, starting transfers between devices, body(): arrivals.append(lax.ppermute(leaving, EVERY, routes))  10.4 us
    ppermute x1, waiting for transfers between devices, body(): lax.ppermute(chip_block, EVERY, [(at(c, 1, v), at(lands[c][v], 1, c)) for...  10.1 us
    all_to_all x1, waiting for transfers between devices, summed_over(): lax.all_to_all(sent, EVERY, 0, 0, tiled=True, axis_index_groups=groups)  4.63 us
    ppermute x1, starting transfers between devices, body(): lax.ppermute(half_of(shares, 1 - side), EVERY, across)  3.54 us
    ppermute x1, starting transfers between devices, body(): partial = partial + lax.ppermute(partial, EVERY, swap)  2.86 us
  transfers between devices with their start and end apart: 15, of which 6 were waited for; matrix products, arithmetic and copies ran while one was open for 3% of the time, Pallas kernels for 0%

profile of v5, /device:TPU:61, one launch (start us, length us, event | category | flops | bytes accessed | tf_op | source)
XLA Modules:
  0.0 99.7 jit_solution(12090587991808304)
XLA Ops:
  0.7 1.2 %copy.30 = bf16[128,1280]{0,1:T(8,128)(2,1)S(1)} copy(bf16[128,1280]{1,0:T(8,128)(2,1)} %param.11) | data formatting | bytes 655360 | tf_op args[5]
  2.0 0.2 copy.32
  2.3 2.8 %collective-permute-start.3 = (bf16[128,1152]{1,0:T(8,128)(2,1)S(1)}, bf16[128,1152]{1,0:T(8,128)(2,1)S(1)}, u32[]{:S(2)}, u32[]{:S(2)}) collective-permute-start(bf16[128,1152]{1,0:T(8,128)(2,1)S(1)} %pad_maximum_fusion.9), channel_id=1, source_target_pairs={{0,32},{16,48},{1,33},{17,49},{2,34},{18,50},{3,35},{19,51},{4,36}... | collective-permute-start | bytes 884744 | tf_op jit(solution)/shard_map/ppermute | solution.py:114
  5.4 2.9 %collective-permute-start = (f32[2816]{0:T(1024)S(1)}, f32[2816]{0:T(1024)S(1)}, u32[]{:S(2)}, u32[]{:S(2)}) collective-permute-start(f32[2816]{0:T(1024)S(1)} %pad_maximum_fusion.12), channel_id=1, source_target_pairs={{0,16},{16,0},{1,17},{17,1},{2,18},{18,2},{3,19},{19,3},{4,20},{20... | collective-permute-start | bytes 33800 | tf_op jit(solution)/shard_map/ppermute | solution.py:90
  8.3 0.8 collective-permute-done
  9.1 0.8 broadcast_in_dim.7
  9.8 10.4 %all-to-all-start = ((f32[16,1,2816]{2,1,0:T(1,128)}), f32[16,1,2816]{2,1,0:T(1,128)S(1)}, u32[]{:S(2)}, u32[]{:S(2)}) async-start(f32[16,1,2816]{2,1,0:T(1,128)} %broadcast_in_dim.7), calls=%async_computation | async-start | bytes 360448 | tf_op jit(solution)/shard_map/all_to_all | solution.py:24
  20.3 2.5 %collective-permute-start.1 = (bf16[2,128,256]{2,1,0:T(8,128)(2,1)S(1)}, bf16[2,128,256]{2,1,0:T(8,128)(2,1)S(1)}, u32[]{:S(2)}, u32[]{:S(2)}) collective-permute-start(bf16[2,128,256]{2,1,0:T(8,128)(2,1)S(1)} %pad_maximum_fusion.10), channel_id=1, source_target_pairs={{0,16},{16,0},{1,17},{17,1},{2,18},{18,2},{3,19},{19,3},{4,20},{20... | collective-permute-start | bytes 393224 | tf_op jit(solution)/shard_map/ppermute | solution.py:102
  22.8 0.2 copy.31
  23.1 1.9 %collective-permute-start.4 = (bf16[256,1152]{1,0:T(8,128)(2,1)S(1)}, bf16[256,1152]{1,0:T(8,128)(2,1)S(1)}, u32[]{:S(2)}, u32[]{:S(2)}) collective-permute-start(bf16[256,1152]{1,0:T(8,128)(2,1)S(1)} %pad_maximum_fusion.8), channel_id=1, source_target_pairs={{0,16},{16,0},{1,17},{17,1},{2,18},{18,2},{3,19},{19,3},{4,20},{20... | collective-permute-start | bytes 1769480 | tf_op jit(solution)/shard_map/ppermute | solution.py:115
  25.0 4.6 %all-to-all-done = f32[16,1,2816]{2,1,0:T(1,128)S(1)} async-done(((f32[16,1,2816]{2,1,0:T(1,128)}), f32[16,1,2816]{2,1,0:T(1,128)S(1)}, u32[]{:S(2)}, u32[]{:S(2)}) %all-to-all-start) | async-done | bytes 180256 | tf_op jit(solution)/shard_map/all_to_all | solution.py:24
  29.6 0.1 reduce_sum.79
  29.9 1.9 %collective-permute-start.2 = (bf16[2,128,256]{2,1,0:T(8,128)(2,1)S(1)}, bf16[2,128,256]{2,1,0:T(8,128)(2,1)S(1)}, u32[]{:S(2)}, u32[]{:S(2)}) collective-permute-start(bf16[2,128,256]{2,1,0:T(8,128)(2,1)S(1)} %pad_maximum_fusion.11), channel_id=1, source_target_pairs={{16,272},{17,208},{18,144},{19,80},{20,16},{21,464},{22,400},{23,3... | collective-permute-start | bytes 393224 | tf_op jit(solution)/shard_map/ppermute | solution.py:126
  31.8 10.1 %collective-permute-done.2 = bf16[2,128,256]{2,1,0:T(8,128)(2,1)S(1)} collective-permute-done((bf16[2,128,256]{2,1,0:T(8,128)(2,1)S(1)}, bf16[2,128,256]{2,1,0:T(8,128)(2,1)S(1)}, u32[]{:S(2)}, u32[]{:S(2)}) %collective-permute-start.2) | collective-permute-done | bytes 131104 | tf_op jit(solution)/shard_map/ppermute | solution.py:126
  42.0 0.4 fusion.4
  42.4 1.6 %broadcast_in_dim.8 = bf16[16,2,128,256]{3,2,1,0:T(8,128)(2,1)} broadcast(bf16[2,128,256]{2,1,0:T(8,128)(2,1)S(1)} %broadcast_select_fusion.4), dimensions={1,2,3} | broadcast | bytes 2228224 | tf_op jit(solution)/shard_map/broadcast_in_dim | solution.py:145
  43.9 12.9 %all-to-all-start.1 = ((bf16[16,2,128,256]{3,2,1,0:T(8,128)(2,1)}), bf16[16,2,128,256]{3,2,1,0:T(8,128)(2,1)S(1)}, u32[]{:S(2)}, u32[]{:S(2)}) async-start(bf16[16,2,128,256]{3,2,1,0:T(8,128)(2,1)} %broadcast_in_dim.8), calls=%async_computation.1 | async-start | bytes 4194304 | tf_op jit(solution)/shard_map/all_to_all | solution.py:144
  57.0 0.7 collective-permute-start.10
  57.7 4.3 %collective-permute-start.7 = (f32[32,640]{1,0:T(8,128)S(1)}, f32[32,640]{1,0:T(8,128)S(1)}, u32[]{:S(2)}, u32[]{:S(2)}) collective-permute-start(f32[32,640]{1,0:T(8,128)S(1)} %get-tuple-element.36), channel_id=1, source_target_pairs={{0,64},{1,65},{2,66},{3,67},{4,68},{5,69},{6,70},{7,71},{8,72},{9,... | collective-permute-start | bytes 245768 | tf_op jit(solution)/shard_map/ppermute | solution.py:162
  62.0 3.1 %collective-permute-start.8 = (f32[32,640]{1,0:T(8,128)S(1)}, f32[32,640]{1,0:T(8,128)S(1)}, u32[]{:S(2)}, u32[]{:S(2)}) collective-permute-start(f32[32,640]{1,0:T(8,128)S(1)} %get-tuple-element.39), channel_id=1, source_target_pairs={{0,128},{1,129},{2,130},{3,131},{4,132},{5,133},{6,134},{7,135},{8... | collective-permute-start | bytes 245768 | tf_op jit(solution)/shard_map/ppermute | solution.py:162
  65.1 2.3 %collective-permute-start.9 = (f32[32,640]{1,0:T(8,128)S(1)}, f32[32,640]{1,0:T(8,128)S(1)}, u32[]{:S(2)}, u32[]{:S(2)}) collective-permute-start(f32[32,640]{1,0:T(8,128)S(1)} %get-tuple-element.38), channel_id=1, source_target_pairs={{0,192},{1,193},{2,194},{3,195},{4,196},{5,197},{6,198},{7,199},{8... | collective-permute-start | bytes 245768 | tf_op jit(solution)/shard_map/ppermute | solution.py:162
  67.4 18.1 %all-to-all-done.1 = bf16[16,2,128,256]{3,2,1,0:T(8,128)(2,1)S(1)} async-done(((bf16[16,2,128,256]{3,2,1,0:T(8,128)(2,1)}), bf16[16,2,128,256]{3,2,1,0:T(8,128)(2,1)S(1)}, u32[]{:S(2)}, u32[]{:S(2)}) %all-to-all-start.1) | async-done | bytes 2097184 | tf_op jit(solution)/shard_map/all_to_all | solution.py:144
  85.6 0.3 collective-permute-done.9
  86.0 3.5 %collective-permute-start.11 = (f32[2,8,640]{2,1,0:T(8,128)S(1)}, f32[2,8,640]{2,1,0:T(8,128)S(1)}, u32[]{:S(2)}, u32[]{:S(2)}) collective-permute-start(f32[2,8,640]{2,1,0:T(8,128)S(1)} %dynamic-slice_bitcast_fusion.4), channel_id=1, source_target_pairs={{0,32},{16,48},{1,33},{17,49},{2,34},{18,50},{3,35},{19,51},{4,36}... | collective-permute-start | bytes 122888 | tf_op jit(solution)/shard_map/ppermute | solution.py:173
  89.5 1.9 %collective-permute-start.5 = (bf16[16,128,256]{2,1,0:T(8,128)(2,1)S(1)}, bf16[16,128,256]{2,1,0:T(8,128)(2,1)S(1)}, u32[]{:S(2)}, u32[]{:S(2)}) collective-permute-start(bf16[16,128,256]{2,1,0:T(8,128)(2,1)S(1)} %broadcast_select_fusion.1), channel_id=1, source_target_pairs={{0,16},{16,0},{1,17},{17,1},{2,18},{18,2},{3,19},{19,3},{4,20},{20... | collective-permute-start | bytes 3145736 | tf_op jit(solution)/shard_map/ppermute | solution.py:166
  91.5 2.5 %collective-permute-start.6 = (bf16[16,128,256]{2,1,0:T(8,128)(2,1)S(1)}, bf16[16,128,256]{2,1,0:T(8,128)(2,1)S(1)}, u32[]{:S(2)}, u32[]{:S(2)}) collective-permute-start(bf16[16,128,256]{2,1,0:T(8,128)(2,1)S(1)} %slice_bitcast_fusion), channel_id=1, source_target_pairs={{16,0},{17,1},{18,2},{19,3},{20,4},{21,5},{22,6},{23,7},{24,8},{25... | collective-permute-start | bytes 3145736 | tf_op jit(solution)/shard_map/ppermute | solution.py:167
  94.1 1.9 %collective-permute-start.12 = (f32[8,1280]{1,0:T(8,128)S(1)}, f32[8,1280]{1,0:T(8,128)S(1)}, u32[]{:S(2)}, u32[]{:S(2)}) collective-permute-start(f32[8,1280]{1,0:T(8,128)S(1)} %fusion.34), channel_id=1, source_target_pairs={{0,16},{16,0},{1,17},{17,1},{2,18},{18,2},{3,19},{19,3},{4,20},{20... | collective-permute-start | bytes 122888 | tf_op jit(solution)/shard_map/ppermute | solution.py:40
  96.1 1.1 %collective-permute-done.12 = f32[8,1280]{1,0:T(8,128)S(1)} collective-permute-done((f32[8,1280]{1,0:T(8,128)S(1)}, f32[8,1280]{1,0:T(8,128)S(1)}, u32[]{:S(2)}, u32[]{:S(2)}) %collective-permute-start.12) | collective-permute-done | bytes 40992 | tf_op jit(solution)/shard_map/ppermute | solution.py:40
  97.2 0.7 fusion.40
  97.9 0.5 convolution_bitcast_fusion.1
  98.4 0.5 convolution_bitcast_fusion
  98.9 0.8 copy.35
  (51 shorter events, 1.0 us)
Async XLA Ops:
  0.6 1.6 %copy-start.2 = (s32[128,256]{1,0:T(8,128)S(1)}, s32[128,256]{1,0:T(8,128)}, u32[]{:S(2)}) copy-start(s32[128,256]{1,0:T(8,128)} %param.10) | copy-start | bytes 393220
  0.6 1.6 %copy-start.4 = (bf16[128,256]{1,0:T(8,128)(2,1)S(1)}, bf16[128,256]{1,0:T(8,128)(2,1)}, u32[]{:S(2)}) copy-start(bf16[128,256]{1,0:T(8,128)(2,1)} %param.9) | copy-start | bytes 196612
  0.7 4.5 %copy-start = (bf16[128,1280]{1,0:T(8,128)(2,1)S(1)}, bf16[128,1280]{1,0:T(8,128)(2,1)}, u32[]{:S(2)}) copy-start(bf16[128,1280]{1,0:T(8,128)(2,1)} %param.11) | copy-start | bytes 983044
  1.9 3.3 %copy-start.1 = (bf16[128,256]{1,0:T(8,128)(2,1)S(1)}, bf16[128,256]{1,0:T(8,128)(2,1)}, u32[]{:S(2)}) copy-start(bf16[128,256]{1,0:T(8,128)(2,1)} %param.7) | copy-start | bytes 196612
  2.0 3.3 %copy-start.3 = (s32[128,256]{1,0:T(8,128)S(1)}, s32[128,256]{1,0:T(8,128)}, u32[]{:S(2)}) copy-start(s32[128,256]{1,0:T(8,128)} %param.8) | copy-start | bytes 393220
  2.3 20.7 %collective-permute-start.3 = (bf16[128,1152]{1,0:T(8,128)(2,1)S(1)}, bf16[128,1152]{1,0:T(8,128)(2,1)S(1)}, u32[]{:S(2)}, u32[]{:S(2)}) collective-permute-start(bf16[128,1152]{1,0:T(8,128)(2,1)S(1)} %pad_maximum_fusion.9), channel_id=1, source_target_pairs={{0,32},{16,48},{1,33},{17,49},{2,34},{18,50},{3,35},{19,51},{4,36}... | collective-permute-start | bytes 884744 | tf_op jit(solution)/shard_map/ppermute | solution.py:114
  5.4 3.7 %collective-permute-start = (f32[2816]{0:T(1024)S(1)}, f32[2816]{0:T(1024)S(1)}, u32[]{:S(2)}, u32[]{:S(2)}) collective-permute-start(f32[2816]{0:T(1024)S(1)} %pad_maximum_fusion.12), channel_id=1, source_target_pairs={{0,16},{16,0},{1,17},{17,1},{2,18},{18,2},{3,19},{19,3},{4,20},{20... | collective-permute-start | bytes 33800 | tf_op jit(solution)/shard_map/ppermute | solution.py:90
  9.8 19.8 %all-to-all-start = ((f32[16,1,2816]{2,1,0:T(1,128)}), f32[16,1,2816]{2,1,0:T(1,128)S(1)}, u32[]{:S(2)}, u32[]{:S(2)}) async-start(f32[16,1,2816]{2,1,0:T(1,128)} %broadcast_in_dim.7), calls=%async_computation | async-start | bytes 360448 | tf_op jit(solution)/shard_map/all_to_all | solution.py:24
  20.3 9.5 %collective-permute-start.1 = (bf16[2,128,256]{2,1,0:T(8,128)(2,1)S(1)}, bf16[2,128,256]{2,1,0:T(8,128)(2,1)S(1)}, u32[]{:S(2)}, u32[]{:S(2)}) collective-permute-start(bf16[2,128,256]{2,1,0:T(8,128)(2,1)S(1)} %pad_maximum_fusion.10), channel_id=1, source_target_pairs={{0,16},{16,0},{1,17},{17,1},{2,18},{18,2},{3,19},{19,3},{4,20},{20... | collective-permute-start | bytes 393224 | tf_op jit(solution)/shard_map/ppermute | solution.py:102
  23.1 18.9 %collective-permute-start.4 = (bf16[256,1152]{1,0:T(8,128)(2,1)S(1)}, bf16[256,1152]{1,0:T(8,128)(2,1)S(1)}, u32[]{:S(2)}, u32[]{:S(2)}) collective-permute-start(bf16[256,1152]{1,0:T(8,128)(2,1)S(1)} %pad_maximum_fusion.8), channel_id=1, source_target_pairs={{0,16},{16,0},{1,17},{17,1},{2,18},{18,2},{3,19},{19,3},{4,20},{20... | collective-permute-start | bytes 1769480 | tf_op jit(solution)/shard_map/ppermute | solution.py:115
  29.9 12.0 %collective-permute-start.2 = (bf16[2,128,256]{2,1,0:T(8,128)(2,1)S(1)}, bf16[2,128,256]{2,1,0:T(8,128)(2,1)S(1)}, u32[]{:S(2)}, u32[]{:S(2)}) collective-permute-start(bf16[2,128,256]{2,1,0:T(8,128)(2,1)S(1)} %pad_maximum_fusion.11), channel_id=1, source_target_pairs={{16,272},{17,208},{18,144},{19,80},{20,16},{21,464},{22,400},{23,3... | collective-permute-start | bytes 393224 | tf_op jit(solution)/shard_map/ppermute | solution.py:126
  43.9 12.9 %copy-start.5 = (f32[128,256]{1,0:T(8,128)S(1)}, f32[128,256]{1,0:T(8,128)}, u32[]{:S(2)}) copy-start(f32[128,256]{1,0:T(8,128)} %param.6) | copy-start | bytes 393220
  43.9 41.5 %all-to-all-start.1 = ((bf16[16,2,128,256]{3,2,1,0:T(8,128)(2,1)}), bf16[16,2,128,256]{3,2,1,0:T(8,128)(2,1)S(1)}, u32[]{:S(2)}, u32[]{:S(2)}) async-start(bf16[16,2,128,256]{3,2,1,0:T(8,128)(2,1)} %broadcast_in_dim.8), calls=%async_computation.1 | async-start | bytes 4194304 | tf_op jit(solution)/shard_map/all_to_all | solution.py:144
  57.0 28.6 %collective-permute-start.10 = (f32[32,640]{1,0:T(8,128)S(1)}, f32[32,640]{1,0:T(8,128)S(1)}, u32[]{:S(2)}, u32[]{:S(2)}) collective-permute-start(f32[32,640]{1,0:T(8,128)S(1)} %get-tuple-element.37), channel_id=1, source_target_pairs={{0,256},{1,257},{2,258},{3,259},{4,260},{5,261},{6,262},{7,263},{8... | collective-permute-start | bytes 245768 | tf_op jit(solution)/shard_map/ppermute | solution.py:162
  57.7 27.9 %collective-permute-start.7 = (f32[32,640]{1,0:T(8,128)S(1)}, f32[32,640]{1,0:T(8,128)S(1)}, u32[]{:S(2)}, u32[]{:S(2)}) collective-permute-start(f32[32,640]{1,0:T(8,128)S(1)} %get-tuple-element.36), channel_id=1, source_target_pairs={{0,64},{1,65},{2,66},{3,67},{4,68},{5,69},{6,70},{7,71},{8,72},{9,... | collective-permute-start | bytes 245768 | tf_op jit(solution)/shard_map/ppermute | solution.py:162
  62.0 23.6 %collective-permute-start.8 = (f32[32,640]{1,0:T(8,128)S(1)}, f32[32,640]{1,0:T(8,128)S(1)}, u32[]{:S(2)}, u32[]{:S(2)}) collective-permute-start(f32[32,640]{1,0:T(8,128)S(1)} %get-tuple-element.39), channel_id=1, source_target_pairs={{0,128},{1,129},{2,130},{3,131},{4,132},{5,133},{6,134},{7,135},{8... | collective-permute-start | bytes 245768 | tf_op jit(solution)/shard_map/ppermute | solution.py:162
  65.1 20.8 %collective-permute-start.9 = (f32[32,640]{1,0:T(8,128)S(1)}, f32[32,640]{1,0:T(8,128)S(1)}, u32[]{:S(2)}, u32[]{:S(2)}) collective-permute-start(f32[32,640]{1,0:T(8,128)S(1)} %get-tuple-element.38), channel_id=1, source_target_pairs={{0,192},{1,193},{2,194},{3,195},{4,196},{5,197},{6,198},{7,199},{8... | collective-permute-start | bytes 245768 | tf_op jit(solution)/shard_map/ppermute | solution.py:162
  86.0 8.0 %collective-permute-start.11 = (f32[2,8,640]{2,1,0:T(8,128)S(1)}, f32[2,8,640]{2,1,0:T(8,128)S(1)}, u32[]{:S(2)}, u32[]{:S(2)}) collective-permute-start(f32[2,8,640]{2,1,0:T(8,128)S(1)} %dynamic-slice_bitcast_fusion.4), channel_id=1, source_target_pairs={{0,32},{16,48},{1,33},{17,49},{2,34},{18,50},{3,35},{19,51},{4,36}... | collective-permute-start | bytes 122888 | tf_op jit(solution)/shard_map/ppermute | solution.py:173
  89.5 8.3 %collective-permute-start.5 = (bf16[16,128,256]{2,1,0:T(8,128)(2,1)S(1)}, bf16[16,128,256]{2,1,0:T(8,128)(2,1)S(1)}, u32[]{:S(2)}, u32[]{:S(2)}) collective-permute-start(bf16[16,128,256]{2,1,0:T(8,128)(2,1)S(1)} %broadcast_select_fusion.1), channel_id=1, source_target_pairs={{0,16},{16,0},{1,17},{17,1},{2,18},{18,2},{3,19},{19,3},{4,20},{20... | collective-permute-start | bytes 3145736 | tf_op jit(solution)/shard_map/ppermute | solution.py:166
  91.5 6.8 %collective-permute-start.6 = (bf16[16,128,256]{2,1,0:T(8,128)(2,1)S(1)}, bf16[16,128,256]{2,1,0:T(8,128)(2,1)S(1)}, u32[]{:S(2)}, u32[]{:S(2)}) collective-permute-start(bf16[16,128,256]{2,1,0:T(8,128)(2,1)S(1)} %slice_bitcast_fusion), channel_id=1, source_target_pairs={{16,0},{17,1},{18,2},{19,3},{20,4},{21,5},{22,6},{23,7},{24,8},{25... | collective-permute-start | bytes 3145736 | tf_op jit(solution)/shard_map/ppermute | solution.py:167
  94.1 3.1 %collective-permute-start.12 = (f32[8,1280]{1,0:T(8,128)S(1)}, f32[8,1280]{1,0:T(8,128)S(1)}, u32[]{:S(2)}, u32[]{:S(2)}) collective-permute-start(f32[8,1280]{1,0:T(8,128)S(1)} %fusion.34), channel_id=1, source_target_pairs={{0,16},{16,0},{1,17},{17,1},{2,18},{18,2},{3,19},{19,3},{4,20},{20... | collective-permute-start | bytes 122888 | tf_op jit(solution)/shard_map/ppermute | solution.py:40

commit v6 on v5

--- a/solution.py
+++ b/solution.py
@@ -18,9 +18,8 @@
     return jnp.stack([jnp.sum(weight, 0), jnp.sum(kept, 0), jnp.sum(kept * values, 0)])
 
 
-def summed_over(flat, groups):
-    peers = len(groups[0])
-    sent = jnp.broadcast_to(flat[None, None], (peers, 1, flat.size))
+def summed_over(by_side, groups):
+    sent = jnp.concatenate([by_side[:, None]] * (len(groups[0]) // by_side.shape[0]), 0)
     arrived = lax.all_to_all(sent, EVERY, 0, 0, tiled=True, axis_index_groups=groups)
     return jnp.sum(arrived, axis=(0, 1))
 
@@ -89,7 +88,9 @@
     partial = jnp.concatenate([moments_now.reshape(-1), moments_prev.reshape(-1), squares])
     partial = partial + lax.ppermute(partial, EVERY, swap)
     columns = [[at(k, h, c) for k in range(chips)] for c in range(cols) for h in range(CORES)]
-    total = summed_over(partial, columns)
+    common, both = partial[: 3 * (width + tested)], partial[3 * (width + tested) :]
+    by_side = jnp.stack([jnp.concatenate([common, half]) for half in jnp.split(both, 2)])
+    total = summed_over(by_side, columns)
     centre_now, spread_now = finished(total[: 3 * width].reshape(3, width))
     centre_prev, spread_prev = finished(
         total[3 * width : 3 * (width + tested)].reshape(3, tested)
@@ -169,6 +170,8 @@
     total_rows = kept
     for arrived in arrivals:
         total_rows = total_rows + arrived
+    power = squares / samples_all
+    total_rows = total_rows * lax.rsqrt(power + epsilon)[None, :]
     shares = total_rows.reshape(2, CORES, out_rows, share)
     own, other_half = half_of(shares, side), lax.ppermute(half_of(shares, 1 - side), EVERY, across)
     left_chip = side == 0
@@ -177,13 +180,7 @@
     )
     cross = folded(shares, core, swap)
     spread_rows = lax.dynamic_slice_in_dim(spread_prev, row * out_rows, out_rows, 0)
-    power = squares / samples_all
-    assoc_score = (
-        cross
-        * lax.rsqrt(spread_rows + epsilon)[:, None]
-        * lax.rsqrt(power + epsilon)[None, :]
-        / math.sqrt(samples_all)
-    )
+    assoc_score = cross * lax.rsqrt(spread_rows + epsilon)[:, None] / math.sqrt(samples_all)
 
     def product(a, b):
         return lax.dot_general(

time: 100 us -> 110 us (1.10)
  the two profiles are of different devices: /device:TPU:61 before, /device:TPU:1 now
where the time goes in v6:
time: 110 us; the launch traced here: 109 us
  starting transfers between devices  59.4 us (54%)
  waiting for transfers between devices  33.6 us (31%)
  local copies, waits for them, and re-layouts  9.02 us (8%)
  other arithmetic  4.48 us (4%)
  matrix products  1.33 us (1%)
  between operations  1.23 us (1%)
    all_to_all x1, waiting for transfers between devices, body(): lax.all_to_all(jnp.broadcast_to(chip_block[None], (cols, *chip_block.shap...  17.1 us
    all_to_all x1, starting transfers between devices, body(): lax.all_to_all(jnp.broadcast_to(chip_block[None], (cols, *chip_block.shap...  14 us
    ppermute x4, starting transfers between devices, body(): arrivals.append(lax.ppermute(leaving, EVERY, routes))  10.2 us
    ppermute x1, starting transfers between devices, body(): partial = partial + lax.ppermute(partial, EVERY, swap)  8.79 us
    ppermute x1, waiting for transfers between devices, body(): lax.ppermute(chip_block, EVERY, [(at(c, 1, v), at(lands[c][v], 1, c)) for...  7.63 us
    unnamed x20, local copies, waits for them, and re-layouts  6.33 us
    all_to_all x1, waiting for transfers between devices, summed_over(): lax.all_to_all(sent, EVERY, 0, 0, tiled=True, axis_index_groups=groups)  6.01 us
    all_to_all x1, starting transfers between devices, summed_over(): lax.all_to_all(sent, EVERY, 0, 0, tiled=True, axis_index_groups=groups)  5.97 us
  transfers between devices with their start and end apart: 15, of which 5 were waited for; matrix products, arithmetic and copies ran while one was open for 8% of the time, Pallas kernels for 0%

profile of v6, /device:TPU:1, one launch (start us, length us, event | category | flops | bytes accessed | tf_op | source)
XLA Modules:
  0.0 109.0 jit_solution(2880866022514097743)
XLA Ops:
  0.7 1.0 fusion.31
  1.7 1.0 fusion.32
  2.7 1.1 multiply_reduce_fusion
  3.8 8.8 %collective-permute-start = (f32[2816]{0:T(1024)S(1)}, f32[2816]{0:T(1024)S(1)}, u32[]{:S(2)}, u32[]{:S(2)}) collective-permute-start(f32[2816]{0:T(1024)S(1)} %pad_maximum_fusion.13), channel_id=1, source_target_pairs={{0,16},{16,0},{1,17},{17,1},{2,18},{18,2},{3,19},{19,3},{4,20},{20... | collective-permute-start | bytes 33800 | tf_op jit(solution)/shard_map/ppermute | solution.py:89
  12.6 1.2 %copy.17 = bf16[128,1280]{0,1:T(8,128)(2,1)S(1)} copy(bf16[128,1280]{1,0:T(8,128)(2,1)} %param.11) | data formatting | bytes 655360 | tf_op args[5]
  14.1 1.9 %collective-permute-start.3 = (bf16[128,1152]{1,0:T(8,128)(2,1)S(1)}, bf16[128,1152]{1,0:T(8,128)(2,1)S(1)}, u32[]{:S(2)}, u32[]{:S(2)}) collective-permute-start(bf16[128,1152]{1,0:T(8,128)(2,1)S(1)} %pad_maximum_fusion.9), channel_id=1, source_target_pairs={{0,32},{16,48},{1,33},{17,49},{2,34},{18,50},{3,35},{19,51},{4,36}... | collective-permute-start | bytes 884744 | tf_op jit(solution)/shard_map/ppermute | solution.py:115
  18.0 0.6 constant_dynamic-update-slice_fusion.4
  18.6 0.6 constant_dynamic-update-slice_fusion.3
  19.2 0.6 constant_dynamic-update-slice_fusion.2
  19.8 0.6 constant_dynamic-update-slice_fusion.1
  20.5 0.6 constant_dynamic-update-slice_fusion
  21.1 6.0 %all-to-all-start = ((f32[16,1,2176]{2,1,0:T(1,128)}), f32[16,1,2176]{2,1,0:T(1,128)S(1)}, u32[]{:S(2)}, u32[]{:S(2)}) async-start(f32[16,1,2176]{2,1,0:T(1,128)} %constant_dynamic-update-slice_fusion), calls=%async_computation | async-start | bytes 278528 | tf_op jit(solution)/shard_map/all_to_all | solution.py:23
  27.1 2.5 %collective-permute-start.1 = (bf16[2,128,256]{2,1,0:T(8,128)(2,1)S(1)}, bf16[2,128,256]{2,1,0:T(8,128)(2,1)S(1)}, u32[]{:S(2)}, u32[]{:S(2)}) collective-permute-start(bf16[2,128,256]{2,1,0:T(8,128)(2,1)S(1)} %pad_maximum_fusion.10), channel_id=1, source_target_pairs={{0,16},{16,0},{1,17},{17,1},{2,18},{18,2},{3,19},{19,3},{4,20},{20... | collective-permute-start | bytes 393224 | tf_op jit(solution)/shard_map/ppermute | solution.py:103
  29.8 6.0 %all-to-all-done = f32[16,1,2176]{2,1,0:T(1,128)S(1)} async-done(((f32[16,1,2176]{2,1,0:T(1,128)}), f32[16,1,2176]{2,1,0:T(1,128)S(1)}, u32[]{:S(2)}, u32[]{:S(2)}) %all-to-all-start) | async-done | bytes 139296 | tf_op jit(solution)/shard_map/all_to_all | solution.py:23
  36.0 3.9 %collective-permute-start.4 = (bf16[256,1152]{1,0:T(8,128)(2,1)S(1)}, bf16[256,1152]{1,0:T(8,128)(2,1)S(1)}, u32[]{:S(2)}, u32[]{:S(2)}) collective-permute-start(bf16[256,1152]{1,0:T(8,128)(2,1)S(1)} %pad_maximum_fusion.8), channel_id=1, source_target_pairs={{0,16},{16,0},{1,17},{17,1},{2,18},{18,2},{3,19},{19,3},{4,20},{20... | collective-permute-start | bytes 1769480 | tf_op jit(solution)/shard_map/ppermute | solution.py:116
  40.0 2.5 %collective-permute-start.2 = (bf16[2,128,256]{2,1,0:T(8,128)(2,1)S(1)}, bf16[2,128,256]{2,1,0:T(8,128)(2,1)S(1)}, u32[]{:S(2)}, u32[]{:S(2)}) collective-permute-start(bf16[2,128,256]{2,1,0:T(8,128)(2,1)S(1)} %pad_maximum_fusion.11), channel_id=1, source_target_pairs={{16,272},{17,208},{18,144},{19,80},{20,16},{21,464},{22,400},{23,3... | collective-permute-start | bytes 393224 | tf_op jit(solution)/shard_map/ppermute | solution.py:127
  42.5 7.6 %collective-permute-done.2 = bf16[2,128,256]{2,1,0:T(8,128)(2,1)S(1)} collective-permute-done((bf16[2,128,256]{2,1,0:T(8,128)(2,1)S(1)}, bf16[2,128,256]{2,1,0:T(8,128)(2,1)S(1)}, u32[]{:S(2)}, u32[]{:S(2)}) %collective-permute-start.2) | collective-permute-done | bytes 131104 | tf_op jit(solution)/shard_map/ppermute | solution.py:127
  50.5 1.6 %broadcast_in_dim.8 = bf16[16,2,128,256]{3,2,1,0:T(8,128)(2,1)} broadcast(bf16[2,128,256]{2,1,0:T(8,128)(2,1)S(1)} %broadcast_select_fusion.4), dimensions={1,2,3} | broadcast | bytes 2228224 | tf_op jit(solution)/shard_map/broadcast_in_dim | solution.py:146
  52.1 14.0 %all-to-all-start.1 = ((bf16[16,2,128,256]{3,2,1,0:T(8,128)(2,1)}), bf16[16,2,128,256]{3,2,1,0:T(8,128)(2,1)S(1)}, u32[]{:S(2)}, u32[]{:S(2)}) async-start(bf16[16,2,128,256]{3,2,1,0:T(8,128)(2,1)} %broadcast_in_dim.8), calls=%async_computation.1 | async-start | bytes 4194304 | tf_op jit(solution)/shard_map/all_to_all | solution.py:145
  66.4 0.7 collective-permute-start.10
  67.0 2.2 %collective-permute-start.7 = (f32[32,640]{1,0:T(8,128)S(1)}, f32[32,640]{1,0:T(8,128)S(1)}, u32[]{:S(2)}, u32[]{:S(2)}) collective-permute-start(f32[32,640]{1,0:T(8,128)S(1)} %get-tuple-element.32), channel_id=1, source_target_pairs={{0,64},{1,65},{2,66},{3,67},{4,68},{5,69},{6,70},{7,71},{8,72},{9,... | collective-permute-start | bytes 245768 | tf_op jit(solution)/shard_map/ppermute | solution.py:163
  69.2 2.2 %collective-permute-start.8 = (f32[32,640]{1,0:T(8,128)S(1)}, f32[32,640]{1,0:T(8,128)S(1)}, u32[]{:S(2)}, u32[]{:S(2)}) collective-permute-start(f32[32,640]{1,0:T(8,128)S(1)} %get-tuple-element.35), channel_id=1, source_target_pairs={{0,128},{1,129},{2,130},{3,131},{4,132},{5,133},{6,134},{7,135},{8... | collective-permute-start | bytes 245768 | tf_op jit(solution)/shard_map/ppermute | solution.py:163
  71.4 5.2 %collective-permute-start.9 = (f32[32,640]{1,0:T(8,128)S(1)}, f32[32,640]{1,0:T(8,128)S(1)}, u32[]{:S(2)}, u32[]{:S(2)}) collective-permute-start(f32[32,640]{1,0:T(8,128)S(1)} %get-tuple-element.34), channel_id=1, source_target_pairs={{0,192},{1,193},{2,194},{3,195},{4,196},{5,197},{6,198},{7,199},{8... | collective-permute-start | bytes 245768 | tf_op jit(solution)/shard_map/ppermute | solution.py:163
  76.6 17.1 %all-to-all-done.1 = bf16[16,2,128,256]{3,2,1,0:T(8,128)(2,1)S(1)} async-done(((bf16[16,2,128,256]{3,2,1,0:T(8,128)(2,1)}), bf16[16,2,128,256]{3,2,1,0:T(8,128)(2,1)S(1)}, u32[]{:S(2)}, u32[]{:S(2)}) %all-to-all-start.1) | async-done | bytes 2097184 | tf_op jit(solution)/shard_map/all_to_all | solution.py:145
  93.9 1.7 %collective-permute-done.9 = f32[32,640]{1,0:T(8,128)S(1)} collective-permute-done((f32[32,640]{1,0:T(8,128)S(1)}, f32[32,640]{1,0:T(8,128)S(1)}, u32[]{:S(2)}, u32[]{:S(2)}) %collective-permute-start.9) | collective-permute-done | bytes 81952 | tf_op jit(solution)/shard_map/ppermute | solution.py:163
  95.6 3.3 %collective-permute-start.11 = (f32[2,8,640]{2,1,0:T(8,128)S(1)}, f32[2,8,640]{2,1,0:T(8,128)S(1)}, u32[]{:S(2)}, u32[]{:S(2)}) collective-permute-start(f32[2,8,640]{2,1,0:T(8,128)S(1)} %dynamic-slice_bitcast_fusion.4), channel_id=1, source_target_pairs={{0,32},{16,48},{1,33},{17,49},{2,34},{18,50},{3,35},{19,51},{4,36}... | collective-permute-start | bytes 122888 | tf_op jit(solution)/shard_map/ppermute | solution.py:176
  99.0 1.9 %collective-permute-start.5 = (bf16[16,128,256]{2,1,0:T(8,128)(2,1)S(1)}, bf16[16,128,256]{2,1,0:T(8,128)(2,1)S(1)}, u32[]{:S(2)}, u32[]{:S(2)}) collective-permute-start(bf16[16,128,256]{2,1,0:T(8,128)(2,1)S(1)} %broadcast_select_fusion.1), channel_id=1, source_target_pairs={{0,16},{16,0},{1,17},{17,1},{2,18},{18,2},{3,19},{19,3},{4,20},{20... | collective-permute-start | bytes 3145736 | tf_op jit(solution)/shard_map/ppermute | solution.py:167
  101.0 2.5 %collective-permute-start.6 = (bf16[16,128,256]{2,1,0:T(8,128)(2,1)S(1)}, bf16[16,128,256]{2,1,0:T(8,128)(2,1)S(1)}, u32[]{:S(2)}, u32[]{:S(2)}) collective-permute-start(bf16[16,128,256]{2,1,0:T(8,128)(2,1)S(1)} %slice_bitcast_fusion), channel_id=1, source_target_pairs={{16,0},{17,1},{18,2},{19,3},{20,4},{21,5},{22,6},{23,7},{24,8},{25... | collective-permute-start | bytes 3145736 | tf_op jit(solution)/shard_map/ppermute | solution.py:168
  103.5 1.9 %collective-permute-start.12 = (f32[8,1280]{1,0:T(8,128)S(1)}, f32[8,1280]{1,0:T(8,128)S(1)}, u32[]{:S(2)}, u32[]{:S(2)}) collective-permute-start(f32[8,1280]{1,0:T(8,128)S(1)} %fusion.34), channel_id=1, source_target_pairs={{0,16},{16,0},{1,17},{17,1},{2,18},{18,2},{3,19},{19,3},{4,20},{20... | collective-permute-start | bytes 122888 | tf_op jit(solution)/shard_map/ppermute | solution.py:39
  105.5 1.1 %collective-permute-done.12 = f32[8,1280]{1,0:T(8,128)S(1)} collective-permute-done((f32[8,1280]{1,0:T(8,128)S(1)}, f32[8,1280]{1,0:T(8,128)S(1)}, u32[]{:S(2)}, u32[]{:S(2)}) %collective-permute-start.12) | collective-permute-done | bytes 40992 | tf_op jit(solution)/shard_map/ppermute | solution.py:39
  106.6 0.7 fusion.39
  108.3 0.8 copy.22
  (62 shorter events, 4.5 us)
Async XLA Ops:
  0.6 13.2 %copy-start.1 = (s32[128,256]{1,0:T(8,128)S(1)}, s32[128,256]{1,0:T(8,128)}, u32[]{:S(2)}) copy-start(s32[128,256]{1,0:T(8,128)} %param.10) | copy-start | bytes 393220
  0.6 13.2 %copy-start.3 = (bf16[128,256]{1,0:T(8,128)(2,1)S(1)}, bf16[128,256]{1,0:T(8,128)(2,1)}, u32[]{:S(2)}) copy-start(bf16[128,256]{1,0:T(8,128)(2,1)} %param.9) | copy-start | bytes 196612
  3.8 12.3 %collective-permute-start = (f32[2816]{0:T(1024)S(1)}, f32[2816]{0:T(1024)S(1)}, u32[]{:S(2)}, u32[]{:S(2)}) collective-permute-start(f32[2816]{0:T(1024)S(1)} %pad_maximum_fusion.13), channel_id=1, source_target_pairs={{0,16},{16,0},{1,17},{17,1},{2,18},{18,2},{3,19},{19,3},{4,20},{20... | collective-permute-start | bytes 33800 | tf_op jit(solution)/shard_map/ppermute | solution.py:89
  13.8 13.2 %copy-start = (bf16[128,256]{1,0:T(8,128)(2,1)S(1)}, bf16[128,256]{1,0:T(8,128)(2,1)}, u32[]{:S(2)}) copy-start(bf16[128,256]{1,0:T(8,128)(2,1)} %param.7) | copy-start | bytes 196612
  13.8 13.2 %copy-start.2 = (s32[128,256]{1,0:T(8,128)S(1)}, s32[128,256]{1,0:T(8,128)}, u32[]{:S(2)}) copy-start(s32[128,256]{1,0:T(8,128)} %param.8) | copy-start | bytes 393220
  14.1 21.8 %collective-permute-start.3 = (bf16[128,1152]{1,0:T(8,128)(2,1)S(1)}, bf16[128,1152]{1,0:T(8,128)(2,1)S(1)}, u32[]{:S(2)}, u32[]{:S(2)}) collective-permute-start(bf16[128,1152]{1,0:T(8,128)(2,1)S(1)} %pad_maximum_fusion.9), channel_id=1, source_target_pairs={{0,32},{16,48},{1,33},{17,49},{2,34},{18,50},{3,35},{19,51},{4,36}... | collective-permute-start | bytes 884744 | tf_op jit(solution)/shard_map/ppermute | solution.py:115
  21.1 14.7 %all-to-all-start = ((f32[16,1,2176]{2,1,0:T(1,128)}), f32[16,1,2176]{2,1,0:T(1,128)S(1)}, u32[]{:S(2)}, u32[]{:S(2)}) async-start(f32[16,1,2176]{2,1,0:T(1,128)} %constant_dynamic-update-slice_fusion), calls=%async_computation | async-start | bytes 278528 | tf_op jit(solution)/shard_map/all_to_all | solution.py:23
  27.1 12.8 %collective-permute-start.1 = (bf16[2,128,256]{2,1,0:T(8,128)(2,1)S(1)}, bf16[2,128,256]{2,1,0:T(8,128)(2,1)S(1)}, u32[]{:S(2)}, u32[]{:S(2)}) collective-permute-start(bf16[2,128,256]{2,1,0:T(8,128)(2,1)S(1)} %pad_maximum_fusion.10), channel_id=1, source_target_pairs={{0,16},{16,0},{1,17},{17,1},{2,18},{18,2},{3,19},{19,3},{4,20},{20... | collective-permute-start | bytes 393224 | tf_op jit(solution)/shard_map/ppermute | solution.py:103
  36.0 14.1 %collective-permute-start.4 = (bf16[256,1152]{1,0:T(8,128)(2,1)S(1)}, bf16[256,1152]{1,0:T(8,128)(2,1)S(1)}, u32[]{:S(2)}, u32[]{:S(2)}) collective-permute-start(bf16[256,1152]{1,0:T(8,128)(2,1)S(1)} %pad_maximum_fusion.8), channel_id=1, source_target_pairs={{0,16},{16,0},{1,17},{17,1},{2,18},{18,2},{3,19},{19,3},{4,20},{20... | collective-permute-start | bytes 1769480 | tf_op jit(solution)/shard_map/ppermute | solution.py:116
  40.0 10.1 %collective-permute-start.2 = (bf16[2,128,256]{2,1,0:T(8,128)(2,1)S(1)}, bf16[2,128,256]{2,1,0:T(8,128)(2,1)S(1)}, u32[]{:S(2)}, u32[]{:S(2)}) collective-permute-start(bf16[2,128,256]{2,1,0:T(8,128)(2,1)S(1)} %pad_maximum_fusion.11), channel_id=1, source_target_pairs={{16,272},{17,208},{18,144},{19,80},{20,16},{21,464},{22,400},{23,3... | collective-permute-start | bytes 393224 | tf_op jit(solution)/shard_map/ppermute | solution.py:127
  52.1 14.0 %copy-start.4 = (f32[128,256]{1,0:T(8,128)S(1)}, f32[128,256]{1,0:T(8,128)}, u32[]{:S(2)}) copy-start(f32[128,256]{1,0:T(8,128)} %param.6) | copy-start | bytes 393220
  52.1 41.6 %all-to-all-start.1 = ((bf16[16,2,128,256]{3,2,1,0:T(8,128)(2,1)}), bf16[16,2,128,256]{3,2,1,0:T(8,128)(2,1)S(1)}, u32[]{:S(2)}, u32[]{:S(2)}) async-start(bf16[16,2,128,256]{3,2,1,0:T(8,128)(2,1)} %broadcast_in_dim.8), calls=%async_computation.1 | async-start | bytes 4194304 | tf_op jit(solution)/shard_map/all_to_all | solution.py:145
  66.4 27.5 %collective-permute-start.10 = (f32[32,640]{1,0:T(8,128)S(1)}, f32[32,640]{1,0:T(8,128)S(1)}, u32[]{:S(2)}, u32[]{:S(2)}) collective-permute-start(f32[32,640]{1,0:T(8,128)S(1)} %get-tuple-element.33), channel_id=1, source_target_pairs={{0,256},{1,257},{2,258},{3,259},{4,260},{5,261},{6,262},{7,263},{8... | collective-permute-start | bytes 245768 | tf_op jit(solution)/shard_map/ppermute | solution.py:163
  67.0 26.8 %collective-permute-start.7 = (f32[32,640]{1,0:T(8,128)S(1)}, f32[32,640]{1,0:T(8,128)S(1)}, u32[]{:S(2)}, u32[]{:S(2)}) collective-permute-start(f32[32,640]{1,0:T(8,128)S(1)} %get-tuple-element.32), channel_id=1, source_target_pairs={{0,64},{1,65},{2,66},{3,67},{4,68},{5,69},{6,70},{7,71},{8,72},{9,... | collective-permute-start | bytes 245768 | tf_op jit(solution)/shard_map/ppermute | solution.py:163
  69.2 24.6 %collective-permute-start.8 = (f32[32,640]{1,0:T(8,128)S(1)}, f32[32,640]{1,0:T(8,128)S(1)}, u32[]{:S(2)}, u32[]{:S(2)}) collective-permute-start(f32[32,640]{1,0:T(8,128)S(1)} %get-tuple-element.35), channel_id=1, source_target_pairs={{0,128},{1,129},{2,130},{3,131},{4,132},{5,133},{6,134},{7,135},{8... | collective-permute-start | bytes 245768 | tf_op jit(solution)/shard_map/ppermute | solution.py:163
  71.4 24.2 %collective-permute-start.9 = (f32[32,640]{1,0:T(8,128)S(1)}, f32[32,640]{1,0:T(8,128)S(1)}, u32[]{:S(2)}, u32[]{:S(2)}) collective-permute-start(f32[32,640]{1,0:T(8,128)S(1)} %get-tuple-element.34), channel_id=1, source_target_pairs={{0,192},{1,193},{2,194},{3,195},{4,196},{5,197},{6,198},{7,199},{8... | collective-permute-start | bytes 245768 | tf_op jit(solution)/shard_map/ppermute | solution.py:163
  95.6 7.8 %collective-permute-start.11 = (f32[2,8,640]{2,1,0:T(8,128)S(1)}, f32[2,8,640]{2,1,0:T(8,128)S(1)}, u32[]{:S(2)}, u32[]{:S(2)}) collective-permute-start(f32[2,8,640]{2,1,0:T(8,128)S(1)} %dynamic-slice_bitcast_fusion.4), channel_id=1, source_target_pairs={{0,32},{16,48},{1,33},{17,49},{2,34},{18,50},{3,35},{19,51},{4,36}... | collective-permute-start | bytes 122888 | tf_op jit(solution)/shard_map/ppermute | solution.py:176
  99.0 8.4 %collective-permute-start.5 = (bf16[16,128,256]{2,1,0:T(8,128)(2,1)S(1)}, bf16[16,128,256]{2,1,0:T(8,128)(2,1)S(1)}, u32[]{:S(2)}, u32[]{:S(2)}) collective-permute-start(bf16[16,128,256]{2,1,0:T(8,128)(2,1)S(1)} %broadcast_select_fusion.1), channel_id=1, source_target_pairs={{0,16},{16,0},{1,17},{17,1},{2,18},{18,2},{3,19},{19,3},{4,20},{20... | collective-permute-start | bytes 3145736 | tf_op jit(solution)/shard_map/ppermute | solution.py:167
  101.0 6.8 %collective-permute-start.6 = (bf16[16,128,256]{2,1,0:T(8,128)(2,1)S(1)}, bf16[16,128,256]{2,1,0:T(8,128)(2,1)S(1)}, u32[]{:S(2)}, u32[]{:S(2)}) collective-permute-start(bf16[16,128,256]{2,1,0:T(8,128)(2,1)S(1)} %slice_bitcast_fusion), channel_id=1, source_target_pairs={{16,0},{17,1},{18,2},{19,3},{20,4},{21,5},{22,6},{23,7},{24,8},{25... | collective-permute-start | bytes 3145736 | tf_op jit(solution)/shard_map/ppermute | solution.py:168
  103.5 3.1 %collective-permute-start.12 = (f32[8,1280]{1,0:T(8,128)S(1)}, f32[8,1280]{1,0:T(8,128)S(1)}, u32[]{:S(2)}, u32[]{:S(2)}) collective-permute-start(f32[8,1280]{1,0:T(8,128)S(1)} %fusion.34), channel_id=1, source_target_pairs={{0,16},{16,0},{1,17},{17,1},{2,18},{18,2},{3,19},{19,3},{4,20},{20... | collective-permute-start | bytes 122888 | tf_op jit(solution)/shard_map/ppermute | solution.py:39

commit v7 on v5

--- a/solution.py
+++ b/solution.py
@@ -169,6 +169,8 @@
     total_rows = kept
     for arrived in arrivals:
         total_rows = total_rows + arrived
+    power = jnp.where(side == 0, squares[:share], squares[share:]) / samples_all
+    total_rows = total_rows * lax.rsqrt(power + epsilon)[None, :]
     shares = total_rows.reshape(2, CORES, out_rows, share)
     own, other_half = half_of(shares, side), lax.ppermute(half_of(shares, 1 - side), EVERY, across)
     left_chip = side == 0
@@ -177,13 +179,7 @@
     )
     cross = folded(shares, core, swap)
     spread_rows = lax.dynamic_slice_in_dim(spread_prev, row * out_rows, out_rows, 0)
-    power = squares / samples_all
-    assoc_score = (
-        cross
-        * lax.rsqrt(spread_rows + epsilon)[:, None]
-        * lax.rsqrt(power + epsilon)[None, :]
-        / math.sqrt(samples_all)
-    )
+    assoc_score = cross * lax.rsqrt(spread_rows + epsilon)[:, None] / math.sqrt(samples_all)
 
     def product(a, b):
         return lax.dot_general(

time: 100 us -> 100 us (level)
  no operation moved by 1% of the time
where the time goes in v7:
time: 100 us; the launch traced here: 99.7 us
  starting transfers between devices  55.5 us (56%)
  waiting for transfers between devices  35 us (35%)
  local copies, waits for them, and re-layouts  4.92 us (5%)
  other arithmetic  1.58 us (2%)
  matrix products  1.38 us (1%)
  between operations  1.21 us (1%)
    all_to_all x1, waiting for transfers between devices, body(): lax.all_to_all(jnp.broadcast_to(chip_block[None], (cols, *chip_block.shap...  18.1 us
    all_to_all x1, starting transfers between devices, body(): lax.all_to_all(jnp.broadcast_to(chip_block[None], (cols, *chip_block.shap...  12.9 us
    all_to_all x1, starting transfers between devices, summed_over(): lax.all_to_all(sent, EVERY, 0, 0, tiled=True, axis_index_groups=groups)  10.4 us
    ppermute x4, starting transfers between devices, body(): arrivals.append(lax.ppermute(leaving, EVERY, routes))  10.4 us
    ppermute x1, waiting for transfers between devices, body(): lax.ppermute(chip_block, EVERY, [(at(c, 1, v), at(lands[c][v], 1, c)) for...  10.1 us
    all_to_all x1, waiting for transfers between devices, summed_over(): lax.all_to_all(sent, EVERY, 0, 0, tiled=True, axis_index_groups=groups)  4.63 us
    ppermute x1, starting transfers between devices, body(): lax.ppermute(half_of(shares, 1 - side), EVERY, across)  3.54 us
    ppermute x1, starting transfers between devices, body(): partial = partial + lax.ppermute(partial, EVERY, swap)  2.86 us
  transfers between devices with their start and end apart: 15, of which 6 were waited for; matrix products, arithmetic and copies ran while one was open for 3% of the time, Pallas kernels for 0%

profile of v7, /device:TPU:61, one launch (start us, length us, event | category | flops | bytes accessed | tf_op | source)
XLA Modules:
  0.0 99.7 jit_solution(9760935716957383644)
XLA Ops:
  0.7 1.2 %copy.30 = bf16[128,1280]{0,1:T(8,128)(2,1)S(1)} copy(bf16[128,1280]{1,0:T(8,128)(2,1)} %param.11) | data formatting | bytes 655360 | tf_op args[5]
  2.0 0.2 copy.32
  2.3 2.8 %collective-permute-start.3 = (bf16[128,1152]{1,0:T(8,128)(2,1)S(1)}, bf16[128,1152]{1,0:T(8,128)(2,1)S(1)}, u32[]{:S(2)}, u32[]{:S(2)}) collective-permute-start(bf16[128,1152]{1,0:T(8,128)(2,1)S(1)} %pad_maximum_fusion.9), channel_id=1, source_target_pairs={{0,32},{16,48},{1,33},{17,49},{2,34},{18,50},{3,35},{19,51},{4,36}... | collective-permute-start | bytes 884744 | tf_op jit(solution)/shard_map/ppermute | solution.py:114
  5.4 2.9 %collective-permute-start = (f32[2816]{0:T(1024)S(1)}, f32[2816]{0:T(1024)S(1)}, u32[]{:S(2)}, u32[]{:S(2)}) collective-permute-start(f32[2816]{0:T(1024)S(1)} %pad_maximum_fusion.12), channel_id=1, source_target_pairs={{0,16},{16,0},{1,17},{17,1},{2,18},{18,2},{3,19},{19,3},{4,20},{20... | collective-permute-start | bytes 33800 | tf_op jit(solution)/shard_map/ppermute | solution.py:90
  8.3 0.8 collective-permute-done
  9.1 0.8 broadcast_in_dim.7
  9.8 10.4 %all-to-all-start = ((f32[16,1,2816]{2,1,0:T(1,128)}), f32[16,1,2816]{2,1,0:T(1,128)S(1)}, u32[]{:S(2)}, u32[]{:S(2)}) async-start(f32[16,1,2816]{2,1,0:T(1,128)} %broadcast_in_dim.7), calls=%async_computation | async-start | bytes 360448 | tf_op jit(solution)/shard_map/all_to_all | solution.py:24
  20.3 2.5 %collective-permute-start.1 = (bf16[2,128,256]{2,1,0:T(8,128)(2,1)S(1)}, bf16[2,128,256]{2,1,0:T(8,128)(2,1)S(1)}, u32[]{:S(2)}, u32[]{:S(2)}) collective-permute-start(bf16[2,128,256]{2,1,0:T(8,128)(2,1)S(1)} %pad_maximum_fusion.10), channel_id=1, source_target_pairs={{0,16},{16,0},{1,17},{17,1},{2,18},{18,2},{3,19},{19,3},{4,20},{20... | collective-permute-start | bytes 393224 | tf_op jit(solution)/shard_map/ppermute | solution.py:102
  22.8 0.2 copy.31
  23.1 1.9 %collective-permute-start.4 = (bf16[256,1152]{1,0:T(8,128)(2,1)S(1)}, bf16[256,1152]{1,0:T(8,128)(2,1)S(1)}, u32[]{:S(2)}, u32[]{:S(2)}) collective-permute-start(bf16[256,1152]{1,0:T(8,128)(2,1)S(1)} %pad_maximum_fusion.8), channel_id=1, source_target_pairs={{0,16},{16,0},{1,17},{17,1},{2,18},{18,2},{3,19},{19,3},{4,20},{20... | collective-permute-start | bytes 1769480 | tf_op jit(solution)/shard_map/ppermute | solution.py:115
  25.0 4.6 %all-to-all-done = f32[16,1,2816]{2,1,0:T(1,128)S(1)} async-done(((f32[16,1,2816]{2,1,0:T(1,128)}), f32[16,1,2816]{2,1,0:T(1,128)S(1)}, u32[]{:S(2)}, u32[]{:S(2)}) %all-to-all-start) | async-done | bytes 180256 | tf_op jit(solution)/shard_map/all_to_all | solution.py:24
  29.6 0.1 reduce_sum.79
  29.9 1.9 %collective-permute-start.2 = (bf16[2,128,256]{2,1,0:T(8,128)(2,1)S(1)}, bf16[2,128,256]{2,1,0:T(8,128)(2,1)S(1)}, u32[]{:S(2)}, u32[]{:S(2)}) collective-permute-start(bf16[2,128,256]{2,1,0:T(8,128)(2,1)S(1)} %pad_maximum_fusion.11), channel_id=1, source_target_pairs={{16,272},{17,208},{18,144},{19,80},{20,16},{21,464},{22,400},{23,3... | collective-permute-start | bytes 393224 | tf_op jit(solution)/shard_map/ppermute | solution.py:126
  31.8 10.1 %collective-permute-done.2 = bf16[2,128,256]{2,1,0:T(8,128)(2,1)S(1)} collective-permute-done((bf16[2,128,256]{2,1,0:T(8,128)(2,1)S(1)}, bf16[2,128,256]{2,1,0:T(8,128)(2,1)S(1)}, u32[]{:S(2)}, u32[]{:S(2)}) %collective-permute-start.2) | collective-permute-done | bytes 131104 | tf_op jit(solution)/shard_map/ppermute | solution.py:126
  42.0 0.4 fusion.4
  42.4 1.6 %broadcast_in_dim.8 = bf16[16,2,128,256]{3,2,1,0:T(8,128)(2,1)} broadcast(bf16[2,128,256]{2,1,0:T(8,128)(2,1)S(1)} %broadcast_select_fusion.4), dimensions={1,2,3} | broadcast | bytes 2228224 | tf_op jit(solution)/shard_map/broadcast_in_dim | solution.py:145
  43.9 12.9 %all-to-all-start.1 = ((bf16[16,2,128,256]{3,2,1,0:T(8,128)(2,1)}), bf16[16,2,128,256]{3,2,1,0:T(8,128)(2,1)S(1)}, u32[]{:S(2)}, u32[]{:S(2)}) async-start(bf16[16,2,128,256]{3,2,1,0:T(8,128)(2,1)} %broadcast_in_dim.8), calls=%async_computation.1 | async-start | bytes 4194304 | tf_op jit(solution)/shard_map/all_to_all | solution.py:144
  57.0 0.7 collective-permute-start.10
  57.7 4.3 %collective-permute-start.7 = (f32[32,640]{1,0:T(8,128)S(1)}, f32[32,640]{1,0:T(8,128)S(1)}, u32[]{:S(2)}, u32[]{:S(2)}) collective-permute-start(f32[32,640]{1,0:T(8,128)S(1)} %get-tuple-element.36), channel_id=1, source_target_pairs={{0,64},{1,65},{2,66},{3,67},{4,68},{5,69},{6,70},{7,71},{8,72},{9,... | collective-permute-start | bytes 245768 | tf_op jit(solution)/shard_map/ppermute | solution.py:162
  62.0 3.1 %collective-permute-start.8 = (f32[32,640]{1,0:T(8,128)S(1)}, f32[32,640]{1,0:T(8,128)S(1)}, u32[]{:S(2)}, u32[]{:S(2)}) collective-permute-start(f32[32,640]{1,0:T(8,128)S(1)} %get-tuple-element.39), channel_id=1, source_target_pairs={{0,128},{1,129},{2,130},{3,131},{4,132},{5,133},{6,134},{7,135},{8... | collective-permute-start | bytes 245768 | tf_op jit(solution)/shard_map/ppermute | solution.py:162
  65.1 2.3 %collective-permute-start.9 = (f32[32,640]{1,0:T(8,128)S(1)}, f32[32,640]{1,0:T(8,128)S(1)}, u32[]{:S(2)}, u32[]{:S(2)}) collective-permute-start(f32[32,640]{1,0:T(8,128)S(1)} %get-tuple-element.38), channel_id=1, source_target_pairs={{0,192},{1,193},{2,194},{3,195},{4,196},{5,197},{6,198},{7,199},{8... | collective-permute-start | bytes 245768 | tf_op jit(solution)/shard_map/ppermute | solution.py:162
  67.4 18.1 %all-to-all-done.1 = bf16[16,2,128,256]{3,2,1,0:T(8,128)(2,1)S(1)} async-done(((bf16[16,2,128,256]{3,2,1,0:T(8,128)(2,1)}), bf16[16,2,128,256]{3,2,1,0:T(8,128)(2,1)S(1)}, u32[]{:S(2)}, u32[]{:S(2)}) %all-to-all-start.1) | async-done | bytes 2097184 | tf_op jit(solution)/shard_map/all_to_all | solution.py:144
  85.6 0.3 collective-permute-done.9
  86.0 3.5 %collective-permute-start.11 = (f32[2,8,640]{2,1,0:T(8,128)S(1)}, f32[2,8,640]{2,1,0:T(8,128)S(1)}, u32[]{:S(2)}, u32[]{:S(2)}) collective-permute-start(f32[2,8,640]{2,1,0:T(8,128)S(1)} %dynamic-slice_bitcast_fusion.4), channel_id=1, source_target_pairs={{0,32},{16,48},{1,33},{17,49},{2,34},{18,50},{3,35},{19,51},{4,36}... | collective-permute-start | bytes 122888 | tf_op jit(solution)/shard_map/ppermute | solution.py:175
  89.5 1.9 %collective-permute-start.5 = (bf16[16,128,256]{2,1,0:T(8,128)(2,1)S(1)}, bf16[16,128,256]{2,1,0:T(8,128)(2,1)S(1)}, u32[]{:S(2)}, u32[]{:S(2)}) collective-permute-start(bf16[16,128,256]{2,1,0:T(8,128)(2,1)S(1)} %broadcast_select_fusion.1), channel_id=1, source_target_pairs={{0,16},{16,0},{1,17},{17,1},{2,18},{18,2},{3,19},{19,3},{4,20},{20... | collective-permute-start | bytes 3145736 | tf_op jit(solution)/shard_map/ppermute | solution.py:166
  91.5 2.5 %collective-permute-start.6 = (bf16[16,128,256]{2,1,0:T(8,128)(2,1)S(1)}, bf16[16,128,256]{2,1,0:T(8,128)(2,1)S(1)}, u32[]{:S(2)}, u32[]{:S(2)}) collective-permute-start(bf16[16,128,256]{2,1,0:T(8,128)(2,1)S(1)} %slice_bitcast_fusion), channel_id=1, source_target_pairs={{16,0},{17,1},{18,2},{19,3},{20,4},{21,5},{22,6},{23,7},{24,8},{25... | collective-permute-start | bytes 3145736 | tf_op jit(solution)/shard_map/ppermute | solution.py:167
  94.1 1.9 %collective-permute-start.12 = (f32[8,1280]{1,0:T(8,128)S(1)}, f32[8,1280]{1,0:T(8,128)S(1)}, u32[]{:S(2)}, u32[]{:S(2)}) collective-permute-start(f32[8,1280]{1,0:T(8,128)S(1)} %fusion.34), channel_id=1, source_target_pairs={{0,16},{16,0},{1,17},{17,1},{2,18},{18,2},{3,19},{19,3},{4,20},{20... | collective-permute-start | bytes 122888 | tf_op jit(solution)/shard_map/ppermute | solution.py:40
  96.1 1.1 %collective-permute-done.12 = f32[8,1280]{1,0:T(8,128)S(1)} collective-permute-done((f32[8,1280]{1,0:T(8,128)S(1)}, f32[8,1280]{1,0:T(8,128)S(1)}, u32[]{:S(2)}, u32[]{:S(2)}) %collective-permute-start.12) | collective-permute-done | bytes 40992 | tf_op jit(solution)/shard_map/ppermute | solution.py:40
  97.2 0.7 fusion.39
  97.9 0.5 convolution_bitcast_fusion.1
  98.4 0.5 convolution_bitcast_fusion
  98.9 0.8 copy.35
  (51 shorter events, 1.0 us)
Async XLA Ops:
  0.6 1.6 %copy-start.2 = (s32[128,256]{1,0:T(8,128)S(1)}, s32[128,256]{1,0:T(8,128)}, u32[]{:S(2)}) copy-start(s32[128,256]{1,0:T(8,128)} %param.10) | copy-start | bytes 393220
  0.6 1.6 %copy-start.4 = (bf16[128,256]{1,0:T(8,128)(2,1)S(1)}, bf16[128,256]{1,0:T(8,128)(2,1)}, u32[]{:S(2)}) copy-start(bf16[128,256]{1,0:T(8,128)(2,1)} %param.9) | copy-start | bytes 196612
  0.7 4.5 %copy-start = (bf16[128,1280]{1,0:T(8,128)(2,1)S(1)}, bf16[128,1280]{1,0:T(8,128)(2,1)}, u32[]{:S(2)}) copy-start(bf16[128,1280]{1,0:T(8,128)(2,1)} %param.11) | copy-start | bytes 983044
  1.9 3.3 %copy-start.1 = (bf16[128,256]{1,0:T(8,128)(2,1)S(1)}, bf16[128,256]{1,0:T(8,128)(2,1)}, u32[]{:S(2)}) copy-start(bf16[128,256]{1,0:T(8,128)(2,1)} %param.7) | copy-start | bytes 196612
  2.0 3.3 %copy-start.3 = (s32[128,256]{1,0:T(8,128)S(1)}, s32[128,256]{1,0:T(8,128)}, u32[]{:S(2)}) copy-start(s32[128,256]{1,0:T(8,128)} %param.8) | copy-start | bytes 393220
  2.3 20.7 %collective-permute-start.3 = (bf16[128,1152]{1,0:T(8,128)(2,1)S(1)}, bf16[128,1152]{1,0:T(8,128)(2,1)S(1)}, u32[]{:S(2)}, u32[]{:S(2)}) collective-permute-start(bf16[128,1152]{1,0:T(8,128)(2,1)S(1)} %pad_maximum_fusion.9), channel_id=1, source_target_pairs={{0,32},{16,48},{1,33},{17,49},{2,34},{18,50},{3,35},{19,51},{4,36}... | collective-permute-start | bytes 884744 | tf_op jit(solution)/shard_map/ppermute | solution.py:114
  5.4 3.7 %collective-permute-start = (f32[2816]{0:T(1024)S(1)}, f32[2816]{0:T(1024)S(1)}, u32[]{:S(2)}, u32[]{:S(2)}) collective-permute-start(f32[2816]{0:T(1024)S(1)} %pad_maximum_fusion.12), channel_id=1, source_target_pairs={{0,16},{16,0},{1,17},{17,1},{2,18},{18,2},{3,19},{19,3},{4,20},{20... | collective-permute-start | bytes 33800 | tf_op jit(solution)/shard_map/ppermute | solution.py:90
  9.8 19.8 %all-to-all-start = ((f32[16,1,2816]{2,1,0:T(1,128)}), f32[16,1,2816]{2,1,0:T(1,128)S(1)}, u32[]{:S(2)}, u32[]{:S(2)}) async-start(f32[16,1,2816]{2,1,0:T(1,128)} %broadcast_in_dim.7), calls=%async_computation | async-start | bytes 360448 | tf_op jit(solution)/shard_map/all_to_all | solution.py:24
  20.3 9.5 %collective-permute-start.1 = (bf16[2,128,256]{2,1,0:T(8,128)(2,1)S(1)}, bf16[2,128,256]{2,1,0:T(8,128)(2,1)S(1)}, u32[]{:S(2)}, u32[]{:S(2)}) collective-permute-start(bf16[2,128,256]{2,1,0:T(8,128)(2,1)S(1)} %pad_maximum_fusion.10), channel_id=1, source_target_pairs={{0,16},{16,0},{1,17},{17,1},{2,18},{18,2},{3,19},{19,3},{4,20},{20... | collective-permute-start | bytes 393224 | tf_op jit(solution)/shard_map/ppermute | solution.py:102
  23.1 18.9 %collective-permute-start.4 = (bf16[256,1152]{1,0:T(8,128)(2,1)S(1)}, bf16[256,1152]{1,0:T(8,128)(2,1)S(1)}, u32[]{:S(2)}, u32[]{:S(2)}) collective-permute-start(bf16[256,1152]{1,0:T(8,128)(2,1)S(1)} %pad_maximum_fusion.8), channel_id=1, source_target_pairs={{0,16},{16,0},{1,17},{17,1},{2,18},{18,2},{3,19},{19,3},{4,20},{20... | collective-permute-start | bytes 1769480 | tf_op jit(solution)/shard_map/ppermute | solution.py:115
  29.9 12.0 %collective-permute-start.2 = (bf16[2,128,256]{2,1,0:T(8,128)(2,1)S(1)}, bf16[2,128,256]{2,1,0:T(8,128)(2,1)S(1)}, u32[]{:S(2)}, u32[]{:S(2)}) collective-permute-start(bf16[2,128,256]{2,1,0:T(8,128)(2,1)S(1)} %pad_maximum_fusion.11), channel_id=1, source_target_pairs={{16,272},{17,208},{18,144},{19,80},{20,16},{21,464},{22,400},{23,3... | collective-permute-start | bytes 393224 | tf_op jit(solution)/shard_map/ppermute | solution.py:126
  43.9 12.9 %copy-start.5 = (f32[128,256]{1,0:T(8,128)S(1)}, f32[128,256]{1,0:T(8,128)}, u32[]{:S(2)}) copy-start(f32[128,256]{1,0:T(8,128)} %param.6) | copy-start | bytes 393220
  43.9 41.5 %all-to-all-start.1 = ((bf16[16,2,128,256]{3,2,1,0:T(8,128)(2,1)}), bf16[16,2,128,256]{3,2,1,0:T(8,128)(2,1)S(1)}, u32[]{:S(2)}, u32[]{:S(2)}) async-start(bf16[16,2,128,256]{3,2,1,0:T(8,128)(2,1)} %broadcast_in_dim.8), calls=%async_computation.1 | async-start | bytes 4194304 | tf_op jit(solution)/shard_map/all_to_all | solution.py:144
  57.0 28.6 %collective-permute-start.10 = (f32[32,640]{1,0:T(8,128)S(1)}, f32[32,640]{1,0:T(8,128)S(1)}, u32[]{:S(2)}, u32[]{:S(2)}) collective-permute-start(f32[32,640]{1,0:T(8,128)S(1)} %get-tuple-element.37), channel_id=1, source_target_pairs={{0,256},{1,257},{2,258},{3,259},{4,260},{5,261},{6,262},{7,263},{8... | collective-permute-start | bytes 245768 | tf_op jit(solution)/shard_map/ppermute | solution.py:162
  57.7 27.9 %collective-permute-start.7 = (f32[32,640]{1,0:T(8,128)S(1)}, f32[32,640]{1,0:T(8,128)S(1)}, u32[]{:S(2)}, u32[]{:S(2)}) collective-permute-start(f32[32,640]{1,0:T(8,128)S(1)} %get-tuple-element.36), channel_id=1, source_target_pairs={{0,64},{1,65},{2,66},{3,67},{4,68},{5,69},{6,70},{7,71},{8,72},{9,... | collective-permute-start | bytes 245768 | tf_op jit(solution)/shard_map/ppermute | solution.py:162
  62.0 23.6 %collective-permute-start.8 = (f32[32,640]{1,0:T(8,128)S(1)}, f32[32,640]{1,0:T(8,128)S(1)}, u32[]{:S(2)}, u32[]{:S(2)}) collective-permute-start(f32[32,640]{1,0:T(8,128)S(1)} %get-tuple-element.39), channel_id=1, source_target_pairs={{0,128},{1,129},{2,130},{3,131},{4,132},{5,133},{6,134},{7,135},{8... | collective-permute-start | bytes 245768 | tf_op jit(solution)/shard_map/ppermute | solution.py:162
  65.1 20.8 %collective-permute-start.9 = (f32[32,640]{1,0:T(8,128)S(1)}, f32[32,640]{1,0:T(8,128)S(1)}, u32[]{:S(2)}, u32[]{:S(2)}) collective-permute-start(f32[32,640]{1,0:T(8,128)S(1)} %get-tuple-element.38), channel_id=1, source_target_pairs={{0,192},{1,193},{2,194},{3,195},{4,196},{5,197},{6,198},{7,199},{8... | collective-permute-start | bytes 245768 | tf_op jit(solution)/shard_map/ppermute | solution.py:162
  86.0 8.0 %collective-permute-start.11 = (f32[2,8,640]{2,1,0:T(8,128)S(1)}, f32[2,8,640]{2,1,0:T(8,128)S(1)}, u32[]{:S(2)}, u32[]{:S(2)}) collective-permute-start(f32[2,8,640]{2,1,0:T(8,128)S(1)} %dynamic-slice_bitcast_fusion.4), channel_id=1, source_target_pairs={{0,32},{16,48},{1,33},{17,49},{2,34},{18,50},{3,35},{19,51},{4,36}... | collective-permute-start | bytes 122888 | tf_op jit(solution)/shard_map/ppermute | solution.py:175
  89.5 8.3 %collective-permute-start.5 = (bf16[16,128,256]{2,1,0:T(8,128)(2,1)S(1)}, bf16[16,128,256]{2,1,0:T(8,128)(2,1)S(1)}, u32[]{:S(2)}, u32[]{:S(2)}) collective-permute-start(bf16[16,128,256]{2,1,0:T(8,128)(2,1)S(1)} %broadcast_select_fusion.1), channel_id=1, source_target_pairs={{0,16},{16,0},{1,17},{17,1},{2,18},{18,2},{3,19},{19,3},{4,20},{20... | collective-permute-start | bytes 3145736 | tf_op jit(solution)/shard_map/ppermute | solution.py:166
  91.5 6.8 %collective-permute-start.6 = (bf16[16,128,256]{2,1,0:T(8,128)(2,1)S(1)}, bf16[16,128,256]{2,1,0:T(8,128)(2,1)S(1)}, u32[]{:S(2)}, u32[]{:S(2)}) collective-permute-start(bf16[16,128,256]{2,1,0:T(8,128)(2,1)S(1)} %slice_bitcast_fusion), channel_id=1, source_target_pairs={{16,0},{17,1},{18,2},{19,3},{20,4},{21,5},{22,6},{23,7},{24,8},{25... | collective-permute-start | bytes 3145736 | tf_op jit(solution)/shard_map/ppermute | solution.py:167
  94.1 3.1 %collective-permute-start.12 = (f32[8,1280]{1,0:T(8,128)S(1)}, f32[8,1280]{1,0:T(8,128)S(1)}, u32[]{:S(2)}, u32[]{:S(2)}) collective-permute-start(f32[8,1280]{1,0:T(8,128)S(1)} %fusion.34), channel_id=1, source_target_pairs={{0,16},{16,0},{1,17},{17,1},{2,18},{18,2},{3,19},{19,3},{4,20},{20... | collective-permute-start | bytes 122888 | tf_op jit(solution)/shard_map/ppermute | solution.py:40
